TPU v7x, 128 devices: a whole 4x4x4 slice. The times are simulated.
128 devices in a mesh: dp: 8 (over x_hi, z), fsdp: 8 (over y, core), enc: 2 (over x_lo).
Axes of the slice: x: 4 (x_hi: 2, x_lo: 2; x = x_hi * 2 + x_lo), y: 4, z: 4, core: 2. Of those that a mesh axis runs over, the one named last changes fastest.
Arguments:
- queries: bfloat16 [12288, 4096], P(('dp', 'fsdp'), 'enc'), may hold values from -9 to 9
- nbr_keys: bfloat16 [384, 128, 4096], P('dp', 'fsdp', 'enc'), may hold values from -6 to 6
- nbr_values: bfloat16 [384, 128, 4096], P('dp', 'fsdp', 'enc'), may hold values from -6 to 6
- out_proj: bfloat16 [4096, 8192], P('enc', 'fsdp'), may hold values from -0.09375 to 0.09375
- nbr_source: int32 [192, 2], replicated, may hold values from 0 to 7, as said below
- nbr_index: int32 [192, 2], replicated, may hold values from 0 to 47
- nbr_count: int32 [192], replicated, may hold values from 1 to 2
- cotangent: bfloat16 [12288, 8192], P('dp', 'fsdp'), may hold values from -2.390625 to 2.390625
Outputs:
- attended: bfloat16 [12288, 4096], P(('dp', 'fsdp'), 'enc')
- grad_queries: bfloat16 [12288, 4096], P(('dp', 'fsdp'), 'enc')
- grad_keys: bfloat16 [384, 128, 4096], P('dp', 'fsdp', 'enc')
- grad_values: bfloat16 [384, 128, 4096], P('dp', 'fsdp', 'enc')
- grad_proj: bfloat16 [4096, 8192], P('enc', 'fsdp')
Inputs may be any that keep to these rules, and one draw needn't show every extreme that they name: `nbr_source`: among the 6 slots of the spans of one device, no source group is named more than 1 times, and some group exactly 1 times.
All inputs are finite; a program needn't handle non-finite values.
Results may differ from a plain program's by a relative error of at most 0.013.
Values may be sent and summed in bfloat16 or wider, within the bound.
A program may use at most 128 MiB of HBM per device.

v0:
```python
import math

import jax
import jax.numpy as jnp
from jax import lax
from jax.sharding import PartitionSpec as P

HEAD_DIM = 128
SPAN = 64
SLOTS = 2


def local(queries, nbr_keys, nbr_values, out_proj, nbr_source, nbr_index, nbr_count, cotangent):
    dp_count = lax.axis_size("dp")
    fsdp_count = lax.axis_size("fsdp")
    peer_count = dp_count * fsdp_count
    token_rows, width_halved = queries.shape
    heads_here = width_halved // HEAD_DIM
    spans_here = token_rows // SPAN
    slot_count = SLOTS * spans_here
    capacity = (slot_count + dp_count - 1) // dp_count
    group_size, piece_rows, piece_width = nbr_keys.shape
    neighbour_len = piece_rows * fsdp_count
    scale = 1.0 / math.sqrt(HEAD_DIM)
    my_group = lax.axis_index("dp")
    my_place = my_group * fsdp_count + lax.axis_index("fsdp")
    all_sources = nbr_source.reshape(peer_count, slot_count)
    all_indices = nbr_index.reshape(peer_count, slot_count)
    slot_iota = jnp.arange(slot_count, dtype=jnp.int32)
    earlier = slot_iota[None, :] < slot_iota[:, None]
    same_source = all_sources[:, :, None] == all_sources[:, None, :]
    ranks = jnp.sum(jnp.logical_and(same_source, earlier[None]), axis=2)
    cap_iota = jnp.arange(capacity, dtype=jnp.int32)
    selected = jnp.logical_and(
        (all_sources == my_group)[:, :, None], ranks[:, :, None] == cap_iota[None, None, :]
    )
    picked = jnp.sum(jnp.where(selected, all_indices[:, :, None], 0), axis=1)
    present = jnp.any(selected, axis=1)
    flat_pick = picked.reshape(-1)
    send_keys = jnp.take(nbr_keys, flat_pick, axis=0)
    send_values = jnp.take(nbr_values, flat_pick, axis=0)
    got_keys, got_values = (
        lax.all_to_all(send_keys, ("dp", "fsdp"), split_axis=0, concat_axis=0, tiled=True),
        lax.all_to_all(send_values, ("dp", "fsdp"), split_axis=0, concat_axis=0, tiled=True),
    )
    got_keys = got_keys.reshape(dp_count, fsdp_count, capacity, piece_rows, piece_width)
    got_values = got_values.reshape(dp_count, fsdp_count, capacity, piece_rows, piece_width)
    my_sources = lax.dynamic_index_in_dim(all_sources, my_place, 0, keepdims=False)
    my_ranks = lax.dynamic_index_in_dim(ranks, my_place, 0, keepdims=False)
    slot_keys = got_keys[my_sources, :, my_ranks].reshape(
        spans_here, SLOTS * neighbour_len, heads_here, HEAD_DIM
    )
    slot_values = got_values[my_sources, :, my_ranks].reshape(
        spans_here, SLOTS * neighbour_len, heads_here, HEAD_DIM
    )
    local_counts = lax.dynamic_slice_in_dim(nbr_count, my_place * spans_here, spans_here)
    live_keys = jnp.repeat(
        jnp.arange(SLOTS)[None, :] < local_counts[:, None], neighbour_len, axis=1
    )
    query_blocks = queries.reshape(spans_here, SPAN, heads_here, HEAD_DIM)
    scores = (
        jnp.einsum("cqhd,ckhd->chqk", query_blocks, slot_keys, preferred_element_type=jnp.float32)
        * scale
    )
    scores = jnp.where(live_keys[:, None, None, :], scores, -1e30)
    peak = jnp.max(scores, axis=-1, keepdims=True)
    expo = jnp.exp(scores - peak)
    probs = expo / jnp.sum(expo, axis=-1, keepdims=True)
    probs_b = probs.astype(jnp.bfloat16)
    attended = jnp.einsum(
        "chqk,ckhd->cqhd", probs_b, slot_values, preferred_element_type=jnp.float32
    )
    attended = attended.astype(jnp.bfloat16).reshape(token_rows, width_halved)
    gathered = lax.all_gather(attended, "fsdp", axis=0, tiled=True)
    upstream = lax.psum_scatter(
        lax.dot_general(
            cotangent, out_proj, (((1,), (1,)), ((), ())), preferred_element_type=jnp.float32
        ),
        "fsdp",
        scatter_dimension=0,
        tiled=True,
    ).astype(jnp.bfloat16)
    proj_term = lax.dot_general(
        gathered, cotangent, (((0,), (0,)), ((), ())), preferred_element_type=jnp.float32
    )
    grad_proj = lax.psum(proj_term.astype(jnp.bfloat16), "dp")
    upstream_blocks = upstream.reshape(spans_here, SPAN, heads_here, HEAD_DIM)
    probability_gradient = jnp.einsum(
        "cqhd,ckhd->chqk", upstream_blocks, slot_values, preferred_element_type=jnp.float32
    )
    centre = jnp.sum(probs * probability_gradient, axis=-1, keepdims=True)
    dscores = (probs * (probability_gradient - centre) * scale).astype(jnp.bfloat16)
    grad_queries = jnp.einsum(
        "chqk,ckhd->cqhd", dscores, slot_keys, preferred_element_type=jnp.float32
    )
    grad_queries = grad_queries.astype(jnp.bfloat16).reshape(token_rows, width_halved)
    slot_key_grads = jnp.einsum(
        "chqk,cqhd->ckhd", dscores, query_blocks, preferred_element_type=jnp.float32
    ).astype(jnp.bfloat16)
    value_slot_gradients = jnp.einsum(
        "chqk,cqhd->ckhd", probs_b, upstream_blocks, preferred_element_type=jnp.float32
    ).astype(jnp.bfloat16)
    location_table = jnp.logical_and(
        my_sources[None, None, :] == jnp.arange(dp_count, dtype=jnp.int32)[:, None, None],
        my_ranks[None, None, :] == cap_iota[None, :, None],
    ).astype(jnp.bfloat16)
    key_slot_table = slot_key_grads.reshape(slot_count, fsdp_count, piece_rows * piece_width)
    value_slot_table = value_slot_gradients.reshape(
        slot_count, fsdp_count, piece_rows * piece_width
    )
    back_keys = jnp.einsum(
        "vnt,tqg->vqng", location_table, key_slot_table, preferred_element_type=jnp.float32
    ).astype(jnp.bfloat16)
    back_values = jnp.einsum(
        "vnt,tqg->vqng", location_table, value_slot_table, preferred_element_type=jnp.float32
    ).astype(jnp.bfloat16)
    ret_keys, ret_values = (
        lax.all_to_all(
            back_keys.reshape(peer_count * capacity, piece_rows, piece_width),
            ("dp", "fsdp"),
            split_axis=0,
            concat_axis=0,
            tiled=True,
        ),
        lax.all_to_all(
            back_values.reshape(peer_count * capacity, piece_rows, piece_width),
            ("dp", "fsdp"),
            split_axis=0,
            concat_axis=0,
            tiled=True,
        ),
    )
    owner_table = jnp.logical_and(
        flat_pick[None, :] == jnp.arange(group_size, dtype=jnp.int32)[:, None],
        present.reshape(-1)[None, :],
    ).astype(jnp.bfloat16)
    grad_keys = jnp.dot(
        owner_table,
        ret_keys.reshape(peer_count * capacity, piece_rows * piece_width),
        preferred_element_type=jnp.float32,
    )
    grad_values = jnp.dot(
        owner_table,
        ret_values.reshape(peer_count * capacity, piece_rows * piece_width),
        preferred_element_type=jnp.float32,
    )
    grad_keys = grad_keys.astype(jnp.bfloat16).reshape(group_size, piece_rows, piece_width)
    grad_values = grad_values.astype(jnp.bfloat16).reshape(group_size, piece_rows, piece_width)
    return (attended, grad_queries, grad_keys, grad_values, grad_proj)


def solution(mesh):
    placed = (
        P(("dp", "fsdp"), "enc"),
        P("dp", "fsdp", "enc"),
        P("dp", "fsdp", "enc"),
        P("enc", "fsdp"),
        P(),
        P(),
        P(),
        P("dp", "fsdp"),
    )
    return jax.shard_map(
        local,
        mesh=mesh,
        in_specs=placed,
        out_specs=(
            P(("dp", "fsdp"), "enc"),
            P(("dp", "fsdp"), "enc"),
            P("dp", "fsdp", "enc"),
            P("dp", "fsdp", "enc"),
            P("enc", "fsdp"),
        ),
        check_vma=False,
    )
```

profile of v0, /device:TPU:0, one launch (start us, length us, event | category | flops | bytes accessed | tf_op | source)
XLA Modules:
  0.0 502.5 jit_solution(7877312089183280143)
XLA Ops:
  9.1 11.3 %fusion.82 = f32[1536,2048]{1,0:T(8,128)} fusion(bf16[1536,1024]{1,0:T(8,128)(2,1)S(1)} %copy-done, bf16[2048,1024]{1,0:T(8,128)(2,1)} %param.13), kind=kOutput, calls=%fused_computation.97 | convolution fusion | flops 6442450944 | bytes 19922944 | tf_op jit(solution)/shard_map/dot_general | solution.py:76
  22.1 4.7 gather_fusion.3
  26.8 4.7 gather_fusion.2
  31.5 5.8 %broadcast_select_fusion = (bf16[64,16,2048]{2,1,0:T(8,128)(2,1)}, bf16[64,16,2048]{2,1,0:T(8,128)(2,1)S(1)}) fusion(bf16[64,16,2048]{2,1,0:T(8,128)(2,1)} %gather_fusion.3, pred[64]{0:T(512)(128)(4,1)S(1)} %compare_and_fusion.1, bf16[64,16,2048]{2,1,0:T(8,128)(2,1)} %gather_fusion.2), kind=kLoop, calls=%fused_computation.14 | loop fusion | flops 4194304 | bytes 16777280 | tf_op jit(solution)/shard_map/jit(_take)/select_n | solution.py:40
  37.3 74.8 %all_to_all.20 = bf16[64,16,2048]{2,1,0:T(8,128)(2,1)} all-to-all(bf16[64,16,2048]{2,1,0:T(8,128)(2,1)S(1)} %get-tuple-element.9), channel_id=1, replica_groups=mesh['dp'=8,'fsdp'=8,'enc'=2] {'dp','fsdp'}, dimensions={0} | all-to-all | bytes 8388608 | tf_op jit(solution)/shard_map/all_to_all | solution.py:44
  112.1 8.3 %all-to-all-start.1 = ((bf16[64,16,2048]{2,1,0:T(8,128)(2,1)}), bf16[64,16,2048]{2,1,0:T(8,128)(2,1)}, u32[]{:S(2)}, u32[]{:S(2)}) async-start(bf16[64,16,2048]{2,1,0:T(8,128)(2,1)} %get-tuple-element.8), calls=%async_computation.1 | async-start | bytes 8388608 | tf_op jit(solution)/shard_map/all_to_all | solution.py:43
  123.1 4.7 gather_fusion
  127.8 4.6 copy.106
  132.4 59.0 %all-to-all-done.1 = bf16[64,16,2048]{2,1,0:T(8,128)(2,1)} async-done(((bf16[64,16,2048]{2,1,0:T(8,128)(2,1)}), bf16[64,16,2048]{2,1,0:T(8,128)(2,1)}, u32[]{:S(2)}, u32[]{:S(2)}) %all-to-all-start.1) | async-done | bytes 4194336 | tf_op jit(solution)/shard_map/all_to_all | solution.py:43
  191.4 4.7 gather_fusion.1
  212.4 25.6 %convert_bitcast_fusion.1 = bf16[3,256,16,128]{3,1,2,0:T(8,128)(2,1)} fusion(f32[3,16,64,256]{3,2,1,0:T(8,128)} %fusion.9, bf16[3,64,16,128]{3,2,1,0:T(8,128)(2,1)} %bitcast.119, f32[3,16,64,256]{3,2,1,0:T(8,128)} %copy-done.9, f32[3,16,64]{2,1,0:T(8,128)S(1)} %get-tuple-element.10), kind=kOutput, calls=%fused_computation.22 | convolution fusion | flops 208407808 | bytes 10235904 | tf_op jit(solution)/shard_map/chqk,cqhd->ckhd/dot_general | solution.py:97
  238.0 5.6 %copy.97 = bf16[3,256,16,128]{3,2,1,0:T(8,128)(2,1)} copy(bf16[3,256,16,128]{3,1,2,0:T(8,128)(2,1)} %convert_bitcast_fusion.1) | data formatting | bytes 6291456 | tf_op jit(solution)/shard_map/convert_element_type | solution.py:99
  243.6 6.2 %reshape.273 = bf16[6,8,32768]{2,1,0:T(8,128)(2,1)} reshape(bf16[3,256,16,128]{3,2,1,0:T(8,128)(2,1)} %copy.97) | data formatting | bytes 6291456 | tf_op jit(solution)/shard_map/reshape | solution.py:107
  249.8 3.9 fusion.2
  256.0 4.4 copy.110
  260.4 5.8 %all-to-all-start.2 = ((bf16[64,16,2048]{2,1,0:T(8,128)(2,1)}), bf16[64,16,2048]{2,1,0:T(8,128)(2,1)}, u32[]{:S(2)}, u32[]{:S(2)}) async-start(bf16[64,16,2048]{2,1,0:T(8,128)(2,1)} %bitcast.105), calls=%async_computation.3 | async-start | bytes 8388608 | tf_op jit(solution)/shard_map/all_to_all | solution.py:118
  266.2 5.0 convert_bitcast_fusion
  271.2 4.9 copy.101
  276.2 5.8 %reshape.277 = bf16[6,8,32768]{2,1,0:T(8,128)(2,1)} reshape(bf16[3,256,16,128]{3,2,1,0:T(8,128)(2,1)} %copy.101) | data formatting | bytes 6291456 | tf_op jit(solution)/shard_map/reshape | solution.py:108
  282.0 3.9 fusion.3
  288.2 4.4 copy.113
  292.5 24.7 %all-to-all-done.2 = bf16[64,16,2048]{2,1,0:T(8,128)(2,1)} async-done(((bf16[64,16,2048]{2,1,0:T(8,128)(2,1)}), bf16[64,16,2048]{2,1,0:T(8,128)(2,1)}, u32[]{:S(2)}, u32[]{:S(2)}) %all-to-all-start.2) | async-done | bytes 4194336 | tf_op jit(solution)/shard_map/all_to_all | solution.py:118
  317.3 13.7 %all-to-all-start.3 = ((bf16[64,16,2048]{2,1,0:T(8,128)(2,1)}), bf16[64,16,2048]{2,1,0:T(8,128)(2,1)}, u32[]{:S(2)}, u32[]{:S(2)}) async-start(bf16[64,16,2048]{2,1,0:T(8,128)(2,1)} %bitcast.104), calls=%async_computation.4 | async-start | bytes 8388608 | tf_op jit(solution)/shard_map/all_to_all | solution.py:125
  331.1 11.3 %convolution_convert_fusion.4 = bf16[2048,1024]{1,0:T(8,128)(2,1)} fusion(bf16[1536,2048]{1,0:T(8,128)(2,1)} %all-gather.2.cloned.1.call-done, bf16[1536,1024]{1,0:T(8,128)(2,1)S(1)} %copy-done), kind=kOutput, calls=%fused_computation.16 | convolution fusion | flops 6444548096 | bytes 13631488 | tf_op jit(solution)/shard_map/dot_general | solution.py:83
  342.7 23.6 %fusion.41 = bf16[3,64,16,128]{3,1,2,0:T(8,128)(2,1)} fusion(bf16[3,256,16,128]{3,2,1,0:T(8,128)(2,1)} %bitcast.112, f32[3,16,64,256]{3,2,1,0:T(8,128)} %fusion.9, f32[3,16,64,256]{3,2,1,0:T(8,128)} %copy-done.9, f32[3,16,64]{2,1,0:T(8,128)S(1)} %get-tuple-element.10), kind=kOutput, calls=%fused_computation.44 | convolution fusion | flops 207228160 | bytes 10235904 | tf_op jit(solution)/shard_map/chqk,ckhd->cqhd/dot_general | solution.py:93
  369.1 4.6 copy.111
  374.6 3.6 copy.112
  378.2 10.6 %all-to-all-done.3 = bf16[64,16,2048]{2,1,0:T(8,128)(2,1)} async-done(((bf16[64,16,2048]{2,1,0:T(8,128)(2,1)}), bf16[64,16,2048]{2,1,0:T(8,128)(2,1)}, u32[]{:S(2)}, u32[]{:S(2)}) %all-to-all-start.3) | async-done | bytes 4194336 | tf_op jit(solution)/shard_map/all_to_all | solution.py:125
  388.9 4.9 copy.114
  394.7 3.6 copy.115
  398.3 92.7 %all-reduce.2.cloned.1.call-done = bf16[2048,1024]{1,0:T(8,128)(2,1)} async-done(((bf16[2048,1024]{1,0:T(8,128)(2,1)}), bf16[2048,1024]{1,0:T(8,128)(2,1)}) %all-reduce.2.cloned.1.call-update) | async-done | bytes 4194320 | tf_op jit(solution)/shard_map/psum | solution.py:86
  490.9 4.6 copy.149
  (69 shorter events, 32.0 us)
Async XLA Ops:
  7.2 1.9 copy-start
  7.2 199.6 %reduce-scatter.2.cloned.1.call-start = ((), (), s32[]{:S(2)}) async-start(), calls=%async_computation.5 | async-start | bytes 14155776 | tf_op jit(solution)/shard_map/reduce_scatter | solution.py:75
  20.4 0.7 copy-start.6
  20.4 1.4 copy-start.7
  112.1 10.8 %copy-start.8 = (s32[192]{0:T(256)S(1)}, s32[192]{0:T(256)}, u32[]{:S(2)}) copy-start(s32[192]{0:T(256)} %param.16) | copy-start | bytes 2308
  112.1 79.2 %all-to-all-start.1 = ((bf16[64,16,2048]{2,1,0:T(8,128)(2,1)}), bf16[64,16,2048]{2,1,0:T(8,128)(2,1)}, u32[]{:S(2)}, u32[]{:S(2)}) async-start(bf16[64,16,2048]{2,1,0:T(8,128)(2,1)} %get-tuple-element.8), calls=%async_computation.1 | async-start | bytes 8388608 | tf_op jit(solution)/shard_map/all_to_all | solution.py:43
  120.5 210.6 %all-gather.2.cloned.1.call-start = ((), (), s32[]{:S(2)}) async-start(), calls=%async_computation.6 | async-start | bytes 7077888 | tf_op jit(solution)/shard_map/all_gather | solution.py:74
  196.0 3.0 copy-start.4
  199.0 1.7 copy-start.1
  200.7 1.9 copy-start.2
  202.2 2.7 copy-start.9
  206.8 2.8 copy-start.3
  208.7 0.9 copy-start.5
  260.4 56.9 %all-to-all-start.2 = ((bf16[64,16,2048]{2,1,0:T(8,128)(2,1)}), bf16[64,16,2048]{2,1,0:T(8,128)(2,1)}, u32[]{:S(2)}, u32[]{:S(2)}) async-start(bf16[64,16,2048]{2,1,0:T(8,128)(2,1)} %bitcast.105), calls=%async_computation.3 | async-start | bytes 8388608 | tf_op jit(solution)/shard_map/all_to_all | solution.py:118
  317.3 71.6 %all-to-all-start.3 = ((bf16[64,16,2048]{2,1,0:T(8,128)(2,1)}), bf16[64,16,2048]{2,1,0:T(8,128)(2,1)}, u32[]{:S(2)}, u32[]{:S(2)}) async-start(bf16[64,16,2048]{2,1,0:T(8,128)(2,1)} %bitcast.104), calls=%async_computation.4 | async-start | bytes 8388608 | tf_op jit(solution)/shard_map/all_to_all | solution.py:125
  331.0 159.9 %all-reduce.2.cloned.1.call-start = ((), (), s32[]{:S(2)}) async-start(), calls=%async_computation.7 | async-start | bytes 8388608 | tf_op jit(solution)/shard_map/psum | solution.py:86
Sparse Core Ops, SparseCore 0:
  20.5 164.7 reduce-scatter.1
  206.7 38.3 all-gather.1
  342.6 148.3 all-reduce.1
where the time goes:
time: 511 us; the launch traced here: 503 us
  waiting for transfers between devices  187 us (37%)
  local copies, waits for them, and re-layouts  95.5 us (19%)
  matrix products  92.9 us (18%)
  blocking collectives  74.8 us (15%)
  starting transfers between devices  28 us (5%)
  between operations  14.5 us (3%)
  other arithmetic  9.69 us (2%)
    psum x1, waiting for transfers between devices, local(): grad_proj = lax.psum(proj_term.astype(jnp.bfloat16), 'dp')  92.7 us
    all_to_all x1, blocking collectives, local(): lax.all_to_all(send_values, ('dp', 'fsdp'), split_axis=0, concat_axis=0,...  74.8 us
    all_to_all x1, waiting for transfers between devices, local(): lax.all_to_all(send_keys, ('dp', 'fsdp'), split_axis=0, concat_axis=0, ti...  59 us
    unnamed x34, local copies, waits for them, and re-layouts  46.4 us
    dot_general x1, matrix products, local(): jnp.einsum('chqk,cqhd->ckhd', dscores, query_blocks, preferred_element_ty...  25.6 us
    all_to_all x1, waiting for transfers between devices, local(): lax.all_to_all(back_keys.reshape(peer_count * capacity, piece_rows, piece...  24.7 us
    dot_general x1, matrix products, local(): jnp.einsum('chqk,ckhd->cqhd', dscores, slot_keys, preferred_element_type=...  23.6 us
    all_to_all x1, starting transfers between devices, local(): lax.all_to_all(back_values.reshape(peer_count * capacity, piece_rows, pie...  13.7 us
  transfers between devices with their start and end apart: 6, of which 4 were waited for; matrix products, arithmetic and copies ran while one was open for 35% of the time, Pallas kernels for 0%

commit v1 on v0

v1 whole, which is shorter than its diff:
```python
import math

import jax
import jax.numpy as jnp
from jax import lax
from jax.experimental import pallas as pl
from jax.experimental.pallas import tpu as pltpu
from jax.sharding import PartitionSpec as P

HEAD_DIM = 128
SPAN = 64
SLOTS = 2
MESH = pl.DeviceIdType.MESH
ANY = pl.BlockSpec(memory_space=pl.ANY)
VM = pl.BlockSpec(memory_space=pltpu.VMEM)
SM = pl.BlockSpec(memory_space=pltpu.SMEM)
NT = (((1,), (1,)), ((), ()))
TN = (((0,), (0,)), ((), ()))
NN = (((1,), (0,)), ((), ()))
SCALE = 1.0 / math.sqrt(HEAD_DIM)
BIG = 60 << 20


def dot(a, b, dims):
    return lax.dot_general(a, b, dims, preferred_element_type=jnp.float32)


def enter(axes):
    barrier = pltpu.get_barrier_semaphore()
    total = 0
    for axis, size in axes:
        here = lax.axis_index(axis)
        for step in range(1, size):
            pl.semaphore_signal(
                barrier, inc=1, device_id={axis: lax.rem(here + step, size)}, device_id_type=MESH
            )
            total += 1
    pl.semaphore_wait(barrier, total)


def remote(src, dst, send, recv, axis, peer):
    return pltpu.make_async_remote_copy(
        src_ref=src, dst_ref=dst, send_sem=send, recv_sem=recv, device_id={axis: peer}, device_id_type=MESH
    )


def upstream_kernel(cot_ref, proj_ref, out_ref):
    rows = 512
    for start in range(0, cot_ref.shape[0], rows):
        out_ref[0, start : start + rows, :] = dot(
            cot_ref[start : start + rows, :], proj_ref[...], NT
        ).astype(jnp.bfloat16)


def project_kernel(att_ref, cot_ref, out_ref):
    out_ref[...] = dot(att_ref[0], cot_ref[...], TN).astype(jnp.bfloat16)


def spread_kernel(
    nd, nf, width, selc, q, k, v, kt, vt, qg, q_heads, q_send, k_own, v_own,
    qs, qr, ks, kr, vs, vr, gs, gr, own,
):
    dp, fs = lax.axis_index("dp"), lax.axis_index("fsdp")
    enter((("dp", nd), ("fsdp", nf)))

    def cols(ref, place):
        return ref.at[:, :, pl.ds(pl.multiple_of(place * width, width), width)]

    q_own = pltpu.make_async_copy(cols(q, fs), q_heads.at[fs], own.at[0])
    q_own.start()
    takes = [
        pltpu.make_async_copy(cols(k, fs), k_own, own.at[1]),
        pltpu.make_async_copy(cols(v, fs), v_own, own.at[2]),
    ]
    for take in takes:
        take.start()
    moves = {}
    for name, ref, out, send, recv in (
        ("q", q, q_heads, qs, qr),
        ("k", k, kt, ks, kr),
        ("v", v, vt, vs, vr),
    ):
        moves[name] = []
        for step in range(1, nf):
            peer = lax.rem(fs + step, nf)
            move = remote(cols(ref, peer), out.at[fs], send.at[step], recv.at[step], "fsdp", peer)
            move.start()
            moves[name].append(move)
    for take in takes:
        take.wait()
    puts = [
        pltpu.make_async_copy(k_own, kt.at[fs], own.at[3]),
        pltpu.make_async_copy(v_own, vt.at[fs], own.at[4]),
    ]
    for put in puts:
        put.start()
    q_own.wait()
    for move in moves["q"]:
        move.wait_recv()

    @pl.loop(0, nd)
    def _(group):
        @pl.loop(0, nf)
        def _(home):
            q_send[group, home] = q_heads[home, selc[group, home]]

    sends = []
    for step in range(1, nd):
        peer = lax.rem(dp + step, nd)
        move = remote(q_send.at[peer], qg.at[dp], gs.at[step], gr.at[step], "dp", peer)
        move.start()
        sends.append(move)
    put = pltpu.make_async_copy(q_send.at[dp], qg.at[dp], own.at[5])
    put.start()
    for move in moves["q"]:
        move.wait_send()
    for move in moves["k"] + moves["v"] + sends:
        move.wait()
    for copy in puts + [put]:
        copy.wait()


def forward_kernel(nf, refs, q, kt, vt, o_ref, st_ref):
    lane = lax.broadcasted_iota(jnp.int32, (SPAN, 128), 1)
    st_ref[...] = jnp.zeros_like(st_ref)
    o_ref[...] = jnp.zeros_like(o_ref)
    length = kt.shape[0] * kt.shape[2]

    @pl.loop(0, refs[0])
    def _(j):
        r, n = refs[1 + 3 * j], refs[2 + 3 * j]
        d, home = r // nf, r % nf
        keys = kt[:, n].reshape(length, -1)
        values = vt[:, n].reshape(length, -1)
        query = q[r]
        stats = st_ref[d]
        outs = []
        for h in range(keys.shape[1] // HEAD_DIM):
            part = slice(h * HEAD_DIM, (h + 1) * HEAD_DIM)
            scores = dot(query[:, part], keys[:, part], NT) * SCALE
            peak = jnp.max(scores, axis=1, keepdims=True)
            expo = jnp.exp(scores - peak)
            total = jnp.sum(expo, axis=1, keepdims=True)
            outs.append(dot(expo.astype(jnp.bfloat16), values[:, part], NN).astype(jnp.bfloat16))
            stats = jnp.where(lane == 4 * home + 2 * h, peak, stats)
            stats = jnp.where(lane == 4 * home + 2 * h + 1, total, stats)
        o_ref[r] = jnp.concatenate(outs, axis=1)
        st_ref[d] = stats


def meet_kernel(
    nd, nf, spans, selc, gsrc, count, u, o, st, ug, hs_out, att, u_send, o_home, st_home, hs, ss, sr, os, orr, us, ur, hsn, hr, own,
):
    dp = lax.axis_index("dp")
    enter((("dp", nd),))
    own_copies = [
        pltpu.make_async_copy(st.at[dp], st_home.at[dp], own.at[0]),
        pltpu.make_async_copy(o.at[dp], o_home.at[dp], own.at[1]),
    ]
    for copy in own_copies:
        copy.start()
    peers = [lax.rem(dp + step, nd) for step in range(1, nd)]
    stats = [
        remote(st.at[p], st_home.at[dp], ss.at[i], sr.at[i], "dp", p) for i, p in enumerate(peers)
    ]
    outs = [
        remote(o.at[p], o_home.at[dp], os.at[i], orr.at[i], "dp", p) for i, p in enumerate(peers)
    ]
    for move in stats + outs:
        move.start()

    @pl.loop(0, nd)
    def _(group):
        @pl.loop(0, nf)
        def _(home):
            u_send[group, home] = u[home * spans + selc[group, home]]

    ups = [
        remote(u_send.at[p], ug.at[dp], us.at[i], ur.at[i], "dp", p) for i, p in enumerate(peers)
    ]
    for move in ups:
        move.start()
    u_own = pltpu.make_async_copy(u_send.at[dp], ug.at[dp], own.at[2])
    u_own.start()
    for copy in own_copies:
        copy.wait()
    for move in stats + outs:
        move.wait_recv()
    lane = lax.broadcasted_iota(jnp.int32, (SPAN, 128), 1)

    def pick(array, at):
        return jnp.sum(jnp.where(lane == at, array, 0.0), axis=1, keepdims=True)

    def combine(i, table):
        home = i // spans
        g0, g1 = gsrc[2 * i], gsrc[2 * i + 1]
        both = count[i] > 1
        s0, s1 = st_home[g0], st_home[g1]
        o0, o1 = o_home[g0, home].astype(jnp.float32), o_home[g1, home].astype(jnp.float32)
        mine = u[i].astype(jnp.float32)
        pieces = []
        for h in range(u.shape[2] // HEAD_DIM):
            part = slice(h * HEAD_DIM, (h + 1) * HEAD_DIM)
            at = 4 * home + 2 * h
            m0, l0 = pick(s0, at), pick(s0, at + 1)
            m1 = jnp.where(both, pick(s1, at), -1e30)
            l1 = jnp.where(both, pick(s1, at + 1), 0.0)
            peak = jnp.maximum(m0, m1)
            a0, a1 = jnp.exp(m0 - peak), jnp.exp(m1 - peak)
            total = a0 * l0 + a1 * l1
            piece = (a0 * o0[:, part] + a1 * jnp.where(both, o1[:, part], 0.0)) / total
            pieces.append(piece.astype(jnp.bfloat16))
            centre = jnp.sum(piece * mine[:, part], axis=1, keepdims=True)
            table = jnp.where(lane == 4 * i + h, peak + jnp.log(total), table)
            table = jnp.where(lane == 4 * i + 2 + h, centre, table)
        att[i] = jnp.concatenate(pieces, axis=1)
        return table

    hs[...] = lax.fori_loop(0, nf * spans, combine, jnp.zeros((SPAN, 128), jnp.float32))
    gives = [
        remote(hs, hs_out.at[dp], hsn.at[i], hr.at[i], "dp", p) for i, p in enumerate(peers)
    ]
    for move in gives:
        move.start()
    hs_own = pltpu.make_async_copy(hs, hs_out.at[dp], own.at[3])
    hs_own.start()
    for move in stats + outs:
        move.wait_send()
    for move in ups + gives:
        move.wait()
    u_own.wait()
    hs_own.wait()


def backward_kernel(nf, spans, refs, q, u, hs, kt, vt, dq_ref, dk_ref, dv_ref, k_acc, v_acc):
    lane = lax.broadcasted_iota(jnp.int32, (SPAN, 128), 1)
    dq_ref[...] = jnp.zeros_like(dq_ref)
    k_acc[...] = jnp.zeros_like(k_acc)
    v_acc[...] = jnp.zeros_like(v_acc)
    pieces, nbrs, piece = kt.shape[0], kt.shape[1], kt.shape[2]
    length = pieces * piece

    def pick(array, at):
        return jnp.sum(jnp.where(lane == at, array, 0.0), axis=1, keepdims=True)

    @pl.loop(0, refs[0])
    def _(j):
        r, n, c = refs[1 + 3 * j], refs[2 + 3 * j], refs[3 + 3 * j]
        d, home = r // nf, r % nf
        keys = kt[:, n].reshape(length, -1)
        values = vt[:, n].reshape(length, -1)
        query, up, table = q[r], u[r], hs[d]
        at = 4 * (home * spans + c)
        dqs = []
        for h in range(keys.shape[1] // HEAD_DIM):
            part = slice(h * HEAD_DIM, (h + 1) * HEAD_DIM)
            scores = dot(query[:, part], keys[:, part], NT) * SCALE
            probs = jnp.exp(scores - pick(table, at + h))
            dprobs = dot(up[:, part], values[:, part], NT)
            ds = (probs * (dprobs - pick(table, at + 2 + h)) * SCALE).astype(jnp.bfloat16)
            dqs.append(dot(ds, keys[:, part], NN).astype(jnp.bfloat16))
            k_acc[n, :, part] += dot(ds, query[:, part], TN)
            v_acc[n, :, part] += dot(probs.astype(jnp.bfloat16), up[:, part], TN)
        dq_ref[r] = jnp.concatenate(dqs, axis=1)

    @pl.loop(0, nbrs)
    def _(n):
        dk_ref[:, n] = k_acc[n].reshape(pieces, piece, -1).astype(jnp.bfloat16)
        dv_ref[:, n] = v_acc[n].reshape(pieces, piece, -1).astype(jnp.bfloat16)


def return_kernel(
    nd, nf, width, spans, gsrc, count, dq, dk, dv, gq, gk, gv, dq_home, dq_sum, k_own, v_own,
    qs, qr, ks, kr, vs, vr, ys, yr, own,
):
    dp, fs = lax.axis_index("dp"), lax.axis_index("fsdp")
    enter((("dp", nd), ("fsdp", nf)))

    def cols(ref, place):
        return ref.at[:, :, pl.ds(pl.multiple_of(place * width, width), width)]

    firsts = [
        pltpu.make_async_copy(dq.at[dp], dq_home.at[dp], own.at[0]),
        pltpu.make_async_copy(dk.at[fs], k_own, own.at[1]),
        pltpu.make_async_copy(dv.at[fs], v_own, own.at[2]),
    ]
    for copy in firsts:
        copy.start()
    backs = []
    for step in range(1, nd):
        peer = lax.rem(dp + step, nd)
        move = remote(dq.at[peer], dq_home.at[dp], qs.at[step], qr.at[step], "dp", peer)
        move.start()
        backs.append(move)
    moves = []
    for ref, out, send, recv in ((dk, gk, ks, kr), (dv, gv, vs, vr)):
        for step in range(1, nf):
            peer = lax.rem(fs + step, nf)
            move = remote(ref.at[peer], cols(out, fs), send.at[step], recv.at[step], "fsdp", peer)
            move.start()
            moves.append(move)
    for copy in firsts:
        copy.wait()
    puts = [
        pltpu.make_async_copy(k_own, cols(gk, fs), own.at[3]),
        pltpu.make_async_copy(v_own, cols(gv, fs), own.at[4]),
    ]
    for put in puts:
        put.start()
    for move in backs:
        move.wait_recv()

    @pl.loop(0, nf)
    def _(home):
        for c in range(spans):
            i = home * spans + c
            d0 = dq_home[gsrc[2 * i], home].astype(jnp.float32)
            d1 = dq_home[gsrc[2 * i + 1], home].astype(jnp.float32)
            dq_sum[home, c] = (d0 + jnp.where(count[i] > 1, d1, 0.0)).astype(jnp.bfloat16)

    for step in range(1, nf):
        peer = lax.rem(fs + step, nf)
        move = remote(dq_sum.at[peer], cols(gq, fs), ys.at[step], yr.at[step], "fsdp", peer)
        move.start()
        moves.append(move)
    put = pltpu.make_async_copy(dq_sum.at[fs], cols(gq, fs), own.at[5])
    put.start()
    for move in backs:
        move.wait_send()
    for move in moves:
        move.wait()
    for copy in puts + [put]:
        copy.wait()


def dma(*shape):
    return pltpu.SemaphoreType.DMA(shape)


def comm(number, mib=BIG):
    return pltpu.CompilerParams(collective_id=number, has_side_effects=True, vmem_limit_bytes=mib)


def local(queries, nbr_keys, nbr_values, out_proj, nbr_source, nbr_index, nbr_count, cotangent):
    nd, nf = lax.axis_size("dp"), lax.axis_size("fsdp")
    bf, f32, i32 = jnp.bfloat16, jnp.float32, jnp.int32
    token_rows, full_width = queries.shape
    spans = token_rows // SPAN
    nbrs, piece, _ = nbr_keys.shape
    width = full_width // nf
    rows, columns = cotangent.shape
    slots = SLOTS * spans
    refs_all = nd * nf
    me = lax.axis_index("dp")

    sources = nbr_source.reshape(nd, nf, slots)
    indices = nbr_index.reshape(nd, nf, slots)
    counts = nbr_count.reshape(nd, nf, spans)
    slot = jnp.arange(slots, dtype=i32)
    my_sources = lax.dynamic_index_in_dim(sources, me, 0, keepdims=False)
    my_counts = lax.dynamic_index_in_dim(counts, me, 0, keepdims=False)
    hit = my_sources[None] == jnp.arange(nd, dtype=i32)[:, None, None]
    selc = jnp.sum(jnp.where(hit, slot // SLOTS, 0), axis=2)
    gsrc = my_sources.reshape(-1)
    count = my_counts.reshape(-1)
    alive = jnp.logical_and(
        sources == me, (slot % SLOTS)[None, None] < jnp.repeat(counts, SLOTS, axis=2)
    ).reshape(refs_all, slots)
    live = jnp.any(alive, axis=1)
    nidx = jnp.sum(jnp.where(alive, indices.reshape(refs_all, slots), 0), axis=1)
    cidx = jnp.sum(jnp.where(alive, slot // SLOTS, 0), axis=1)
    ref_iota = jnp.arange(refs_all, dtype=i32)
    rank = jnp.sum(jnp.logical_and(live[None, :], ref_iota[None, :] < ref_iota[:, None]), axis=1)
    place = jnp.logical_and(live[None, :], rank[None, :] == ref_iota[:, None])
    entry = jnp.stack([ref_iota, nidx, cidx], axis=1)
    listed = jnp.sum(jnp.where(place[:, :, None], entry[None], 0), axis=1)
    refs = jnp.concatenate([jnp.sum(live.astype(i32))[None], listed.reshape(-1)])

    partial = pl.pallas_call(
        upstream_kernel,
        grid=(nf,),
        in_specs=[
            pl.BlockSpec((rows, columns), lambda f: (0, 0), pipeline_mode=pl.Buffered(1)),
            pl.BlockSpec((width, columns), lambda f: (f, 0)),
        ],
        out_specs=pl.BlockSpec((1, rows, width), lambda f: (f, 0, 0)),
        out_shape=jax.ShapeDtypeStruct((nf, rows, width), bf),
        name="upstream",
        cost_estimate=pl.CostEstimate(
            flops=2 * rows * columns * full_width, bytes_accessed=14 << 20, transcendentals=0
        ),
    )(cotangent, out_proj)
    upstream = lax.psum_scatter(
        partial.reshape(nf * rows, width), "fsdp", scatter_dimension=0, tiled=True
    ).reshape(nf * spans, SPAN, width)

    kt, vt, qg = pl.pallas_call(
        lambda *a: spread_kernel(nd, nf, width, *a),
        in_specs=[SM, ANY, ANY, ANY],
        out_specs=[ANY, ANY, ANY],
        out_shape=[
            jax.ShapeDtypeStruct((nf, nbrs, piece, width), bf),
            jax.ShapeDtypeStruct((nf, nbrs, piece, width), bf),
            jax.ShapeDtypeStruct((nd, nf, SPAN, width), bf),
        ],
        scratch_shapes=[
            pltpu.VMEM((nf, spans, SPAN, width), bf),
            pltpu.VMEM((nd, nf, SPAN, width), bf),
            pltpu.VMEM((nbrs, piece, width), bf),
            pltpu.VMEM((nbrs, piece, width), bf),
            dma(nf), dma(nf), dma(nf), dma(nf), dma(nf), dma(nf), dma(nd), dma(nd), dma(6),
        ],
        compiler_params=comm(1),
        name="spread",
        cost_estimate=pl.CostEstimate(flops=0, bytes_accessed=300 << 20, transcendentals=0),
    )(selc, queries.reshape(spans, SPAN, full_width), nbr_keys, nbr_values)
    qr = qg.reshape(refs_all, SPAN, width)

    o, st = pl.pallas_call(
        lambda *a: forward_kernel(nf, *a),
        in_specs=[SM, VM, VM, VM],
        out_specs=[VM, VM],
        out_shape=[
            jax.ShapeDtypeStruct((refs_all, SPAN, width), bf),
            jax.ShapeDtypeStruct((nd, SPAN, 128), f32),
        ],
        compiler_params=pltpu.CompilerParams(vmem_limit_bytes=BIG),
        name="forward",
    )(refs, qr, kt, vt)

    ug, hs, att = pl.pallas_call(
        lambda *a: meet_kernel(nd, nf, spans, *a),
        in_specs=[SM, SM, SM, VM, ANY, ANY],
        out_specs=[ANY, ANY, VM],
        out_shape=[
            jax.ShapeDtypeStruct((nd, nf, SPAN, width), bf),
            jax.ShapeDtypeStruct((nd, SPAN, 128), f32),
            jax.ShapeDtypeStruct((nf * spans, SPAN, width), bf),
        ],
        scratch_shapes=[
            pltpu.VMEM((nd, nf, SPAN, width), bf),
            pltpu.VMEM((nd, nf, SPAN, width), bf),
            pltpu.VMEM((nd, SPAN, 128), f32),
            pltpu.VMEM((SPAN, 128), f32),
            dma(nd), dma(nd), dma(nd), dma(nd), dma(nd), dma(nd), dma(nd), dma(nd), dma(4),
        ],
        compiler_params=comm(2),
        name="meet",
    )(selc, gsrc, count, upstream, o.reshape(nd, nf, SPAN, width), st)

    gathered = lax.all_gather(att.reshape(rows, width), "fsdp", axis=0, tiled=True)
    gathered = gathered.reshape(nf, rows, width)

    dq, dk, dv = pl.pallas_call(
        lambda *a: backward_kernel(nf, spans, *a),
        in_specs=[SM, VM, VM, VM, VM, VM],
        out_specs=[VM, VM, VM],
        out_shape=[
            jax.ShapeDtypeStruct((refs_all, SPAN, width), bf),
            jax.ShapeDtypeStruct((nf, nbrs, piece, width), bf),
            jax.ShapeDtypeStruct((nf, nbrs, piece, width), bf),
        ],
        scratch_shapes=[
            pltpu.VMEM((nbrs, nf * piece, width), f32),
            pltpu.VMEM((nbrs, nf * piece, width), f32),
        ],
        compiler_params=pltpu.CompilerParams(vmem_limit_bytes=BIG),
        name="backward",
        cost_estimate=pl.CostEstimate(flops=10 << 30, bytes_accessed=20 << 20, transcendentals=0),
    )(refs, qr, ug.reshape(refs_all, SPAN, width), hs, kt, vt)

    term = pl.pallas_call(
        project_kernel,
        grid=(nf,),
        in_specs=[
            pl.BlockSpec((1, rows, width), lambda f: (f, 0, 0)),
            pl.BlockSpec((rows, columns), lambda f: (0, 0), pipeline_mode=pl.Buffered(1)),
        ],
        out_specs=pl.BlockSpec((width, columns), lambda f: (f, 0)),
        out_shape=jax.ShapeDtypeStruct((full_width, columns), bf),
        name="project",
        cost_estimate=pl.CostEstimate(
            flops=2 * rows * columns * full_width, bytes_accessed=14 << 20, transcendentals=0
        ),
    )(gathered, cotangent)
    grad_proj = lax.psum(term, "dp")
    my_rows = lax.dynamic_slice_in_dim(
        gathered, lax.axis_index("fsdp") * token_rows, token_rows, axis=1
    )
    attended = jnp.transpose(my_rows, (1, 0, 2)).reshape(token_rows, full_width)

    gq, gk, gv = pl.pallas_call(
        lambda *a: return_kernel(nd, nf, width, spans, *a),
        in_specs=[SM, SM, ANY, ANY, ANY],
        out_specs=[ANY, ANY, ANY],
        out_shape=[
            jax.ShapeDtypeStruct((spans, SPAN, full_width), bf),
            jax.ShapeDtypeStruct((nbrs, piece, full_width), bf),
            jax.ShapeDtypeStruct((nbrs, piece, full_width), bf),
        ],
        scratch_shapes=[
            pltpu.VMEM((nd, nf, SPAN, width), bf),
            pltpu.VMEM((nf, spans, SPAN, width), bf),
            pltpu.VMEM((nbrs, piece, width), bf),
            pltpu.VMEM((nbrs, piece, width), bf),
            dma(nd), dma(nd), dma(nf), dma(nf), dma(nf), dma(nf), dma(nf), dma(nf), dma(6),
        ],
        compiler_params=comm(3),
        name="giveback",
        cost_estimate=pl.CostEstimate(flops=0, bytes_accessed=300 << 20, transcendentals=0),
    )(gsrc, count, dq.reshape(nd, nf, SPAN, width), dk, dv)
    return (attended, gq.reshape(token_rows, full_width), gk, gv, grad_proj)


def solution(mesh):
    placed = (
        P(("dp", "fsdp"), "enc"),
        P("dp", "fsdp", "enc"),
        P("dp", "fsdp", "enc"),
        P("enc", "fsdp"),
        P(),
        P(),
        P(),
        P("dp", "fsdp"),
    )
    return jax.shard_map(
        local,
        mesh=mesh,
        in_specs=placed,
        out_specs=(
            P(("dp", "fsdp"), "enc"),
            P(("dp", "fsdp"), "enc"),
            P("dp", "fsdp", "enc"),
            P("dp", "fsdp", "enc"),
            P("enc", "fsdp"),
        ),
        check_vma=False,
    )
```

time: 511 us -> 441 us (0.86); the launches traced: 503 us -> 440 us
  Pallas kernels: 0 us -> 350 us
  waiting for transfers between devices: 187 us -> 56.5 us
  matrix products: 92.9 us -> 0 us
  local copies, waits for them, and re-layouts: 95.5 us -> 16 us
  blocking collectives: 74.8 us -> 0 us
  starting transfers between devices: 28 us -> 0.12 us
  other arithmetic: 9.69 us -> 3.28 us
    pallas_call x0 -> x7, Pallas kernels: none -> 350 us  [the longest x1 112 us: local(): pl.pallas_call(lambda *a: spread_kernel(nd, nf, width, *a), in_specs=[SM,...]
    all_to_all x3 -> x0, waiting for transfers between devices: 94.3 us -> none  [the longest x1 59 us: local(): lax.all_to_all(send_keys, ('dp', 'fsdp'), split_axis=0, concat_axis=0, ti...]
    dot_general x12 -> x0, matrix products: 92.9 us -> none  [the longest x1 25.6 us: local(): jnp.einsum('chqk,cqhd->ckhd', dscores, query_blocks, preferred_element_ty...]
    psum x1, waiting for transfers between devices: 92.7 us -> 10.9 us  [local(): grad_proj = lax.psum(term, 'dp')]
    all_to_all x1 -> x0, blocking collectives: 74.8 us -> none  [local(): lax.all_to_all(send_values, ('dp', 'fsdp'), split_axis=0, concat_axis=0,...]
    all_gather x1, waiting for transfers between devices: 0.02 us -> 45.5 us  [local(): lax.all_gather(att.reshape(rows, width), 'fsdp', axis=0, tiled=True)]
    unnamed x34 -> x18, local copies, waits for them, and re-layouts: 46.4 us -> 12.5 us
    all_to_all x3 -> x0, starting transfers between devices: 27.9 us -> none  [the longest x1 13.7 us: local(): lax.all_to_all(back_values.reshape(peer_count * capacity, piece_rows, pie...]
  transfers between devices with their start and end apart: 6 -> 3, of which waited for: 4 -> 2; matrix products, arithmetic and copies ran while one was open for 35% -> 2% of each run, Pallas kernels for 0% -> 58%
where the time goes in v1:
time: 441 us; the launch traced here: 440 us
  Pallas kernels  350 us (79%)
  waiting for transfers between devices  56.5 us (13%)
  local copies, waits for them, and re-layouts  16 us (4%)
  between operations  13.9 us (3%)
    pallas_call x1, Pallas kernels, local(): pl.pallas_call(lambda *a: spread_kernel(nd, nf, width, *a), in_specs=[SM,...  112 us
    pallas_call x1, Pallas kernels, local(): pl.pallas_call(lambda *a: return_kernel(nd, nf, width, spans, *a), in_spe...  86.5 us
    pallas_call x1, Pallas kernels, local(): pl.pallas_call(lambda *a: meet_kernel(nd, nf, spans, *a), in_specs=[SM, S...  71.5 us
    all_gather x1, waiting for transfers between devices, local(): lax.all_gather(att.reshape(rows, width), 'fsdp', axis=0, tiled=True)  45.5 us
    pallas_call x1, Pallas kernels, local(): pl.pallas_call(lambda *a: backward_kernel(nf, spans, *a), in_specs=[SM, V...  29.8 us
    pallas_call x1, Pallas kernels, local(): pl.pallas_call(lambda *a: forward_kernel(nf, *a), in_specs=[SM, VM, VM, V...  25.8 us
    unnamed x18, local copies, waits for them, and re-layouts  12.5 us
    pallas_call x1, Pallas kernels, local(): pl.pallas_call(upstream_kernel, grid=(nf,), in_specs=[pl.BlockSpec((rows,...  12.2 us
  transfers between devices with their start and end apart: 3, of which 2 were waited for; matrix products, arithmetic and copies ran while one was open for 2% of the time, Pallas kernels for 58%

profile of v1, /device:TPU:0, one launch (start us, length us, event | category | flops | bytes accessed | tf_op | source)
XLA Modules:
  0.0 440.2 jit_solution(1203713874202450656)
XLA Ops:
  7.2 12.2 %upstream.1 = bf16[8,1536,256]{2,1,0:T(8,128)(2,1)} custom-call(bf16[1536,1024]{1,0:T(8,128)(2,1)} %cot_ref.3, bf16[2048,1024]{1,0:T(8,128)(2,1)} %proj_ref.1), custom_call_target="tpu_custom_call" | custom-call | flops 6442450944 | bytes 14680064 | tf_op jit(solution)/shard_map/upstream/pallas_call | solution.py:379
  19.5 0.6 copy-done.4
  20.1 0.1 reshape.132
  20.3 0.6 reshape.133.a_2_.a_1_
  20.9 0.1 broadcast_in_dim.64
  21.1 0.1 lt.47
  21.2 0.1 copy.18
  21.4 0.2 reduce_or.14
  21.6 0.1 reduce_sum.72
  21.8 0.1 reduce_sum.75
  22.4 0.1 select_reduce_fusion
  22.6 0.1 reshape.136
  22.8 0.6 reshape.131.a_1_.a_0_
  23.5 0.7 select_reduce_fusion.1.a_0_
  24.2 112.4 %spread.1 = (bf16[8,48,16,256]{3,2,1,0:T(8,128)(2,1)}, bf16[8,48,16,256]{3,2,1,0:T(8,128)(2,1)}, bf16[8,8,64,256]{3,2,1,0:T(8,128)(2,1)}) custom-call(s32[8,8]{1,0:T(8,128)} %select_reduce_fusion.1.a_0_, bf16[3,64,2048]{2,1,0:T(8,128)(2,1)} %bitcast.28, bf16[48,16,2048]{2,1,0:T(8,128)(2,1)} %a_2_.1, bf16[48,16,2048]{2,1,0:T(8,128)(2,1)} %a_3_.1), custom_call_target="tpu_custom_call" | custom-call | bytes 314572800 | tf_op jit(solution)/shard_map/spread/pallas_call | solution.py:397
  136.6 0.6 convert_reduce_fusion.1
  137.2 1.3 pad_add_fusion.1.a_0_
  138.5 25.8 %forward.1 = (bf16[64,64,256]{2,1,0:T(8,128)(2,1)}, f32[8,64,128]{2,1,0:T(8,128)}) custom-call(s32[193]{0:T(256)} %pad_add_fusion.1.a_0_, bf16[64,64,256]{2,1,0:T(8,128)(2,1)} %bitcast.24, bf16[8,48,16,256]{3,2,1,0:T(8,128)(2,1)} %get-tuple-element.20.a_2_.a_4_, bf16[8,48,16,256]{3,2,1,0:T(8,128)(2,1)} %get-tuple-element.21.a_3_.a_5_), custom_call_target="tpu_custom_call" | custom-call | tf_op jit(solution)/shard_map/forward/pallas_call | solution.py:419
  164.3 71.5 %meet.1 = (bf16[8,8,64,256]{3,2,1,0:T(8,128)(2,1)}, f32[8,64,128]{2,1,0:T(8,128)}, bf16[24,64,256]{2,1,0:T(8,128)(2,1)}) custom-call(s32[8,8]{1,0:T(8,128)} %select_reduce_fusion.1.a_0_, s32[48]{0:T(128)} %reshape.131.a_1_.a_0_, s32[24]{0:T(128)} %reshape.133.a_2_.a_1_, bf16[24,64,256]{2,1,0:T(8,128)(2,1)} %bitcast.32, bf16[8,8,64,256]{3,2,1,0:T(8,128)(2,1)} %bitcast.27, ...), custom_call_target="tpu_custom_call" | custom-call | tf_op jit(solution)/shard_map/meet/pallas_call | solution.py:431
  235.9 45.5 %all-gather.2.cloned.1.call-done = bf16[12288,256]{1,0:T(8,128)(2,1)} async-done(((bf16[1536,256]{1,0:T(8,128)(2,1)}), bf16[12288,256]{1,0:T(8,128)(2,1)}) %all-gather.2.cloned.1.call-update) | async-done | bytes 6291472 | tf_op jit(solution)/shard_map/all_gather | solution.py:451
  281.5 12.2 %project.1 = bf16[2048,1024]{1,0:T(8,128)(2,1)} custom-call(bf16[8,1536,256]{2,1,0:T(8,128)(2,1)} %bitcast.33, bf16[1536,1024]{1,0:T(8,128)(2,1)} %cot_ref.3), custom_call_target="tpu_custom_call" | custom-call | flops 6442450944 | bytes 14680064 | tf_op jit(solution)/shard_map/project/pallas_call | solution.py:472
  293.7 29.8 %backward.1 = (bf16[64,64,256]{2,1,0:T(8,128)(2,1)}, bf16[8,48,16,256]{3,2,1,0:T(8,128)(2,1)}, bf16[8,48,16,256]{3,2,1,0:T(8,128)(2,1)}) custom-call(s32[193]{0:T(256)} %pad_add_fusion.1.a_0_, bf16[64,64,256]{2,1,0:T(8,128)(2,1)} %bitcast.25, bf16[64,64,256]{2,1,0:T(8,128)(2,1)} %bitcast.37, f32[8,64,128]{2,1,0:T(8,128)} %get-tuple-element.26.a_3_, ...), custom_call_target="tpu_custom_call" | custom-call | flops 10737418240 | bytes 20971520 | tf_op jit(solution)/shard_map/backward/pallas_call | solution.py:454
  323.5 86.5 %giveback.1 = (bf16[3,64,2048]{2,1,0:T(8,128)(2,1)}, bf16[48,16,2048]{2,1,0:T(8,128)(2,1)}, bf16[48,16,2048]{2,1,0:T(8,128)(2,1)}) custom-call(s32[48]{0:T(128)} %reshape.131.a_1_.a_0_, s32[24]{0:T(128)} %reshape.133.a_2_.a_1_, bf16[8,8,64,256]{3,2,1,0:T(8,128)(2,1)} %bitcast.26, bf16[8,48,16,256]{3,2,1,0:T(8,128)(2,1)} %get-tuple-element.28.a_3_, ...), custom_call_target="tpu_custom_call" | custom-call | bytes 314572800 | tf_op jit(solution)/shard_map/giveback/pallas_call | solution.py:492
  410.0 1.3 dynamic-slice_bitcast_fusion
  411.4 1.0 copy.22
  412.4 10.9 %all-reduce.2.cloned.1.call-done = bf16[2048,1024]{1,0:T(8,128)(2,1)} async-done(((bf16[2048,1024]{1,0:T(8,128)(2,1)}), bf16[2048,1024]{1,0:T(8,128)(2,1)}) %all-reduce.2.cloned.1.call-update) | async-done | bytes 4194320 | tf_op jit(solution)/shard_map/psum | solution.py:486
  423.2 2.1 copy.27
  425.3 1.7 copy.28
  427.0 1.4 copy-done.1
  428.3 1.7 copy.29
  430.0 1.7 copy-done
  431.7 2.0 copy.30
  (35 shorter events, 1.0 us)
Async XLA Ops:
  7.2 157.2 %reduce-scatter.2.cloned.1.call-start = ((), (), s32[]{:S(2)}) async-start(), calls=%async_computation.1 | async-start | bytes 7077888 | tf_op jit(solution)/shard_map/reduce_scatter | solution.py:393
  19.4 0.7 copy-start.4
  19.4 1.8 copy-start.3
  19.4 2.1 copy-start.5
  19.5 262.0 %all-gather.2.cloned.1.call-start = ((), (), s32[]{:S(2)}) async-start(), calls=%async_computation.2 | async-start | bytes 7077888 | tf_op jit(solution)/shard_map/all_gather | solution.py:451
  235.9 187.4 %all-reduce.2.cloned.1.call-start = ((), (), s32[]{:S(2)}) async-start(), calls=%async_computation.3 | async-start | bytes 8388608 | tf_op jit(solution)/shard_map/psum | solution.py:486
  410.0 15.3 %copy-start.2 = (bf16[48,16,2048]{2,1,0:T(8,128)(2,1)S(1)}, bf16[48,16,2048]{2,1,0:T(8,128)(2,1)}, u32[]{:S(2)}) copy-start(bf16[48,16,2048]{2,1,0:T(8,128)(2,1)} %get-tuple-element.46) | copy-start | bytes 9437188
  425.3 3.0 copy-start.1
  428.3 3.3 copy-start
Sparse Core Ops, SparseCore 0:
  19.6 126.3 reduce-scatter.1
  236.0 45.4 all-gather.1
  293.8 129.4 all-reduce.1

commit v2 on v1

v2 whole, which is shorter than its diff:
```python
import math

import jax
import jax.numpy as jnp
from jax import lax
from jax.experimental import pallas as pl
from jax.experimental.pallas import tpu as pltpu
from jax.sharding import PartitionSpec as P

HEAD_DIM = 128
SPAN = 64
SLOTS = 2
MESH = pl.DeviceIdType.MESH
ANY = pl.BlockSpec(memory_space=pl.ANY)
VM = pl.BlockSpec(memory_space=pltpu.VMEM)
SM = pl.BlockSpec(memory_space=pltpu.SMEM)
NT = (((1,), (1,)), ((), ()))
TN = (((0,), (0,)), ((), ()))
NN = (((1,), (0,)), ((), ()))
SCALE = 1.0 / math.sqrt(HEAD_DIM)
BIG = 60 << 20


def dot(a, b, dims):
    return lax.dot_general(a, b, dims, preferred_element_type=jnp.float32)


def enter(axes):
    barrier = pltpu.get_barrier_semaphore()
    total = 0
    for axis, size in axes:
        here = lax.axis_index(axis)
        for step in range(1, size):
            pl.semaphore_signal(
                barrier, inc=1, device_id={axis: lax.rem(here + step, size)}, device_id_type=MESH
            )
            total += 1
    pl.semaphore_wait(barrier, total)


def remote(src, dst, send, recv, axis, peer):
    return pltpu.make_async_remote_copy(
        src_ref=src, dst_ref=dst, send_sem=send, recv_sem=recv, device_id={axis: peer}, device_id_type=MESH
    )


def cols(ref, place, width):
    return ref.at[:, :, pl.ds(pl.multiple_of(place * width, width), width)]


def spread_kernel(
    nd, nf, width, selc, q, k, v, cot, proj, kt, vt, qg, ug, u_out,
    q_heads, send, k_own, v_own, cot_vm, proj_vm, sib_send, sib_recv, mine, ring_send, ring_recv,
    qs, qr, ks, kr, vs, vr, gs, gr, us, ur, bs, br, rs, rr, own, load,
):
    dp, fs = lax.axis_index("dp"), lax.axis_index("fsdp")
    chips = nf // 2
    chip, core = fs // 2, lax.rem(fs, 2)
    sibling = chip * 2 + 1 - core
    spans = q_heads.shape[1]
    loads = [
        pltpu.make_async_copy(cot, cot_vm, load.at[0]),
        pltpu.make_async_copy(proj, proj_vm, load.at[1]),
    ]
    for copy in loads:
        copy.start()
    enter((("dp", nd), ("fsdp", nf)))
    q_own = pltpu.make_async_copy(cols(q, fs, width), q_heads.at[fs], own.at[0])
    q_own.start()

    def spread(ref, out, s_sem, r_sem):
        moves = []
        for step in range(1, nf):
            peer = lax.rem(fs + step, nf)
            move = remote(cols(ref, peer, width), out.at[fs], s_sem.at[step], r_sem.at[step], "fsdp", peer)
            move.start()
            moves.append(move)
        return moves

    q_moves = spread(q, q_heads, qs, qr)
    k_moves = spread(k, kt, ks, kr)
    takes = [
        pltpu.make_async_copy(cols(k, fs, width), k_own, own.at[1]),
        pltpu.make_async_copy(cols(v, fs, width), v_own, own.at[2]),
    ]
    for take in takes:
        take.start()
    for copy in loads:
        copy.wait()
    rows = cot_vm.shape[0]
    tile = 512
    sib_moves = []
    for step in range(chips):
        there = lax.rem(chip + step + 1, chips)
        for which in (1 - core, core):
            block = pl.multiple_of((there * 2 + which) * width, width)
            first = len(sib_moves) == step

            @pl.loop(0, rows // tile)
            def _(t):
                at = pl.multiple_of(t * tile, tile)
                value = dot(cot_vm[pl.ds(at, tile), :], proj_vm[pl.ds(block, width), :], NT)
                if first:
                    sib_send[step, pl.ds(at, tile), :] = value.astype(jnp.bfloat16)
                else:
                    mine[step, pl.ds(at, tile), :] = value

            if first:
                move = remote(sib_send.at[step], sib_recv.at[step], bs.at[step], br.at[step], "fsdp", sibling)
                move.start()
                sib_moves.append(move)
    ring_moves = []
    for step in range(chips - 1):
        there = lax.rem(chip + step + 1, chips)
        sib_moves[step].wait_recv()

        @pl.loop(0, rows // tile)
        def _(t):
            at = pl.ds(pl.multiple_of(t * tile, tile), tile)
            ring_send[step, at, :] = (
                mine[step, at, :] + sib_recv[step, at, :].astype(jnp.float32)
            ).astype(jnp.bfloat16)

        move = remote(
            ring_send.at[step], ring_recv.at[step], rs.at[step], rr.at[step], "fsdp", there * 2 + core
        )
        move.start()
        ring_moves.append(move)
    v_moves = spread(v, vt, vs, vr)
    for take in takes:
        take.wait()
    puts = [
        pltpu.make_async_copy(k_own, kt.at[fs], own.at[3]),
        pltpu.make_async_copy(v_own, vt.at[fs], own.at[4]),
    ]
    for put in puts:
        put.start()
    q_own.wait()
    for move in q_moves:
        move.wait_recv()

    def deliver(kind, source, out, s_sem, r_sem):
        @pl.loop(0, nd)
        def _(group):
            @pl.loop(0, nf)
            def _(home):
                send[kind, group, home] = source(home, selc[group, home])

        moves = []
        for step in range(1, nd):
            peer = lax.rem(dp + step, nd)
            move = remote(send.at[kind, peer], out.at[dp], s_sem.at[step], r_sem.at[step], "dp", peer)
            move.start()
            moves.append(move)
        put = pltpu.make_async_copy(send.at[kind, dp], out.at[dp], own.at[5 + kind])
        put.start()
        puts.append(put)
        return moves

    moves = deliver(0, lambda home, c: q_heads[home, c], qg, gs, gr)
    sib_moves[chips - 1].wait_recv()
    for move in ring_moves:
        move.wait_recv()

    @pl.loop(0, rows // SPAN)
    def _(i):
        at = pl.ds(pl.multiple_of(i * SPAN, SPAN), SPAN)
        value = mine[chips - 1, at, :] + sib_recv[chips - 1, at, :].astype(jnp.float32)
        for step in range(chips - 1):
            value += ring_recv[step, at, :].astype(jnp.float32)
        u_out[i] = value.astype(jnp.bfloat16)

    moves += deliver(1, lambda home, c: u_out[home * spans + c], ug, us, ur)
    for move in q_moves + sib_moves + ring_moves:
        move.wait_send()
    for move in k_moves + v_moves + moves:
        move.wait()
    for put in puts:
        put.wait()


UNROLL = 4


def forward_kernel(nf, refs, q, kt, vt, o_ref, st_ref):
    lane = lax.broadcasted_iota(jnp.int32, (SPAN, 128), 1)
    length = kt.shape[0] * kt.shape[2]

    @pl.loop(0, (refs[0] + UNROLL - 1) // UNROLL)
    def _(step):
        done = []
        for more in range(UNROLL):
            j = step * UNROLL + more
            r, n = refs[1 + 4 * j], refs[2 + 4 * j]
            keys = kt[:, n].reshape(length, -1)
            values = vt[:, n].reshape(length, -1)
            query = q[r]
            outs, marks = [], []
            for h in range(keys.shape[1] // HEAD_DIM):
                part = slice(h * HEAD_DIM, (h + 1) * HEAD_DIM)
                scores = dot(query[:, part], keys[:, part], NT) * SCALE
                peak = jnp.max(scores, axis=1, keepdims=True)
                expo = jnp.exp(scores - peak)
                total = jnp.sum(expo, axis=1, keepdims=True)
                outs.append(dot(expo.astype(jnp.bfloat16), values[:, part], NN).astype(jnp.bfloat16))
                marks += [peak, total]
            done.append((r, outs, marks))
        for r, outs, marks in done:
            o_ref[r] = jnp.concatenate(outs, axis=1)
            stats = st_ref[r // nf]
            for i, mark in enumerate(marks):
                stats = jnp.where(lane == 4 * (r % nf) + i, mark, stats)
            st_ref[r // nf] = stats


def meet_kernel(
    nd, nf, spans, gsrc, count, u, o, st, hs_out, att, o_home, st_home, hs, ss, sr, os, orr, hsn, hr, own,
):
    dp = lax.axis_index("dp")
    enter((("dp", nd),))
    own_copies = [
        pltpu.make_async_copy(st.at[dp], st_home.at[dp], own.at[0]),
        pltpu.make_async_copy(o.at[dp], o_home.at[dp], own.at[1]),
    ]
    for copy in own_copies:
        copy.start()
    peers = [lax.rem(dp + step, nd) for step in range(1, nd)]
    stats = [
        remote(st.at[p], st_home.at[dp], ss.at[i], sr.at[i], "dp", p) for i, p in enumerate(peers)
    ]
    outs = [
        remote(o.at[p], o_home.at[dp], os.at[i], orr.at[i], "dp", p) for i, p in enumerate(peers)
    ]
    for move in stats + outs:
        move.start()
    for copy in own_copies:
        copy.wait()
    for move in stats + outs:
        move.wait_recv()
    lane = lax.broadcasted_iota(jnp.int32, (SPAN, 128), 1)

    def pick(array, at):
        return jnp.sum(jnp.where(lane == at, array, 0.0), axis=1, keepdims=True)

    def combine(home, table):
        for c in range(spans):
            i = home * spans + c
            g0, g1 = gsrc[2 * i], gsrc[2 * i + 1]
            both = count[i] > 1
            s0, s1 = st_home[g0], st_home[g1]
            o0, o1 = o_home[g0, home].astype(jnp.float32), o_home[g1, home].astype(jnp.float32)
            mine = u[i].astype(jnp.float32)
            pieces = []
            for h in range(u.shape[2] // HEAD_DIM):
                part = slice(h * HEAD_DIM, (h + 1) * HEAD_DIM)
                at = 4 * home + 2 * h
                m0, l0 = pick(s0, at), pick(s0, at + 1)
                m1 = jnp.where(both, pick(s1, at), -1e30)
                l1 = jnp.where(both, pick(s1, at + 1), 0.0)
                peak = jnp.maximum(m0, m1)
                a0, a1 = jnp.exp(m0 - peak), jnp.exp(m1 - peak)
                total = a0 * l0 + a1 * l1
                piece = (a0 / total) * o0[:, part] + (a1 / total) * jnp.where(both, o1[:, part], 0.0)
                pieces.append(piece.astype(jnp.bfloat16))
                centre = jnp.sum(piece * mine[:, part], axis=1, keepdims=True)
                table = jnp.where(lane == 4 * i + h, peak + jnp.log(total), table)
                table = jnp.where(lane == 4 * i + 2 + h, centre, table)
            att[i] = jnp.concatenate(pieces, axis=1)
        return table

    hs[...] = lax.fori_loop(0, nf, combine, jnp.zeros((SPAN, 128), jnp.float32))
    gives = [
        remote(hs, hs_out.at[dp], hsn.at[i], hr.at[i], "dp", p) for i, p in enumerate(peers)
    ]
    for move in gives:
        move.start()
    hs_own = pltpu.make_async_copy(hs, hs_out.at[dp], own.at[2])
    hs_own.start()
    for move in stats + outs:
        move.wait_send()
    for move in gives:
        move.wait()
    hs_own.wait()


def backward_kernel(nf, spans, refs, q, u, hs, kt, vt, dq_ref, dk_ref, dv_ref, k_acc, v_acc):
    lane = lax.broadcasted_iota(jnp.int32, (SPAN, 128), 1)
    pieces, nbrs, piece = kt.shape[0], kt.shape[1], kt.shape[2]
    length = pieces * piece

    @pl.loop(0, nbrs)
    def _(n):
        k_acc[n] = jnp.zeros(k_acc.shape[1:], jnp.float32)
        v_acc[n] = jnp.zeros(v_acc.shape[1:], jnp.float32)

    def pick(array, at):
        return jnp.sum(jnp.where(lane == at, array, 0.0), axis=1, keepdims=True)

    @pl.loop(0, (refs[0] + UNROLL - 1) // UNROLL)
    def _(step):
        done = []
        for more in range(UNROLL):
            j = step * UNROLL + more
            r, n, c, into = (refs[1 + 4 * j + i] for i in range(4))
            keys = kt[:, n].reshape(length, -1)
            values = vt[:, n].reshape(length, -1)
            query, up, table = q[r], u[r], hs[r // nf]
            at = 4 * ((r % nf) * spans + c)
            dqs, dks, dvs = [], [], []
            for h in range(keys.shape[1] // HEAD_DIM):
                part = slice(h * HEAD_DIM, (h + 1) * HEAD_DIM)
                scores = dot(query[:, part], keys[:, part], NT) * SCALE
                probs = jnp.exp(scores - pick(table, at + h))
                dprobs = dot(up[:, part], values[:, part], NT)
                ds = (probs * (dprobs - pick(table, at + 2 + h)) * SCALE).astype(jnp.bfloat16)
                dqs.append(dot(ds, keys[:, part], NN).astype(jnp.bfloat16))
                dks.append(dot(ds, query[:, part], TN))
                dvs.append(dot(probs.astype(jnp.bfloat16), up[:, part], TN))
            done.append((r, into, dqs, dks, dvs))
        for r, into, dqs, dks, dvs in done:
            dq_ref[r] = jnp.concatenate(dqs, axis=1)
            k_acc[into] += jnp.concatenate(dks, axis=1)
            v_acc[into] += jnp.concatenate(dvs, axis=1)

    @pl.loop(0, nbrs)
    def _(n):
        dk_ref[:, n] = k_acc[n].reshape(pieces, piece, -1).astype(jnp.bfloat16)
        dv_ref[:, n] = v_acc[n].reshape(pieces, piece, -1).astype(jnp.bfloat16)


def return_kernel(
    nd, nf, width, spans, gsrc, count, att, cot, dq, dk, dv, gq, gk, gv, gp, att_all,
    dq_home, dq_sum, k_own, v_own, cot_vm, term, shares, total,
    qs, qr, ks, kr, vs, vr, ys, yr, fa, ga, ba, ca, ts, tr, ps, pr, own, load,
):
    dp, fs = lax.axis_index("dp"), lax.axis_index("fsdp")
    chips = nf // 2
    chip, core = fs // 2, lax.rem(fs, 2)
    sibling = chip * 2 + 1 - core
    load_cot = pltpu.make_async_copy(cot, cot_vm, load.at[0])
    load_cot.start()
    enter((("dp", nd), ("fsdp", nf)))
    peers = [lax.rem(dp + step, nd) for step in range(1, nd)]
    firsts = [
        pltpu.make_async_copy(att, att_all.at[fs], own.at[6]),
        pltpu.make_async_copy(dq.at[dp], dq_home.at[dp], own.at[0]),
        pltpu.make_async_copy(dk.at[fs], k_own, own.at[1]),
        pltpu.make_async_copy(dv.at[fs], v_own, own.at[2]),
    ]
    for copy in firsts:
        copy.start()
    backs = [
        remote(dq.at[p], dq_home.at[dp], qs.at[i], qr.at[i], "dp", p) for i, p in enumerate(peers)
    ]
    for move in backs:
        move.start()
    to_sibling = [remote(att, att_all.at[fs], fa.at[chips - 1], ga.at[chips - 1], "fsdp", sibling)]
    to_sibling[0].start()
    around = []
    for step in range(chips - 1):
        there = lax.rem(chip + step + 1, chips) * 2 + core
        move = remote(att, att_all.at[fs], ba.at[step], ca.at[step], "fsdp", there)
        move.start()
        around.append(move)
    moves = []
    for ref, out, s_sem, r_sem in ((dk, gk, ks, kr), (dv, gv, vs, vr)):
        for step in range(1, nf):
            peer = lax.rem(fs + step, nf)
            move = remote(ref.at[peer], cols(out, fs, width), s_sem.at[step], r_sem.at[step], "fsdp", peer)
            move.start()
            moves.append(move)
    for copy in firsts:
        copy.wait()
    puts = [
        pltpu.make_async_copy(k_own, cols(gk, fs, width), own.at[3]),
        pltpu.make_async_copy(v_own, cols(gv, fs, width), own.at[4]),
    ]
    for put in puts:
        put.start()
    load_cot.wait()
    share = width // nd
    columns = cot_vm.shape[1]
    tile = 256

    def add_dq():
        for move in backs:
            move.wait_recv()

        @pl.loop(0, nf)
        def _(home):
            for c in range(spans):
                i = home * spans + c
                d0 = dq_home[gsrc[2 * i], home].astype(jnp.float32)
                d1 = dq_home[gsrc[2 * i + 1], home].astype(jnp.float32)
                dq_sum[home, c] = (d0 + jnp.where(count[i] > 1, d1, 0.0)).astype(jnp.bfloat16)

        for step in range(1, nf):
            peer = lax.rem(fs + step, nf)
            move = remote(dq_sum.at[peer], cols(gq, fs, width), ys.at[step], yr.at[step], "fsdp", peer)
            move.start()
            moves.append(move)
        put = pltpu.make_async_copy(dq_sum.at[fs], cols(gq, fs, width), own.at[5])
        put.start()
        puts.append(put)

    scatters = []

    def project(turn, block):
        @pl.loop(0, columns // tile)
        def _(t):
            at = pl.ds(pl.multiple_of(t * tile, tile), tile)
            value = dot(att_all[block], cot_vm[:, at], TN).astype(jnp.bfloat16)
            term[turn, :, :, at] = value.reshape(nd, share, tile)

        sent = [
            remote(term.at[turn, p], shares.at[turn, i], ts.at[turn, i], tr.at[turn, i], "dp", p)
            for i, p in enumerate(peers)
        ]
        for move in sent:
            move.start()
        scatters.append((block, sent))

    def finish(turn):
        block, sent = scatters[turn]
        for move in sent:
            move.wait_recv()
        value = term[turn, dp].astype(jnp.float32)
        for i in range(nd - 1):
            value += shares[turn, i].astype(jnp.float32)
        total[turn] = value.astype(jnp.bfloat16)
        here = pl.ds(pl.multiple_of(block * width + dp * share, share), share)
        for i, p in enumerate(peers):
            move = remote(total.at[turn], gp.at[here], ps.at[turn, i], pr.at[turn, i], "dp", p)
            move.start()
            moves.append(move)
        put = pltpu.make_async_copy(total.at[turn], gp.at[here], load.at[1 + turn])
        put.start()
        puts.append(put)

    project(0, fs)
    to_sibling[0].wait_recv()
    project(1, sibling)
    turn = 2
    order = [0, chips - 2] + list(range(1, chips - 2))
    for step in order:
        back = lax.rem(chip + chips - step - 1, chips) * 2
        around[step].wait_recv()
        move = remote(
            att_all.at[back + core], att_all.at[back + core], fa.at[step], ga.at[step], "fsdp", sibling
        )
        move.start()
        to_sibling.append(move)
        project(turn, back + core)
        if turn == 2:
            add_dq()
        finish((turn - 2))
        move.wait_recv()
        project(turn + 1, back + 1 - core)
        finish((turn - 1))
        turn += 2
    for last in range(turn - 2, turn):
        finish(last)
    for move in backs + to_sibling + around:
        move.wait_send()
    for _, sent in scatters:
        for move in sent:
            move.wait_send()
    for move in moves:
        move.wait()
    for put in puts:
        put.wait()


def dma(*shape):
    return pltpu.SemaphoreType.DMA(shape)


def comm(number, mib=BIG):
    return pltpu.CompilerParams(collective_id=number, has_side_effects=True, vmem_limit_bytes=mib)


def local(queries, nbr_keys, nbr_values, out_proj, nbr_source, nbr_index, nbr_count, cotangent):
    nd, nf = lax.axis_size("dp"), lax.axis_size("fsdp")
    bf, f32, i32 = jnp.bfloat16, jnp.float32, jnp.int32
    token_rows, full_width = queries.shape
    spans = token_rows // SPAN
    nbrs, piece, _ = nbr_keys.shape
    width = full_width // nf
    rows, columns = cotangent.shape
    slots = SLOTS * spans
    refs_all = nd * nf
    me = lax.axis_index("dp")

    sources = nbr_source.reshape(nd, nf, slots)
    indices = nbr_index.reshape(nd, nf, slots)
    counts = nbr_count.reshape(nd, nf, spans)
    slot = jnp.arange(slots, dtype=i32)
    my_sources = lax.dynamic_index_in_dim(sources, me, 0, keepdims=False)
    my_counts = lax.dynamic_index_in_dim(counts, me, 0, keepdims=False)
    hit = my_sources[None] == jnp.arange(nd, dtype=i32)[:, None, None]
    selc = jnp.sum(jnp.where(hit, slot // SLOTS, 0), axis=2)
    gsrc = my_sources.reshape(-1)
    count = my_counts.reshape(-1)
    alive = jnp.logical_and(
        sources == me, (slot % SLOTS)[None, None] < jnp.repeat(counts, SLOTS, axis=2)
    ).reshape(refs_all, slots)
    live = jnp.any(alive, axis=1)
    nidx = jnp.sum(jnp.where(alive, indices.reshape(refs_all, slots), 0), axis=1)
    cidx = jnp.sum(jnp.where(alive, slot // SLOTS, 0), axis=1)
    ref_iota = jnp.arange(refs_all, dtype=i32)
    key = jnp.where(live, 0, refs_all) + ref_iota
    rank = jnp.sum(key[None, :] < key[:, None], axis=1)
    place = rank[None, :] == ref_iota[:, None]
    entry = jnp.stack([ref_iota, nidx, cidx, jnp.where(live, nidx, nbrs)], axis=1)
    listed = jnp.sum(jnp.where(place[:, :, None], entry[None], 0), axis=1)
    refs = jnp.concatenate([jnp.sum(live.astype(i32))[None], listed.reshape(-1)])

    chips = nf // 2
    kt, vt, qg, ug, upstream = pl.pallas_call(
        lambda *a: spread_kernel(nd, nf, width, *a),
        in_specs=[SM, ANY, ANY, ANY, ANY, ANY],
        out_specs=[ANY, ANY, ANY, ANY, VM],
        out_shape=[
            jax.ShapeDtypeStruct((nf, nbrs, piece, width), bf),
            jax.ShapeDtypeStruct((nf, nbrs, piece, width), bf),
            jax.ShapeDtypeStruct((nd, nf, SPAN, width), bf),
            jax.ShapeDtypeStruct((nd, nf, SPAN, width), bf),
            jax.ShapeDtypeStruct((nf * spans, SPAN, width), bf),
        ],
        scratch_shapes=[
            pltpu.VMEM((nf, spans, SPAN, width), bf),
            pltpu.VMEM((2, nd, nf, SPAN, width), bf),
            pltpu.VMEM((nbrs, piece, width), bf),
            pltpu.VMEM((nbrs, piece, width), bf),
            pltpu.VMEM((rows, columns), bf),
            pltpu.VMEM((full_width, columns), bf),
            pltpu.VMEM((chips, rows, width), bf),
            pltpu.VMEM((chips, rows, width), bf),
            pltpu.VMEM((chips, rows, width), f32),
            pltpu.VMEM((chips - 1, rows, width), bf),
            pltpu.VMEM((chips - 1, rows, width), bf),
            dma(nf), dma(nf), dma(nf), dma(nf), dma(nf), dma(nf), dma(nd), dma(nd), dma(nd), dma(nd),
            dma(chips), dma(chips), dma(chips), dma(chips), dma(7), dma(2),
        ],
        compiler_params=comm(1),
        name="spread",
    )(selc, queries.reshape(spans, SPAN, full_width), nbr_keys, nbr_values, cotangent, out_proj)
    qr = qg.reshape(refs_all, SPAN, width)

    o, st = pl.pallas_call(
        lambda *a: forward_kernel(nf, *a),
        in_specs=[SM, VM, VM, VM],
        out_specs=[VM, VM],
        out_shape=[
            jax.ShapeDtypeStruct((refs_all, SPAN, width), bf),
            jax.ShapeDtypeStruct((nd, SPAN, 128), f32),
        ],
        compiler_params=pltpu.CompilerParams(vmem_limit_bytes=BIG),
        name="forward",
    )(refs, qr, kt, vt)

    hs, att = pl.pallas_call(
        lambda *a: meet_kernel(nd, nf, spans, *a),
        in_specs=[SM, SM, VM, ANY, ANY],
        out_specs=[ANY, VM],
        out_shape=[
            jax.ShapeDtypeStruct((nd, SPAN, 128), f32),
            jax.ShapeDtypeStruct((nf * spans, SPAN, width), bf),
        ],
        scratch_shapes=[
            pltpu.VMEM((nd, nf, SPAN, width), bf),
            pltpu.VMEM((nd, SPAN, 128), f32),
            pltpu.VMEM((SPAN, 128), f32),
            dma(nd), dma(nd), dma(nd), dma(nd), dma(nd), dma(nd), dma(3),
        ],
        compiler_params=comm(2),
        name="meet",
    )(gsrc, count, upstream, o.reshape(nd, nf, SPAN, width), st)

    dq, dk, dv = pl.pallas_call(
        lambda *a: backward_kernel(nf, spans, *a),
        in_specs=[SM, VM, VM, VM, VM, VM],
        out_specs=[VM, VM, VM],
        out_shape=[
            jax.ShapeDtypeStruct((refs_all, SPAN, width), bf),
            jax.ShapeDtypeStruct((nf, nbrs, piece, width), bf),
            jax.ShapeDtypeStruct((nf, nbrs, piece, width), bf),
        ],
        scratch_shapes=[
            pltpu.VMEM((nbrs + 1, nf * piece, width), f32),
            pltpu.VMEM((nbrs + 1, nf * piece, width), f32),
        ],
        compiler_params=pltpu.CompilerParams(vmem_limit_bytes=BIG),
        name="backward",
    )(refs, qr, ug.reshape(refs_all, SPAN, width), hs, kt, vt)

    gq, gk, gv, grad_proj, gathered = pl.pallas_call(
        lambda *a: return_kernel(nd, nf, width, spans, *a),
        in_specs=[SM, SM, ANY, ANY, ANY, ANY, ANY],
        out_specs=[ANY, ANY, ANY, ANY, VM],
        out_shape=[
            jax.ShapeDtypeStruct((spans, SPAN, full_width), bf),
            jax.ShapeDtypeStruct((nbrs, piece, full_width), bf),
            jax.ShapeDtypeStruct((nbrs, piece, full_width), bf),
            jax.ShapeDtypeStruct((full_width, columns), bf),
            jax.ShapeDtypeStruct((nf, rows, width), bf),
        ],
        scratch_shapes=[
            pltpu.VMEM((nd, nf, SPAN, width), bf),
            pltpu.VMEM((nf, spans, SPAN, width), bf),
            pltpu.VMEM((nbrs, piece, width), bf),
            pltpu.VMEM((nbrs, piece, width), bf),
            pltpu.VMEM((rows, columns), bf),
            pltpu.VMEM((nf, nd, width // nd, columns), bf),
            pltpu.VMEM((nf, nd - 1, width // nd, columns), bf),
            pltpu.VMEM((nf, width // nd, columns), bf),
            dma(nd), dma(nd), dma(nf), dma(nf), dma(nf), dma(nf), dma(nf), dma(nf),
            dma(chips), dma(chips), dma(chips), dma(chips),
            dma(nf, nd), dma(nf, nd), dma(nf, nd), dma(nf, nd), dma(7), dma(1 + nf),
        ],
        compiler_params=comm(3),
        name="giveback",
    )(gsrc, count, att.reshape(rows, width), cotangent, dq.reshape(nd, nf, SPAN, width), dk, dv)
    my_rows = lax.dynamic_slice_in_dim(
        gathered, lax.axis_index("fsdp") * token_rows, token_rows, axis=1
    )
    attended = jnp.transpose(my_rows, (1, 0, 2)).reshape(token_rows, full_width)
    return (attended, gq.reshape(token_rows, full_width), gk, gv, grad_proj)


def solution(mesh):
    placed = (
        P(("dp", "fsdp"), "enc"),
        P("dp", "fsdp", "enc"),
        P("dp", "fsdp", "enc"),
        P("enc", "fsdp"),
        P(),
        P(),
        P(),
        P("dp", "fsdp"),
    )
    return jax.shard_map(
        local,
        mesh=mesh,
        in_specs=placed,
        out_specs=(
            P(("dp", "fsdp"), "enc"),
            P(("dp", "fsdp"), "enc"),
            P("dp", "fsdp", "enc"),
            P("dp", "fsdp", "enc"),
            P("enc", "fsdp"),
        ),
        check_vma=False,
    )
```

time: 441 us -> 380 us (0.86); the launches traced: 440 us -> 374 us
  waiting for transfers between devices: 56.5 us -> 0 us
  between operations: 13.9 us -> 0.82 us
    all_gather x1 -> x0, waiting for transfers between devices: 45.5 us -> none  [local(): lax.all_gather(att.reshape(rows, width), 'fsdp', axis=0, tiled=True)]
    pallas_call x1, Pallas kernels: 86.5 us -> 126 us  [local(): pl.pallas_call(lambda *a: return_kernel(nd, nf, width, spans, *a), in_spe...]
    pallas_call x2 -> x0, Pallas kernels: 24.4 us -> none  [the longest x1 12.2 us: local(): pl.pallas_call(upstream_kernel, grid=(nf,), in_specs=[pl.BlockSpec((rows,...]
    pallas_call x1, Pallas kernels: 71.5 us -> 53.4 us  [local(): pl.pallas_call(lambda *a: meet_kernel(nd, nf, spans, *a), in_specs=[SM, S...]
    psum x1 -> x0, waiting for transfers between devices: 10.9 us -> none  [local(): grad_proj = lax.psum(term, 'dp')]
    pallas_call x1, Pallas kernels: 112 us -> 119 us  [local(): pl.pallas_call(lambda *a: spread_kernel(nd, nf, width, *a), in_specs=[SM,...]
    unnamed x18 -> x12, local copies, waits for them, and re-layouts: 12.5 us -> 12.6 us
  transfers between devices with their start and end apart: 3 -> 0, of which waited for: 2 -> 0; matrix products, arithmetic and copies ran while one was open for 2% -> 0% of each run, Pallas kernels for 58% -> 0%
where the time goes in v2:
time: 380 us; the launch traced here: 374 us
  Pallas kernels  353 us (93%)
  local copies, waits for them, and re-layouts  16.7 us (4%)
  other arithmetic  4.08 us (1%)
    pallas_call x1, Pallas kernels, local(): pl.pallas_call(lambda *a: return_kernel(nd, nf, width, spans, *a), in_spe...  126 us
    pallas_call x1, Pallas kernels, local(): pl.pallas_call(lambda *a: spread_kernel(nd, nf, width, *a), in_specs=[SM,...  119 us
    pallas_call x1, Pallas kernels, local(): pl.pallas_call(lambda *a: meet_kernel(nd, nf, spans, *a), in_specs=[SM, S...  53.4 us
    pallas_call x1, Pallas kernels, local(): pl.pallas_call(lambda *a: backward_kernel(nf, spans, *a), in_specs=[SM, V...  29 us
    pallas_call x1, Pallas kernels, local(): pl.pallas_call(lambda *a: forward_kernel(nf, *a), in_specs=[SM, VM, VM, V...  24.9 us
    unnamed x12, local copies, waits for them, and re-layouts  12.6 us

profile of v2, /device:TPU:0, one launch (start us, length us, event | category | flops | bytes accessed | tf_op | source)
XLA Modules:
  0.0 374.5 jit_solution(5990117543733957762)
XLA Ops:
  0.7 0.8 reshape.136
  1.5 0.6 reshape.137.a_1_
  2.1 0.1 broadcast_in_dim.76
  2.3 0.1 lt.45
  2.4 0.7 select_reduce_fusion.2
  3.2 0.2 reduce_or.15
  3.3 0.1 reduce_or.20
  3.5 0.6 convert_reduce_fusion.1
  4.1 0.2 convert_reduce_fusion
  4.3 0.1 reduce_sum.75
  4.4 0.1 reduce_sum.76
  4.6 0.1 reduce_sum.72
  4.7 0.1 reduce_sum.73
  4.9 0.1 select_reduce_fusion
  5.1 0.1 reshape.139
  5.2 1.3 pad_add_fusion.1.a_0_
  6.5 0.8 copy.18
  7.4 0.7 reshape.135.a_0_
  8.2 0.7 select_reduce_fusion.1.a_0_
  8.8 119.2 %spread.1 = (bf16[8,48,16,256]{3,2,1,0:T(8,128)(2,1)}, bf16[8,48,16,256]{3,2,1,0:T(8,128)(2,1)}, bf16[8,8,64,256]{3,2,1,0:T(8,128)(2,1)}, bf16[8,8,64,256]{3,2,1,0:T(8,128)(2,1)}, bf16[24,64,256]{2,1,0:T(8,128)(2,1)}) custom-call(s32[8,8]{1,0:T(8,128)} %select_reduce_fusion.1.a_0_, bf16[3,64,2048]{2,1,0:T(8,128)(2,1)} %bitcast.31, ...), custom_call_target="tpu_custom_call" | custom-call | tf_op jit(solution)/shard_map/spread/pallas_call | solution.py:519
  128.0 24.9 %forward.1 = (bf16[64,64,256]{2,1,0:T(8,128)(2,1)}, f32[8,64,128]{2,1,0:T(8,128)}) custom-call(s32[257]{0:T(512)} %pad_add_fusion.1.a_0_, bf16[64,64,256]{2,1,0:T(8,128)(2,1)} %bitcast.23, bf16[8,48,16,256]{3,2,1,0:T(8,128)(2,1)} %get-tuple-element.24.a_2_.a_4_, bf16[8,48,16,256]{3,2,1,0:T(8,128)(2,1)} %get-tuple-element.25.a_3_.a_5_), custom_call_target="tpu_custom_call" | custom-call | tf_op jit(solution)/shard_map/forward/pallas_call | solution.py:550
  152.9 53.4 %meet.1 = (f32[8,64,128]{2,1,0:T(8,128)}, bf16[24,64,256]{2,1,0:T(8,128)(2,1)}) custom-call(s32[48]{0:T(128)} %reshape.135.a_0_, s32[24]{0:T(128)} %reshape.137.a_1_, bf16[24,64,256]{2,1,0:T(8,128)(2,1)} %get-tuple-element.22.a_2_, bf16[8,8,64,256]{3,2,1,0:T(8,128)(2,1)} %bitcast.26, f32[8,64,128]{2,1,0:T(8,128)} %get-tuple-element.27.a_4_), custom_call_target="tpu_custom_call" | custom-call | tf_op jit(solution)/shard_map/meet/pallas_call | solution.py:562
  206.4 29.0 %backward.1 = (bf16[64,64,256]{2,1,0:T(8,128)(2,1)}, bf16[8,48,16,256]{3,2,1,0:T(8,128)(2,1)}, bf16[8,48,16,256]{3,2,1,0:T(8,128)(2,1)}) custom-call(s32[257]{0:T(512)} %pad_add_fusion.1.a_0_, bf16[64,64,256]{2,1,0:T(8,128)(2,1)} %bitcast.24, bf16[64,64,256]{2,1,0:T(8,128)(2,1)} %bitcast.27, f32[8,64,128]{2,1,0:T(8,128)} %get-tuple-element.30.a_3_, ...), custom_call_target="tpu_custom_call" | custom-call | tf_op jit(solution)/shard_map/backward/pallas_call | solution.py:580
  235.4 126.3 %giveback.1 = (bf16[3,64,2048]{2,1,0:T(8,128)(2,1)}, bf16[48,16,2048]{2,1,0:T(8,128)(2,1)}, bf16[48,16,2048]{2,1,0:T(8,128)(2,1)}, bf16[2048,1024]{1,0:T(8,128)(2,1)}, bf16[8,1536,256]{2,1,0:T(8,128)(2,1)}) custom-call(s32[48]{0:T(128)} %reshape.135.a_0_, s32[24]{0:T(128)} %reshape.137.a_1_, bf16[1536,256]{1,0:T(8,128)(2,1)} %bitcast.28, ...), custom_call_target="tpu_custom_call" | custom-call | tf_op jit(solution)/shard_map/giveback/pallas_call | solution.py:597
  361.7 1.3 dynamic-slice_bitcast_fusion
  363.0 1.0 copy.22
  364.0 2.1 copy.27
  366.1 1.7 copy.28
  367.8 1.4 copy-done.1
  369.1 1.7 copy.29
  370.8 1.7 copy-done
  372.4 2.0 copy.30
  (19 shorter events, 0.4 us)
Async XLA Ops:
  361.7 4.4 %copy-start.2 = (bf16[48,16,2048]{2,1,0:T(8,128)(2,1)S(1)}, bf16[48,16,2048]{2,1,0:T(8,128)(2,1)}, u32[]{:S(2)}) copy-start(bf16[48,16,2048]{2,1,0:T(8,128)(2,1)} %get-tuple-element.53) | copy-start | bytes 9437188
  366.1 3.0 copy-start.1
  369.1 3.3 copy-start

commit v3 on v2

v3 whole, which is shorter than its diff:
```python
import math

import jax
import jax.numpy as jnp
from jax import lax
from jax.experimental import pallas as pl
from jax.experimental.pallas import tpu as pltpu
from jax.sharding import PartitionSpec as P

HEAD_DIM = 128
SPAN = 64
SLOTS = 2
MESH = pl.DeviceIdType.MESH
ANY = pl.BlockSpec(memory_space=pl.ANY)
VM = pl.BlockSpec(memory_space=pltpu.VMEM)
SM = pl.BlockSpec(memory_space=pltpu.SMEM)
NT = (((1,), (1,)), ((), ()))
TN = (((0,), (0,)), ((), ()))
NN = (((1,), (0,)), ((), ()))
SCALE = 1.0 / math.sqrt(HEAD_DIM)
BIG = 60 << 20


def dot(a, b, dims):
    return lax.dot_general(a, b, dims, preferred_element_type=jnp.float32)


def enter(axes):
    barrier = pltpu.get_barrier_semaphore()
    total = 0
    for axis, size in axes:
        here = lax.axis_index(axis)
        for step in range(1, size):
            pl.semaphore_signal(
                barrier, inc=1, device_id={axis: lax.rem(here + step, size)}, device_id_type=MESH
            )
            total += 1
    pl.semaphore_wait(barrier, total)


def remote(src, dst, send, recv, axis, peer):
    return pltpu.make_async_remote_copy(
        src_ref=src, dst_ref=dst, send_sem=send, recv_sem=recv, device_id={axis: peer}, device_id_type=MESH
    )


def cols(ref, place, width):
    return ref.at[:, :, pl.ds(pl.multiple_of(place * width, width), width)]


def spread_kernel(
    nd, nf, width, src, idx, cnt, q, k, v, cot, proj, kt, vt, qg, ug, hs_out, tab,
    q_heads, send, kt_vm, vt_a, vt_b, qg_vm, ug_vm, u_vm, cot_vm, proj_vm, sib_send, sib_recv, mine, ring_send,
    ring_recv, probs, st, st_home, hs, sel,
    qs, qr, ks, kr, vs, vr, gs, gr, us, ur, bs, br, rs, rr, ss, sr, hsn, hr, own, load,
):
    dp, fs = lax.axis_index("dp"), lax.axis_index("fsdp")
    chips = nf // 2
    chip, core = fs // 2, lax.rem(fs, 2)
    sibling = chip * 2 + 1 - core
    spans = q_heads.shape[1]
    slots = SLOTS * spans
    heads = width // HEAD_DIM
    peers = [lax.rem(dp + step, nd) for step in range(1, nd)]
    loads = [
        pltpu.make_async_copy(cot, cot_vm, load.at[0]),
        pltpu.make_async_copy(proj, proj_vm, load.at[1]),
    ]
    for copy in loads:
        copy.start()
    enter((("dp", nd), ("fsdp", nf)))
    vt_vm = (vt_a, vt_b)

    def v_part(place, head):
        at = pl.multiple_of(place * width + head * HEAD_DIM, HEAD_DIM)
        return v.at[:, :, pl.ds(at, HEAD_DIM)]

    owns = [
        pltpu.make_async_copy(cols(q, fs, width), q_heads.at[fs], own.at[0]),
        pltpu.make_async_copy(cols(k, fs, width), kt_vm.at[fs], own.at[1]),
    ] + [
        pltpu.make_async_copy(v_part(fs, head), vt_vm[head].at[fs], own.at[(2, 11)[head]]) for head in range(heads)
    ]
    for copy in owns:
        copy.start()

    def spread(ref, out, s_sem, r_sem, head=None):
        moves = []
        for step in range(1, nf):
            peer = lax.rem(fs + step, nf)
            if head is None:
                source, target, place = cols(ref, peer, width), out.at[fs], step
            else:
                source, target = v_part(peer, head), vt_vm[head].at[fs]
                place = head * nf + step
            move = remote(source, target, s_sem.at[place], r_sem.at[place], "fsdp", peer)
            move.start()
            moves.append(move)
        return moves

    q_moves = spread(q, q_heads, qs, qr)
    k_moves = spread(k, kt_vm, ks, kr)
    for copy in loads:
        copy.wait()
    rows = cot_vm.shape[0]
    tile = 512
    sib_moves = []
    for step in range(chips):
        there = lax.rem(chip + step + 1, chips)
        for which in (1 - core, core):
            block = pl.multiple_of((there * 2 + which) * width, width)
            first = len(sib_moves) == step

            @pl.loop(0, rows // tile)
            def _(t):
                at = pl.multiple_of(t * tile, tile)
                value = dot(cot_vm[pl.ds(at, tile), :], proj_vm[pl.ds(block, width), :], NT)
                if first:
                    sib_send[step, pl.ds(at, tile), :] = value.astype(jnp.bfloat16)
                else:
                    mine[step, pl.ds(at, tile), :] = value

            if first:
                move = remote(sib_send.at[step], sib_recv.at[step], bs.at[step], br.at[step], "fsdp", sibling)
                move.start()
                sib_moves.append(move)
    ring_moves = []
    for step in range(chips - 1):
        there = lax.rem(chip + step + 1, chips)
        sib_moves[step].wait_recv()

        @pl.loop(0, rows // tile)
        def _(t):
            at = pl.ds(pl.multiple_of(t * tile, tile), tile)
            ring_send[step, at, :] = (
                mine[step, at, :] + sib_recv[step, at, :].astype(jnp.float32)
            ).astype(jnp.bfloat16)

        move = remote(
            ring_send.at[step], ring_recv.at[step], rs.at[step], rr.at[step], "fsdp", there * 2 + core
        )
        move.start()
        ring_moves.append(move)
    v_moves = [spread(v, None, vs, vr, head) for head in range(heads)]

    @pl.loop(0, nd)
    def _(group):
        @pl.loop(0, nf)
        def _(home):
            base = (dp * nf + home) * slots
            span = jnp.int32(0)
            for t in range(slots):
                span = jnp.where(src[base + t] == group, t // SLOTS, span)
            sel[group * nf + home] = span
            r = group * nf + home
            number, where, live = jnp.int32(0), jnp.int32(0), jnp.int32(0)
            for t in range(slots):
                hit = jnp.logical_and(
                    src[r * slots + t] == dp, t % SLOTS < cnt[r * spans + t // SLOTS]
                )
                number = jnp.where(hit, idx[r * slots + t], number)
                where = jnp.where(hit, t // SLOTS, where)
                live = jnp.where(hit, 1, live)
            tab[r] = number
            tab[nd * nf + r] = where
            tab[2 * nd * nf + r] = live

    owns[0].wait()
    for move in q_moves:
        move.wait_recv()
    puts = []

    def deliver(kind, source, out, s_sem, r_sem):
        @pl.loop(0, nd)
        def _(group):
            @pl.loop(0, nf)
            def _(home):
                send[kind, group, home] = source(home, sel[group * nf + home])

        moves = [
            remote(send.at[kind, p], out.at[dp], s_sem.at[i], r_sem.at[i], "dp", p)
            for i, p in enumerate(peers)
        ]
        for move in moves:
            move.start()
        put = pltpu.make_async_copy(send.at[kind, dp], out.at[dp], own.at[3 + kind])
        put.start()
        return moves, put

    def store(source, out, number):
        put = pltpu.make_async_copy(source, out, own.at[number])
        put.start()
        puts.append(put)

    q_there, q_put = deliver(0, lambda home, c: q_heads[home, c], qg_vm, gs, gr)
    q_put.wait()
    for move in q_there:
        move.wait_recv()
    owns[1].wait()
    for move in k_moves:
        move.wait_recv()
    store(qg_vm, qg, 5)
    store(kt_vm, kt, 6)
    lane = lax.broadcasted_iota(jnp.int32, (SPAN, 128), 1)
    length = kt_vm.shape[0] * kt_vm.shape[2]
    group_lanes = heads * nf

    @pl.loop(0, nd)
    def _(d):
        marks = jnp.zeros((SPAN, 128), jnp.float32)
        for f in range(nf):
            n = tab[d * nf + f]
            for h in range(heads):
                part = slice(h * HEAD_DIM, (h + 1) * HEAD_DIM)
                keys = kt_vm[:, n, :, part].reshape(length, HEAD_DIM)
                scores = dot(qg_vm[d, f, :, part], keys, NT) * SCALE
                peak = jnp.max(scores, axis=1, keepdims=True)
                expo = jnp.exp(scores - peak)
                probs[h, d * nf + f] = expo
                marks = jnp.where(lane == heads * f + h, peak, marks)
                total = jnp.sum(expo, axis=1, keepdims=True)
                marks = jnp.where(lane == group_lanes + heads * f + h, total, marks)
        st[d] = marks

    sib_moves[chips - 1].wait_recv()
    for move in ring_moves:
        move.wait_recv()

    @pl.loop(0, rows // SPAN)
    def _(i):
        at = pl.ds(pl.multiple_of(i * SPAN, SPAN), SPAN)
        value = mine[chips - 1, at, :] + sib_recv[chips - 1, at, :].astype(jnp.float32)
        for step in range(chips - 1):
            value += ring_recv[step, at, :].astype(jnp.float32)
        u_vm[i] = value.astype(jnp.bfloat16)

    u_there, u_put = deliver(1, lambda home, c: u_vm[home * spans + c], ug_vm, us, ur)
    u_put.wait()
    for move in u_there:
        move.wait_recv()
    store(ug_vm, ug, 7)
    for h in range(heads):
        owns[2 + h].wait()
        for move in v_moves[h]:
            move.wait_recv()
        part = slice(h * HEAD_DIM, (h + 1) * HEAD_DIM)

        @pl.loop(0, nd)
        def _(d):
            marks = st[d]
            for f in range(nf):
                n = tab[d * nf + f]
                values = vt_vm[h][:, n].reshape(length, HEAD_DIM)
                dprobs = dot(ug_vm[d, f, :, part], values, NT)
                mean = jnp.sum(probs[h, d * nf + f] * dprobs, axis=1, keepdims=True)
                marks = jnp.where(lane == 2 * group_lanes + heads * f + h, mean, marks)
            st[d] = marks

    for h in range(heads):
        store(vt_vm[h], vt.at[:, :, :, pl.ds(h * HEAD_DIM, HEAD_DIM)], 8 + 4 * h)
    stats = [
        remote(st.at[p], st_home.at[dp], ss.at[i], sr.at[i], "dp", p) for i, p in enumerate(peers)
    ]
    for move in stats:
        move.start()
    st_put = pltpu.make_async_copy(st.at[dp], st_home.at[dp], own.at[9])
    st_put.start()
    row = lax.broadcasted_iota(jnp.int32, (1, 128), 1)
    place = lax.rem(row, group_lanes) // heads
    sources = []
    both = []
    for t in range(slots):
        values = jnp.zeros((1, 128), jnp.int32)
        for f in range(nf):
            values = jnp.where(place == f, src[(dp * nf + f) * slots + t], values)
        sources.append(values)
    for c in range(spans):
        values = jnp.zeros((1, 128), jnp.int32)
        for f in range(nf):
            values = jnp.where(place == f, cnt[(dp * nf + f) * spans + c], values)
        both.append(values > 1)
    st_put.wait()
    for move in stats:
        move.wait_recv()
    table = jnp.zeros((SPAN, 128), jnp.float32)
    for c in range(spans):
        pair = []
        for slot in range(SLOTS):
            found = jnp.zeros((SPAN, 128), jnp.float32)
            for g in range(nd):
                found = jnp.where(sources[SLOTS * c + slot] == g, st_home[g], found)
            pair.append(
                [found] + [pltpu.roll(found, 128 - group_lanes * i, axis=1) for i in (1, 2)]
            )
        (m0, l0, e0), (m1, l1, e1) = pair
        m1 = jnp.where(both[c], m1, -1e30)
        l1, e1 = jnp.where(both[c], l1, 0.0), jnp.where(both[c], e1, 0.0)
        peak = jnp.maximum(m0, m1)
        a0, a1 = jnp.exp(m0 - peak), jnp.exp(m1 - peak)
        total = a0 * l0 + a1 * l1
        log_total = peak + jnp.log(total)
        centre = (a0 * e0 + a1 * e1) / total
        for value, at in ((log_total, c * group_lanes), (centre, 64 + c * group_lanes)):
            moved = pltpu.roll(value, at, axis=1) if at else value
            inside = jnp.logical_and(lane >= at, lane < at + group_lanes)
            table = jnp.where(inside, moved, table)
    hs[...] = table
    gives = [
        remote(hs, hs_out.at[dp], hsn.at[i], hr.at[i], "dp", p) for i, p in enumerate(peers)
    ]
    for move in gives:
        move.start()
    store(hs, hs_out.at[dp], 10)
    for move in q_moves + k_moves + sib_moves + ring_moves + q_there + u_there + stats + sum(v_moves, []):
        move.wait_send()
    for move in gives:
        move.wait()
    for put in puts:
        put.wait()


UNROLL = 4


def backward_kernel(nf, tab, q, u, hs, kt, vt, o_ref, dq_ref, dk_ref, dv_ref, k_acc, v_acc, listed):
    lane = lax.broadcasted_iota(jnp.int32, (SPAN, 128), 1)
    pieces, nbrs, piece = kt.shape[0], kt.shape[1], kt.shape[2]
    length = pieces * piece
    heads = kt.shape[3] // HEAD_DIM
    refs = q.shape[0]

    def place(r, ends):
        low, high = ends
        live = tab[2 * refs + r]
        listed[jnp.where(live > 0, low, high)] = r
        return low + live, high - 1 + live

    count, _ = lax.fori_loop(0, refs, place, (jnp.int32(0), jnp.int32(refs - 1)))

    @pl.loop(0, nbrs)
    def _(n):
        k_acc[n] = jnp.zeros(k_acc.shape[1:], jnp.float32)
        v_acc[n] = jnp.zeros(v_acc.shape[1:], jnp.float32)

    def pick(array, at):
        return jnp.sum(jnp.where(lane == at, array, 0.0), axis=1, keepdims=True)

    @pl.loop(0, (count + UNROLL - 1) // UNROLL)
    def _(step):
        done = []
        for more in range(UNROLL):
            r = listed[step * UNROLL + more]
            n, c, live = tab[r], tab[refs + r], tab[2 * refs + r]
            into = jnp.where(live > 0, n, nbrs)
            keys = kt[:, n].reshape(length, -1)
            values = vt[:, n].reshape(length, -1)
            query, up, table = q[r], u[r], hs[r // nf]
            at = heads * (nf * c + r % nf)
            outs, dqs, dks, dvs = [], [], [], []
            for h in range(heads):
                part = slice(h * HEAD_DIM, (h + 1) * HEAD_DIM)
                scores = dot(query[:, part], keys[:, part], NT) * SCALE
                probs = jnp.exp(scores - pick(table, at + h))
                rounded = probs.astype(jnp.bfloat16)
                dprobs = dot(up[:, part], values[:, part], NT)
                ds = (probs * (dprobs - pick(table, 64 + at + h)) * SCALE).astype(jnp.bfloat16)
                outs.append(dot(rounded, values[:, part], NN).astype(jnp.bfloat16))
                dqs.append(dot(ds, keys[:, part], NN).astype(jnp.bfloat16))
                dks.append(dot(ds, query[:, part], TN))
                dvs.append(dot(rounded, up[:, part], TN))
            done.append((r, into, outs, dqs, dks, dvs))
        for r, into, outs, dqs, dks, dvs in done:
            o_ref[r] = jnp.concatenate(outs, axis=1)
            dq_ref[r] = jnp.concatenate(dqs, axis=1)
            k_acc[into] += jnp.concatenate(dks, axis=1)
            v_acc[into] += jnp.concatenate(dvs, axis=1)

    @pl.loop(0, nbrs)
    def _(n):
        dk_ref[:, n] = k_acc[n].reshape(pieces, piece, -1).astype(jnp.bfloat16)
        dv_ref[:, n] = v_acc[n].reshape(pieces, piece, -1).astype(jnp.bfloat16)


def return_kernel(
    nd, nf, width, spans, src, cnt, o, cot, dq, dk, dv, ga_out, gq, gk, gv, gp, att_all,
    o_home, dq_home, dq_sum, k_own, v_own, cot_vm, term, shares, total,
    os, orr, qs, qr, ks, kr, vs, vr, ys, yr, fa, ga, ba, ca, ts, tr, ps, pr, own, load, last_sem,
):
    dp, fs = lax.axis_index("dp"), lax.axis_index("fsdp")
    chips = nf // 2
    chip, core = fs // 2, lax.rem(fs, 2)
    sibling = chip * 2 + 1 - core
    load_cot = pltpu.make_async_copy(cot, cot_vm, load.at[0])
    load_cot.start()
    enter((("dp", nd), ("fsdp", nf)))
    peers = [lax.rem(dp + step, nd) for step in range(1, nd)]
    firsts = [
        pltpu.make_async_copy(o.at[dp], o_home.at[dp], own.at[6]),
        pltpu.make_async_copy(dq.at[dp], dq_home.at[dp], own.at[0]),
        pltpu.make_async_copy(dk.at[fs], k_own, own.at[1]),
        pltpu.make_async_copy(dv.at[fs], v_own, own.at[2]),
    ]
    for copy in firsts:
        copy.start()
    outs = [
        remote(o.at[p], o_home.at[dp], os.at[i], orr.at[i], "dp", p) for i, p in enumerate(peers)
    ]
    backs = [
        remote(dq.at[p], dq_home.at[dp], qs.at[i], qr.at[i], "dp", p) for i, p in enumerate(peers)
    ]
    for move in outs + backs:
        move.start()
    moves = []

    def give(ref, out, s_sem, r_sem):
        for step in range(1, nf):
            peer = lax.rem(fs + step, nf)
            move = remote(ref.at[peer], cols(out, fs, width), s_sem.at[step], r_sem.at[step], "fsdp", peer)
            move.start()
            moves.append(move)

    give(dk, gk, ks, kr)
    for copy in firsts:
        copy.wait()
    puts = [
        pltpu.make_async_copy(k_own, cols(gk, fs, width), own.at[3]),
        pltpu.make_async_copy(v_own, cols(gv, fs, width), own.at[4]),
    ]
    for put in puts:
        put.start()

    def add_slots(home, c, parts):
        base = (dp * nf + home) * SLOTS * spans + SLOTS * c
        first = parts[src[base], home].astype(jnp.float32)
        second = parts[src[base + 1], home].astype(jnp.float32)
        both = cnt[(dp * nf + home) * spans + c] > 1
        return (first + jnp.where(both, second, 0.0)).astype(jnp.bfloat16)

    for move in outs:
        move.wait_recv()

    @pl.loop(0, nf)
    def _(home):
        for c in range(spans):
            at = pl.multiple_of((home * spans + c) * SPAN, SPAN)
            att_all[fs, pl.ds(at, SPAN), :] = add_slots(home, c, o_home)

    att = att_all.at[fs]
    to_sibling = [remote(att, att, fa.at[chips - 1], ga.at[chips - 1], "fsdp", sibling)]
    to_sibling[0].start()
    around = []
    for step in range(chips - 1):
        there = lax.rem(chip + step + 1, chips) * 2 + core
        move = remote(att, att, ba.at[step], ca.at[step], "fsdp", there)
        move.start()
        around.append(move)
    give(dv, gv, vs, vr)
    load_cot.wait()
    share = width // nd
    columns = cot_vm.shape[1]
    tile = 256

    def add_dq():
        for move in backs:
            move.wait_recv()

        @pl.loop(0, nf)
        def _(home):
            for c in range(spans):
                dq_sum[home, c] = add_slots(home, c, dq_home)

        for step in range(1, nf):
            peer = lax.rem(fs + step, nf)
            move = remote(dq_sum.at[peer], cols(gq, fs, width), ys.at[step], yr.at[step], "fsdp", peer)
            move.start()
            moves.append(move)
        put = pltpu.make_async_copy(dq_sum.at[fs], cols(gq, fs, width), own.at[5])
        put.start()
        puts.append(put)

    scatters = []

    def project(turn, block):
        @pl.loop(0, columns // tile)
        def _(t):
            at = pl.ds(pl.multiple_of(t * tile, tile), tile)
            value = dot(att_all[block], cot_vm[:, at], TN).astype(jnp.bfloat16)
            term[turn, :, :, at] = value.reshape(nd, share, tile)

        sent = [
            remote(term.at[turn, p], shares.at[turn, i], ts.at[turn, i], tr.at[turn, i], "dp", p)
            for i, p in enumerate(peers)
        ]
        for move in sent:
            move.start()
        scatters.append((block, sent))

    def finish(turn):
        block, sent = scatters[turn]
        for move in sent:
            move.wait_recv()
        value = term[turn, dp].astype(jnp.float32)
        for i in range(nd - 1):
            value += shares[turn, i].astype(jnp.float32)
        total[turn] = value.astype(jnp.bfloat16)
        here = pl.ds(pl.multiple_of(block * width + dp * share, share), share)
        for i, p in enumerate(peers):
            move = remote(total.at[turn], gp.at[here], ps.at[turn, i], pr.at[turn, i], "dp", p)
            move.start()
            moves.append(move)
        put = pltpu.make_async_copy(total.at[turn], gp.at[here], load.at[1 + turn])
        put.start()
        puts.append(put)

    project(0, fs)
    to_sibling[0].wait_recv()
    project(1, sibling)
    turn = 2
    order = [0, chips - 2] + list(range(1, chips - 2))
    for step in order:
        back = lax.rem(chip + chips - step - 1, chips) * 2
        around[step].wait_recv()
        move = remote(
            att_all.at[back + core], att_all.at[back + core], fa.at[step], ga.at[step], "fsdp", sibling
        )
        move.start()
        to_sibling.append(move)
        project(turn, back + core)
        if turn == 2:
            add_dq()
        finish((turn - 2))
        move.wait_recv()
        project(turn + 1, back + 1 - core)
        finish((turn - 1))
        turn += 2
    for last in range(turn - 2, turn):
        finish(last)
    tokens = spans * SPAN
    for block in range(nf):
        here = pl.ds(pl.multiple_of(fs * tokens, tokens), tokens)
        put = pltpu.make_async_copy(
            att_all.at[block, here], ga_out.at[:, pl.ds(block * width, width)], last_sem.at[block]
        )
        put.start()
        puts.append(put)
    for move in outs + backs + to_sibling + around:
        move.wait_send()
    for _, sent in scatters:
        for move in sent:
            move.wait_send()
    for move in moves:
        move.wait()
    for put in puts:
        put.wait()


def dma(*shape):
    return pltpu.SemaphoreType.DMA(shape)


def comm(number, mib=BIG):
    return pltpu.CompilerParams(collective_id=number, has_side_effects=True, vmem_limit_bytes=mib)


def local(queries, nbr_keys, nbr_values, out_proj, nbr_source, nbr_index, nbr_count, cotangent):
    nd, nf = lax.axis_size("dp"), lax.axis_size("fsdp")
    bf, f32, i32 = jnp.bfloat16, jnp.float32, jnp.int32
    token_rows, full_width = queries.shape
    spans = token_rows // SPAN
    nbrs, piece, _ = nbr_keys.shape
    width = full_width // nf
    rows, columns = cotangent.shape
    refs_all = nd * nf
    chips = nf // 2
    sources, indices = nbr_source.reshape(-1), nbr_index.reshape(-1)
    share = width // nd

    kt, vt, qg, ug, hs, tab = pl.pallas_call(
        lambda *a: spread_kernel(nd, nf, width, *a),
        in_specs=[SM, SM, SM, ANY, ANY, ANY, ANY, ANY],
        out_specs=[ANY, ANY, ANY, ANY, ANY, SM],
        out_shape=[
            jax.ShapeDtypeStruct((nf, nbrs, piece, width), bf),
            jax.ShapeDtypeStruct((nf, nbrs, piece, width), bf),
            jax.ShapeDtypeStruct((nd, nf, SPAN, width), bf),
            jax.ShapeDtypeStruct((nd, nf, SPAN, width), bf),
            jax.ShapeDtypeStruct((nd, SPAN, 128), f32),
            jax.ShapeDtypeStruct((3 * refs_all,), i32),
        ],
        scratch_shapes=[
            pltpu.VMEM((nf, spans, SPAN, width), bf),
            pltpu.VMEM((2, nd, nf, SPAN, width), bf),
            pltpu.VMEM((nf, nbrs, piece, width), bf),
            pltpu.VMEM((nf, nbrs, piece, HEAD_DIM), bf),
            pltpu.VMEM((nf, nbrs, piece, HEAD_DIM), bf),
            pltpu.VMEM((nd, nf, SPAN, width), bf),
            pltpu.VMEM((nd, nf, SPAN, width), bf),
            pltpu.VMEM((nf * spans, SPAN, width), bf),
            pltpu.VMEM((rows, columns), bf),
            pltpu.VMEM((full_width, columns), bf),
            pltpu.VMEM((chips, rows, width), bf),
            pltpu.VMEM((chips, rows, width), bf),
            pltpu.VMEM((chips, rows, width), f32),
            pltpu.VMEM((chips - 1, rows, width), bf),
            pltpu.VMEM((chips - 1, rows, width), bf),
            pltpu.VMEM((width // HEAD_DIM, refs_all, SPAN, nf * piece), f32),
            pltpu.VMEM((nd, SPAN, 128), f32),
            pltpu.VMEM((nd, SPAN, 128), f32),
            pltpu.VMEM((SPAN, 128), f32),
            pltpu.SMEM((refs_all,), i32),
            dma(nf), dma(nf), dma(nf), dma(nf), dma(2 * nf), dma(2 * nf), dma(nd), dma(nd), dma(nd), dma(nd),
            dma(chips), dma(chips), dma(chips), dma(chips), dma(nd), dma(nd), dma(nd), dma(nd), dma(13), dma(2),
        ],
        compiler_params=comm(1),
        name="spread",
    )(
        sources, indices, nbr_count, queries.reshape(spans, SPAN, full_width), nbr_keys, nbr_values,
        cotangent, out_proj,
    )

    o, dq, dk, dv = pl.pallas_call(
        lambda *a: backward_kernel(nf, *a),
        in_specs=[SM, VM, VM, VM, VM, VM],
        out_specs=[VM, VM, VM, VM],
        out_shape=[
            jax.ShapeDtypeStruct((refs_all, SPAN, width), bf),
            jax.ShapeDtypeStruct((refs_all, SPAN, width), bf),
            jax.ShapeDtypeStruct((nf, nbrs, piece, width), bf),
            jax.ShapeDtypeStruct((nf, nbrs, piece, width), bf),
        ],
        scratch_shapes=[
            pltpu.VMEM((nbrs + 1, nf * piece, width), f32),
            pltpu.VMEM((nbrs + 1, nf * piece, width), f32),
            pltpu.SMEM((refs_all,), i32),
        ],
        compiler_params=pltpu.CompilerParams(vmem_limit_bytes=BIG),
        name="backward",
    )(tab, qg.reshape(refs_all, SPAN, width), ug.reshape(refs_all, SPAN, width), hs, kt, vt)

    attended, gq, gk, gv, grad_proj = pl.pallas_call(
        lambda *a: return_kernel(nd, nf, width, spans, *a),
        in_specs=[SM, SM, ANY, ANY, ANY, ANY, ANY],
        out_specs=[ANY, ANY, ANY, ANY, ANY],
        out_shape=[
            jax.ShapeDtypeStruct((token_rows, full_width), bf),
            jax.ShapeDtypeStruct((spans, SPAN, full_width), bf),
            jax.ShapeDtypeStruct((nbrs, piece, full_width), bf),
            jax.ShapeDtypeStruct((nbrs, piece, full_width), bf),
            jax.ShapeDtypeStruct((full_width, columns), bf),
        ],
        scratch_shapes=[
            pltpu.VMEM((nf, rows, width), bf),
            pltpu.VMEM((nd, nf, SPAN, width), bf),
            pltpu.VMEM((nd, nf, SPAN, width), bf),
            pltpu.VMEM((nf, spans, SPAN, width), bf),
            pltpu.VMEM((nbrs, piece, width), bf),
            pltpu.VMEM((nbrs, piece, width), bf),
            pltpu.VMEM((rows, columns), bf),
            pltpu.VMEM((nf, nd, share, columns), bf),
            pltpu.VMEM((nf, nd - 1, share, columns), bf),
            pltpu.VMEM((nf, share, columns), bf),
            dma(nd), dma(nd), dma(nd), dma(nd), dma(nf), dma(nf), dma(nf), dma(nf), dma(nf), dma(nf),
            dma(chips), dma(chips), dma(chips), dma(chips),
            dma(nf, nd), dma(nf, nd), dma(nf, nd), dma(nf, nd), dma(7), dma(1 + nf), dma(nf),
        ],
        compiler_params=comm(3),
        name="giveback",
    )(
        sources, nbr_count, o.reshape(nd, nf, SPAN, width), cotangent,
        dq.reshape(nd, nf, SPAN, width), dk, dv,
    )
    return (attended, gq.reshape(token_rows, full_width), gk, gv, grad_proj)


def solution(mesh):
    placed = (
        P(("dp", "fsdp"), "enc"),
        P("dp", "fsdp", "enc"),
        P("dp", "fsdp", "enc"),
        P("enc", "fsdp"),
        P(),
        P(),
        P(),
        P("dp", "fsdp"),
    )
    return jax.shard_map(
        local,
        mesh=mesh,
        in_specs=placed,
        out_specs=(
            P(("dp", "fsdp"), "enc"),
            P(("dp", "fsdp"), "enc"),
            P("dp", "fsdp", "enc"),
            P("dp", "fsdp", "enc"),
            P("enc", "fsdp"),
        ),
        check_vma=False,
    )
```

time: 380 us -> 342 us (0.900)
  the two profiles are of different devices: /device:TPU:0 before, /device:TPU:98 now
where the time goes in v3:
time: 342 us; the launch traced here: 346 us
  Pallas kernels  330 us (96%)
  local copies, waits for them, and re-layouts  15.7 us (5%)
    pallas_call x1, Pallas kernels, local(): pl.pallas_call(lambda *a: return_kernel(nd, nf, width, spans, *a), in_spe...  166 us
    pallas_call x1, Pallas kernels, local(): pl.pallas_call(lambda *a: spread_kernel(nd, nf, width, *a), in_specs=[SM,...  134 us
    pallas_call x1, Pallas kernels, local(): pl.pallas_call(lambda *a: backward_kernel(nf, *a), in_specs=[SM, VM, VM,...  30.2 us
    unnamed x13, local copies, waits for them, and re-layouts  14.3 us

profile of v3, /device:TPU:98, one launch (start us, length us, event | category | flops | bytes accessed | tf_op | source)
XLA Modules:
  0.0 346.1 jit_solution(16377195054192776744)
XLA Ops:
  0.6 0.8 copy.13
  1.4 0.7 reshape.34.a_0_
  2.2 0.8 copy.14
  3.0 0.7 reshape.35.a_1_
  3.7 133.5 %spread.1 = (bf16[8,48,16,256]{3,2,1,0:T(8,128)(2,1)}, bf16[8,48,16,256]{3,2,1,0:T(8,128)(2,1)}, bf16[8,8,64,256]{3,2,1,0:T(8,128)(2,1)}, bf16[8,8,64,256]{3,2,1...) custom-call(s32[384]{0:T(512)} %reshape.34.a_0_, s32[384]{0:T(512)} %reshape.35.a_1_, s32[192]{0:T(256)} %a_1_.1, ...), custom_call_target="tpu_custom_call" | custom-call | tf_op jit(solution)/shard_map/spread/pallas_call | solution.py:578
  137.2 30.2 %backward.1 = (bf16[64,64,256]{2,1,0:T(8,128)(2,1)}, bf16[64,64,256]{2,1,0:T(8,128)(2,1)}, bf16[8,48,16,256]{3,2,1,0:T(8,128)(2,1)}, bf16[8,48,16,256]{3,2,1,0:T(8,128)(2,1)}) custom-call(s32[192]{0:T(256)} %get-tuple-element.20.a_0_, bf16[64,64,256]{2,1,0:T(8,128)(2,1)} %bitcast.8, bf16[64,64,256]{2,1,0:T(8,128)(2,1)} %bitcast.9, ...), custom_call_target="tpu_custom_call" | custom-call | tf_op jit(solution)/shard_map/backward/pallas_call | solution.py:621
  167.4 166.0 %giveback.1 = (bf16[192,2048]{1,0:T(8,128)(2,1)}, bf16[3,64,2048]{2,1,0:T(8,128)(2,1)}, bf16[48,16,2048]{2,1,0:T(8,128)(2,1)}, bf16[48,16,2048]{2,1,0:T(8,128)(2,1)}, bf16[2048,1024]{1,0:T(8,128)(2,1)}) custom-call(s32[384]{0:T(512)} %reshape.34.a_0_, s32[192]{0:T(256)} %a_1_.1, bf16[8,8,64,256]{3,2,1,0:T(8,128)(2,1)} %bitcast.6, bf16[1536,1024]{1,0:T(8,128)(2,1)} %a_3_.1, ...), custom_call_target="tpu_custom_call" | custom-call | tf_op jit(solution)/shard_map/giveback/pallas_call | solution.py:640
  333.4 0.0 copy-start.2
  333.4 2.2 copy.20
  335.6 2.1 copy.21
  337.7 0.0 copy-done.2
  337.7 0.0 copy-start.1
  337.7 1.7 copy.22
  339.4 1.4 copy-done.1
  340.8 0.0 copy-start
  340.8 1.7 copy.23
  342.4 1.7 copy-done
  344.1 2.0 copy.24
Async XLA Ops:
  333.4 4.3 %copy-start.2 = (bf16[48,16,2048]{2,1,0:T(8,128)(2,1)S(1)}, bf16[48,16,2048]{2,1,0:T(8,128)(2,1)}, u32[]{:S(2)}) copy-start(bf16[48,16,2048]{2,1,0:T(8,128)(2,1)} %get-tuple-element.42) | copy-start | bytes 9437188
  337.7 3.0 copy-start.1
  340.8 3.3 copy-start

commit v4 on v3

--- a/solution.py
+++ b/solution.py
@@ -147,18 +147,19 @@
     def _(group):
         @pl.loop(0, nf)
         def _(home):
-            base = (dp * nf + home) * slots
+            base = (dp * nf + home) * spans
             span = jnp.int32(0)
             for t in range(slots):
-                span = jnp.where(src[base + t] == group, t // SLOTS, span)
+                span = jnp.where(src[t % SLOTS, base + t // SLOTS] == group, t // SLOTS, span)
             sel[group * nf + home] = span
             r = group * nf + home
             number, where, live = jnp.int32(0), jnp.int32(0), jnp.int32(0)
             for t in range(slots):
                 hit = jnp.logical_and(
-                    src[r * slots + t] == dp, t % SLOTS < cnt[r * spans + t // SLOTS]
+                    src[t % SLOTS, r * spans + t // SLOTS] == dp,
+                    t % SLOTS < cnt[r * spans + t // SLOTS],
                 )
-                number = jnp.where(hit, idx[r * slots + t], number)
+                number = jnp.where(hit, idx[t % SLOTS, r * spans + t // SLOTS], number)
                 where = jnp.where(hit, t // SLOTS, where)
                 live = jnp.where(hit, 1, live)
             tab[r] = number
@@ -272,7 +273,7 @@
     for t in range(slots):
         values = jnp.zeros((1, 128), jnp.int32)
         for f in range(nf):
-            values = jnp.where(place == f, src[(dp * nf + f) * slots + t], values)
+            values = jnp.where(place == f, src[t % SLOTS, (dp * nf + f) * spans + t // SLOTS], values)
         sources.append(values)
     for c in range(spans):
         values = jnp.zeros((1, 128), jnp.int32)
@@ -322,7 +323,14 @@
 UNROLL = 4
 
 
-def backward_kernel(nf, tab, q, u, hs, kt, vt, o_ref, dq_ref, dk_ref, dv_ref, k_acc, v_acc, listed):
+def backward_kernel(
+    nf, tab, q_any, u_any, hs_any, kt_any, vt_any, o_any, dq_any, dk_any, dv_any,
+    q, u, hs, kt, vt, o_ref, dq_ref, dk_ref, dv_ref, k_acc, v_acc, listed, sems,
+):
+    pairs = ((q_any, q), (u_any, u), (hs_any, hs), (kt_any, kt), (vt_any, vt))
+    loads = [pltpu.make_async_copy(a, b, sems.at[i]) for i, (a, b) in enumerate(pairs)]
+    for copy in loads:
+        copy.start()
     lane = lax.broadcasted_iota(jnp.int32, (SPAN, 128), 1)
     pieces, nbrs, piece = kt.shape[0], kt.shape[1], kt.shape[2]
     length = pieces * piece
@@ -341,6 +349,9 @@
     def _(n):
         k_acc[n] = jnp.zeros(k_acc.shape[1:], jnp.float32)
         v_acc[n] = jnp.zeros(v_acc.shape[1:], jnp.float32)
+
+    for copy in loads:
+        copy.wait()
 
     def pick(array, at):
         return jnp.sum(jnp.where(lane == at, array, 0.0), axis=1, keepdims=True)
@@ -375,16 +386,51 @@
             k_acc[into] += jnp.concatenate(dks, axis=1)
             v_acc[into] += jnp.concatenate(dvs, axis=1)
 
-    @pl.loop(0, nbrs)
-    def _(n):
-        dk_ref[:, n] = k_acc[n].reshape(pieces, piece, -1).astype(jnp.bfloat16)
-        dv_ref[:, n] = v_acc[n].reshape(pieces, piece, -1).astype(jnp.bfloat16)
+    puts = [
+        pltpu.make_async_copy(o_ref, o_any, sems.at[5]),
+        pltpu.make_async_copy(dq_ref, dq_any, sems.at[6]),
+    ]
+    for put in puts:
+        put.start()
+    for i, (acc, out, put_to) in enumerate(((k_acc, dk_ref, dk_any), (v_acc, dv_ref, dv_any))):
+        @pl.loop(0, nbrs)
+        def _(n):
+            out[:, n] = acc[n].reshape(pieces, piece, -1).astype(jnp.bfloat16)
+
+        put = pltpu.make_async_copy(out, put_to, sems.at[7 + i])
+        put.start()
+        puts.append(put)
+    for put in puts:
+        put.wait()
+
+
+def finish_kernel(*refs):
+    count = len(refs) // 3
+    sems = refs[-1]
+    takes = []
+    for i in range(count):
+        source, held = refs[i], refs[2 * count + i]
+        pieces = 4 if source.shape[0] % 4 == 0 else 1
+        size = source.shape[0] // pieces
+        for j in range(pieces):
+            part = pl.ds(j * size, size)
+            take = pltpu.make_async_copy(source.at[part], held.at[part], sems.at[0, i, j])
+            take.start()
+            takes.append((i, j, part, take))
+    puts = []
+    for i, j, part, take in takes:
+        take.wait()
+        put = pltpu.make_async_copy(refs[2 * count + i].at[part], refs[count + i].at[part], sems.at[1, i, j])
+        put.start()
+        puts.append(put)
+    for put in puts:
+        put.wait()
 
 
 def return_kernel(
     nd, nf, width, spans, src, cnt, o, cot, dq, dk, dv, ga_out, gq, gk, gv, gp, att_all,
-    o_home, dq_home, dq_sum, k_own, v_own, cot_vm, term, shares, total,
-    os, orr, qs, qr, ks, kr, vs, vr, ys, yr, fa, ga, ba, ca, ts, tr, ps, pr, own, load, last_sem,
+    o_home, dq_home, dq_sum, k_own, v_own, cot_vm, term, first_z, first_x, second, middle, keep, total,
+    os, orr, qs, qr, ks, kr, vs, vr, ys, yr, fa, ga, ba, ca, ts, tr, own, load, last_sem,
 ):
     dp, fs = lax.axis_index("dp"), lax.axis_index("fsdp")
     chips = nf // 2
@@ -408,7 +454,7 @@
     backs = [
         remote(dq.at[p], dq_home.at[dp], qs.at[i], qr.at[i], "dp", p) for i, p in enumerate(peers)
     ]
-    for move in outs + backs:
+    for move in outs:
         move.start()
     moves = []
 
@@ -430,10 +476,10 @@
         put.start()
 
     def add_slots(home, c, parts):
-        base = (dp * nf + home) * SLOTS * spans + SLOTS * c
-        first = parts[src[base], home].astype(jnp.float32)
-        second = parts[src[base + 1], home].astype(jnp.float32)
-        both = cnt[(dp * nf + home) * spans + c] > 1
+        span = (dp * nf + home) * spans + c
+        first = parts[src[0, span], home].astype(jnp.float32)
+        second = parts[src[1, span], home].astype(jnp.float32)
+        both = cnt[span] > 1
         return (first + jnp.where(both, second, 0.0)).astype(jnp.bfloat16)
 
     for move in outs:
@@ -478,43 +524,112 @@
         put.start()
         puts.append(put)
 
-    scatters = []
+    nz = nd // 2
+    x_at, z_at = dp // nz, lax.rem(dp, nz)
+    across = lax.rem(dp + nz, nd)
+    z_places = [lax.rem(z_at + step, nz) for step in range(1, nz)]
+    z_peers = [x_at * nz + place for place in z_places]
+    blocks = []
+    flying = {}
+
+    def along_z(turn):
+        return turn % 2 == 0
+
+    def launch(turn, stage, copies):
+        sent = []
+        for i, (source, target, peer) in enumerate(copies):
+            place = stage * (nz - 1) + i
+            move = remote(source, target, ts.at[turn, place], tr.at[turn, place], "dp", peer)
+            move.start()
+            sent.append(move)
+        flying[turn, stage] = sent
+
+    def arrive(turn, stage):
+        for move in flying[turn, stage]:
+            move.wait_recv()
 
     def project(turn, block):
+        blocks.append(block)
+
         @pl.loop(0, columns // tile)
         def _(t):
             at = pl.ds(pl.multiple_of(t * tile, tile), tile)
             value = dot(att_all[block], cot_vm[:, at], TN).astype(jnp.bfloat16)
             term[turn, :, :, at] = value.reshape(nd, share, tile)
 
-        sent = [
-            remote(term.at[turn, p], shares.at[turn, i], ts.at[turn, i], tr.at[turn, i], "dp", p)
-            for i, p in enumerate(peers)
-        ]
-        for move in sent:
-            move.start()
-        scatters.append((block, sent))
-
-    def finish(turn):
-        block, sent = scatters[turn]
-        for move in sent:
-            move.wait_recv()
-        value = term[turn, dp].astype(jnp.float32)
-        for i in range(nd - 1):
-            value += shares[turn, i].astype(jnp.float32)
+        half = turn // 2
+        if along_z(turn):
+            launch(turn, 0, [
+                (term.at[turn, pl.ds(2 * place, 2)], first_z.at[half, i], p)
+                for i, (place, p) in enumerate(zip(z_places, z_peers))
+            ])
+        else:
+            launch(turn, 0, [(term.at[turn, pl.ds((1 - x_at) * nz, nz)], first_x.at[half], across)])
+
+    def add_first(turn):
+        arrive(turn, 0)
+        half = turn // 2
+        if along_z(turn):
+            def total_of(place):
+                value = term[turn, 2 * z_at + place].astype(jnp.float32)
+                for i in range(nz - 1):
+                    value += first_z[half, i, place].astype(jnp.float32)
+                return value
+
+            keep[turn] = total_of(x_at)
+            middle[turn, 0] = total_of(1 - x_at).astype(jnp.bfloat16)
+            launch(turn, 1, [(middle.at[turn, 0], second.at[turn, 0], across)])
+        else:
+            def total_of(place):
+                value = term[turn, x_at * nz + place].astype(jnp.float32)
+                return value + first_x[half, place].astype(jnp.float32)
+
+            keep[turn] = total_of(z_at)
+            for i, place in enumerate(z_places):
+                middle[turn, i] = total_of(place).astype(jnp.bfloat16)
+            launch(turn, 1, [
+                (middle.at[turn, i], second.at[turn, i], p) for i, p in enumerate(z_peers)
+            ])
+
+    def rows_of(turn, part, parts):
+        start = pl.multiple_of(blocks[turn] * width + part * share, share)
+        return gp.at[pl.ds(start, parts * share)]
+
+    owned = {}
+
+    def add_second(turn):
+        arrive(turn, 1)
+        value = keep[turn]
+        for i in range(len(flying[turn, 1])):
+            value += second[turn, i].astype(jnp.float32)
         total[turn] = value.astype(jnp.bfloat16)
-        here = pl.ds(pl.multiple_of(block * width + dp * share, share), share)
-        for i, p in enumerate(peers):
-            move = remote(total.at[turn], gp.at[here], ps.at[turn, i], pr.at[turn, i], "dp", p)
-            move.start()
-            moves.append(move)
-        put = pltpu.make_async_copy(total.at[turn], gp.at[here], load.at[1 + turn])
-        put.start()
-        puts.append(put)
+        part = 2 * z_at + x_at if along_z(turn) else dp
+        here = rows_of(turn, part, 1)
+        owned[turn] = pltpu.make_async_copy(total.at[turn], here, load.at[1 + turn])
+        owned[turn].start()
+        to = [across] if along_z(turn) else z_peers
+        launch(turn, 2, [(total.at[turn], here, p) for p in to])
+
+    def share_all(turn):
+        owned[turn].wait()
+        arrive(turn, 2)
+        if along_z(turn):
+            here = rows_of(turn, 2 * z_at, 2)
+            launch(turn, 3, [(here, here, p) for p in z_peers])
+        else:
+            here = rows_of(turn, x_at * nz, nz)
+            launch(turn, 3, [(here, here, across)])
+
+    def advance(turn):
+        for lag, act in ((2, add_first), (3, add_second), (4, share_all)):
+            if 0 <= turn - lag < nf:
+                act(turn - lag)
 
     project(0, fs)
     to_sibling[0].wait_recv()
     project(1, sibling)
+    for move in backs:
+        move.start()
     turn = 2
     order = [0, chips - 2] + list(range(1, chips - 2))
     for step in order:
@@ -526,15 +641,15 @@
         move.start()
         to_sibling.append(move)
         project(turn, back + core)
-        if turn == 2:
-            add_dq()
-        finish((turn - 2))
+        advance(turn)
         move.wait_recv()
         project(turn + 1, back + 1 - core)
-        finish((turn - 1))
+        advance(turn + 1)
+        if turn == 4:
+            add_dq()
         turn += 2
-    for last in range(turn - 2, turn):
-        finish(last)
+    for later in range(turn, turn + 4):
+        advance(later)
     tokens = spans * SPAN
     for block in range(nf):
         here = pl.ds(pl.multiple_of(fs * tokens, tokens), tokens)
@@ -545,8 +660,10 @@
         puts.append(put)
     for move in outs + backs + to_sibling + around:
         move.wait_send()
-    for _, sent in scatters:
+    for (_, stage), sent in flying.items():
         for move in sent:
+            if stage == 3:
+                move.wait_recv()
             move.wait_send()
     for move in moves:
         move.wait()
@@ -572,7 +689,7 @@
     rows, columns = cotangent.shape
     refs_all = nd * nf
     chips = nf // 2
-    sources, indices = nbr_source.reshape(-1), nbr_index.reshape(-1)
+    sources, indices = nbr_source.T, nbr_index.T
     share = width // nd
 
     kt, vt, qg, ug, hs, tab = pl.pallas_call(
@@ -620,8 +737,8 @@
 
     o, dq, dk, dv = pl.pallas_call(
         lambda *a: backward_kernel(nf, *a),
-        in_specs=[SM, VM, VM, VM, VM, VM],
-        out_specs=[VM, VM, VM, VM],
+        in_specs=[SM, ANY, ANY, ANY, ANY, ANY],
+        out_specs=[ANY, ANY, ANY, ANY],
         out_shape=[
             jax.ShapeDtypeStruct((refs_all, SPAN, width), bf),
             jax.ShapeDtypeStruct((refs_all, SPAN, width), bf),
@@ -629,9 +746,19 @@
             jax.ShapeDtypeStruct((nf, nbrs, piece, width), bf),
         ],
         scratch_shapes=[
+            pltpu.VMEM((refs_all, SPAN, width), bf),
+            pltpu.VMEM((refs_all, SPAN, width), bf),
+            pltpu.VMEM((nd, SPAN, 128), f32),
+            pltpu.VMEM((nf, nbrs, piece, width), bf),
+            pltpu.VMEM((nf, nbrs, piece, width), bf),
+            pltpu.VMEM((refs_all, SPAN, width), bf),
+            pltpu.VMEM((refs_all, SPAN, width), bf),
+            pltpu.VMEM((nf, nbrs, piece, width), bf),
+            pltpu.VMEM((nf, nbrs, piece, width), bf),
             pltpu.VMEM((nbrs + 1, nf * piece, width), f32),
             pltpu.VMEM((nbrs + 1, nf * piece, width), f32),
             pltpu.SMEM((refs_all,), i32),
+            dma(9),
         ],
         compiler_params=pltpu.CompilerParams(vmem_limit_bytes=BIG),
         name="backward",
@@ -657,11 +784,15 @@
             pltpu.VMEM((nbrs, piece, width), bf),
             pltpu.VMEM((rows, columns), bf),
             pltpu.VMEM((nf, nd, share, columns), bf),
-            pltpu.VMEM((nf, nd - 1, share, columns), bf),
+            pltpu.VMEM((nf // 2, nd // 2 - 1, 2, share, columns), bf),
+            pltpu.VMEM((nf // 2, nd // 2, share, columns), bf),
+            pltpu.VMEM((nf, nd // 2 - 1, share, columns), bf),
+            pltpu.VMEM((nf, nd // 2 - 1, share, columns), bf),
+            pltpu.VMEM((nf, share, columns), f32),
             pltpu.VMEM((nf, share, columns), bf),
             dma(nd), dma(nd), dma(nd), dma(nd), dma(nf), dma(nf), dma(nf), dma(nf), dma(nf), dma(nf),
             dma(chips), dma(chips), dma(chips), dma(chips),
-            dma(nf, nd), dma(nf, nd), dma(nf, nd), dma(nf, nd), dma(7), dma(1 + nf), dma(nf),
+            dma(nf, 2 * nd), dma(nf, 2 * nd), dma(7), dma(1 + nf), dma(nf),
         ],
         compiler_params=comm(3),
         name="giveback",
@@ -669,7 +800,17 @@
         sources, nbr_count, o.reshape(nd, nf, SPAN, width), cotangent,
         dq.reshape(nd, nf, SPAN, width), dk, dv,
     )
-    return (attended, gq.reshape(token_rows, full_width), gk, gv, grad_proj)
+    results = [grad_proj, gk, gv, attended, gq.reshape(token_rows, full_width)]
+    grad_proj, gk, gv, attended, gq = pl.pallas_call(
+        finish_kernel,
+        in_specs=[ANY] * len(results),
+        out_specs=[ANY] * len(results),
+        out_shape=[jax.ShapeDtypeStruct(value.shape, value.dtype) for value in results],
+        scratch_shapes=[pltpu.VMEM(value.shape, value.dtype) for value in results] + [dma(2, len(results), 4)],
+        compiler_params=pltpu.CompilerParams(vmem_limit_bytes=BIG),
+        name="finish",
+    )(*results)
+    return (attended, gq, gk, gv, grad_proj)
 
 
 def solution(mesh):

time: 342 us -> 319 us (0.933)
  the two profiles are of different devices: /device:TPU:98 before, /device:TPU:0 now
where the time goes in v4:
time: 319 us
  Pallas kernels  319 us (100%)
    pallas_call x1, Pallas kernels, local(): pl.pallas_call(lambda *a: return_kernel(nd, nf, width, spans, *a), in_spe...  145 us
    pallas_call x1, Pallas kernels, local(): pl.pallas_call(lambda *a: spread_kernel(nd, nf, width, *a), in_specs=[SM,...  136 us
    pallas_call x1, Pallas kernels, local(): pl.pallas_call(lambda *a: backward_kernel(nf, *a), in_specs=[SM, ANY, ANY...  28.5 us
    pallas_call x1, Pallas kernels, local(): pl.pallas_call(finish_kernel, in_specs=[ANY] * len(results), out_specs=[A...  8.78 us

profile of v4, /device:TPU:0, one launch (start us, length us, event | category | flops | bytes accessed | tf_op | source)
XLA Modules:
  0.0 319.2 jit_solution(6746353929303478776)
XLA Ops:
  0.6 136.1 %spread.1 = (bf16[8,48,16,256]{3,2,1,0:T(8,128)(2,1)}, bf16[8,48,16,256]{3,2,1,0:T(8,128)(2,1)}, bf16[8,8,64,256]{3,2,1,0:T(8,128)(2,1)}, bf16[8,8,64,256]{3,2,1...) custom-call(s32[2,192]{1,0:T(2,128)} %bitcast.14, s32[2,192]{1,0:T(2,128)} %bitcast.16, s32[192]{0:T(256)} %a_1_.1, ...), custom_call_target="tpu_custom_call" | custom-call | tf_op jit(solution)/shard_map/spread/pallas_call | solution.py:695
  136.8 28.5 %backward.1 = (bf16[64,64,256]{2,1,0:T(8,128)(2,1)}, bf16[64,64,256]{2,1,0:T(8,128)(2,1)}, bf16[8,48,16,256]{3,2,1,0:T(8,128)(2,1)}, bf16[8,48,16,256]{3,2,1,0:T(8,128)(2,1)}) custom-call(s32[192]{0:T(256)} %get-tuple-element.25.a_0_, bf16[64,64,256]{2,1,0:T(8,128)(2,1)} %bitcast.10, bf16[64,64,256]{2,1,0:T(8,128)(2,1)} %bitcast.11, ...), custom_call_target="tpu_custom_call" | custom-call | tf_op jit(solution)/shard_map/backward/pallas_call | solution.py:738
  165.3 145.2 %giveback.1 = (bf16[192,2048]{1,0:T(8,128)(2,1)}, bf16[3,64,2048]{2,1,0:T(8,128)(2,1)}, bf16[48,16,2048]{2,1,0:T(8,128)(2,1)}, bf16[48,16,2048]{2,1,0:T(8,128)(2,1)}, bf16[2048,1024]{1,0:T(8,128)(2,1)}) custom-call(s32[2,192]{1,0:T(2,128)} %bitcast.15, s32[192]{0:T(256)} %a_1_.1, bf16[8,8,64,256]{3,2,1,0:T(8,128)(2,1)} %bitcast.8, bf16[1536,1024]{1,0:T(8,128)(2,1)} %a_3_.1, ...), custom_call_target="tpu_custom_call" | custom-call | tf_op jit(solution)/shard_map/giveback/pallas_call | solution.py:767
  310.4 8.8 %finish.1 = (bf16[2048,1024]{1,0:T(8,128)(2,1)}, bf16[48,16,2048]{2,1,0:T(8,128)(2,1)}, bf16[48,16,2048]{2,1,0:T(8,128)(2,1)}, bf16[192,2048]{1,0:T(8,128)(2,1)}, bf16[192,2048]{1,0:T(8,128)(2,1)}) custom-call(bf16[2048,1024]{1,0:T(8,128)(2,1)} %get-tuple-element.35.refs_0_, bf16[48,16,2048]{2,1,0:T(8,128)(2,1)} %get-tuple-element.36.refs_1_, ...), custom_call_target="tpu_custom_call" | custom-call | tf_op jit(solution)/shard_map/finish/pallas_call | solution.py:804

commit v5 on v4

--- a/solution.py
+++ b/solution.py
@@ -99,17 +99,31 @@
         return moves
 
     q_moves = spread(q, q_heads, qs, qr)
-    k_moves = spread(k, kt_vm, ks, kr)
+    nbr_half = kt_vm.shape[1] // 2
+
+    def spread_keys(part):
+        here = pl.ds(part * nbr_half, nbr_half)
+        moves = []
+        for step in range(1, nf):
+            peer = lax.rem(fs + step, nf)
+            at = pl.ds(pl.multiple_of(peer * width, width), width)
+            place = part * nf + step
+            move = remote(k.at[here, :, at], kt_vm.at[fs, here], ks.at[place], kr.at[place], "fsdp", peer)
+            move.start()
+            moves.append(move)
+        return moves
+
+    k_moves = spread_keys(0)
     for copy in loads:
         copy.wait()
     rows = cot_vm.shape[0]
     tile = 512
-    sib_moves = []
-    for step in range(chips):
+    sib_moves = {}
+    for turn, step in enumerate((1, 0, 2, 3)):
         there = lax.rem(chip + step + 1, chips)
         for which in (1 - core, core):
             block = pl.multiple_of((there * 2 + which) * width, width)
-            first = len(sib_moves) == step
+            first = len(sib_moves) == turn
 
             @pl.loop(0, rows // tile)
             def _(t):
@@ -123,25 +137,42 @@
             if first:
                 move = remote(sib_send.at[step], sib_recv.at[step], bs.at[step], br.at[step], "fsdp", sibling)
                 move.start()
-                sib_moves.append(move)
+                sib_moves[step] = move
+    half = rows // 2
+    piece = 256
+    halves = [pl.ds(0, half), pl.ds(half, half)]
     ring_moves = []
-    for step in range(chips - 1):
-        there = lax.rem(chip + step + 1, chips)
-        sib_moves[step].wait_recv()
-
-        @pl.loop(0, rows // tile)
+
+    def add_part(step, part, relayed):
+        @pl.loop(0, half // piece)
         def _(t):
-            at = pl.ds(pl.multiple_of(t * tile, tile), tile)
-            ring_send[step, at, :] = (
-                mine[step, at, :] + sib_recv[step, at, :].astype(jnp.float32)
-            ).astype(jnp.bfloat16)
-
+            at = pl.ds(pl.multiple_of(part * half + t * piece, piece), piece)
+            value = mine[step, at, :] + sib_recv[step, at, :].astype(jnp.float32)
+            if relayed:
+                value += ring_recv[1, at, :].astype(jnp.float32)
+            ring_send[step, at, :] = value.astype(jnp.bfloat16)
+
+    def pass_on(step, part, forward):
+        there = lax.rem(chip + (1 if forward else chips - 1), chips) * 2 + core
+        here = halves[part]
+        place = len(ring_moves)
         move = remote(
-            ring_send.at[step], ring_recv.at[step], rs.at[step], rr.at[step], "fsdp", there * 2 + core
+            ring_send.at[step, here], ring_recv.at[step, here], rs.at[place], rr.at[place], "fsdp", there
         )
         move.start()
         ring_moves.append(move)
-    v_moves = [spread(v, None, vs, vr, head) for head in range(heads)]
+
+    sib_moves[1].wait_recv()
+    for part in (0, 1):
+        add_part(1, part, False)
+        pass_on(1, part, part == 0)
+    sib_moves[0].wait_recv()
+    add_part(0, 1, False)
+    pass_on(0, 1, True)
+    sib_moves[2].wait_recv()
+    add_part(2, 0, False)
+    pass_on(2, 0, False)
+    k_moves += spread_keys(1)
 
     @pl.loop(0, nd)
     def _(group):
@@ -194,6 +225,11 @@
         puts.append(put)
 
     q_there, q_put = deliver(0, lambda home, c: q_heads[home, c], qg_vm, gs, gr)
+    for part, step in ((0, 0), (1, 2)):
+        ring_moves[part].wait_recv()
+        add_part(step, part, True)
+        pass_on(step, part, step == 0)
+    v_moves = [spread(v, None, vs, vr, head) for head in range(heads)]
     q_put.wait()
     for move in q_there:
         move.wait_recv()
@@ -224,14 +260,14 @@
         st[d] = marks
 
     sib_moves[chips - 1].wait_recv()
-    for move in ring_moves:
+    for move in ring_moves[2:]:
         move.wait_recv()
 
     @pl.loop(0, rows // SPAN)
     def _(i):
         at = pl.ds(pl.multiple_of(i * SPAN, SPAN), SPAN)
         value = mine[chips - 1, at, :] + sib_recv[chips - 1, at, :].astype(jnp.float32)
-        for step in range(chips - 1):
+        for step in (0, 2):
             value += ring_recv[step, at, :].astype(jnp.float32)
         u_vm[i] = value.astype(jnp.bfloat16)
 
@@ -312,7 +348,7 @@
     for move in gives:
         move.start()
     store(hs, hs_out.at[dp], 10)
-    for move in q_moves + k_moves + sib_moves + ring_moves + q_there + u_there + stats + sum(v_moves, []):
+    for move in q_moves + k_moves + list(sib_moves.values()) + ring_moves + q_there + u_there + stats + sum(v_moves, []):
         move.wait_send()
     for move in gives:
         move.wait()
@@ -429,7 +465,7 @@
 
 def return_kernel(
     nd, nf, width, spans, src, cnt, o, cot, dq, dk, dv, ga_out, gq, gk, gv, gp, att_all,
-    o_home, dq_home, dq_sum, k_own, v_own, cot_vm, term, first_z, first_x, second, middle, keep, total,
+    o_a, o_b, dq_home, dq_sum, k_own, v_own, cot_vm, term, first_z, first_x, second, middle, keep, total,
     os, orr, qs, qr, ks, kr, vs, vr, ys, yr, fa, ga, ba, ca, ts, tr, own, load, last_sem,
 ):
     dp, fs = lax.axis_index("dp"), lax.axis_index("fsdp")
@@ -440,8 +476,10 @@
     load_cot.start()
     enter((("dp", nd), ("fsdp", nf)))
     peers = [lax.rem(dp + step, nd) for step in range(1, nd)]
+    halves = [pl.ds(0, nf // 2), pl.ds(nf // 2, nf // 2)]
     firsts = [
-        pltpu.make_async_copy(o.at[dp], o_home.at[dp], own.at[6]),
+        pltpu.make_async_copy(o.at[dp, halves[0]], o_a.at[dp], own.at[6]),
+        pltpu.make_async_copy(o.at[dp, halves[1]], o_b.at[dp], own.at[7]),
         pltpu.make_async_copy(dq.at[dp], dq_home.at[dp], own.at[0]),
         pltpu.make_async_copy(dk.at[fs], k_own, own.at[1]),
         pltpu.make_async_copy(dv.at[fs], v_own, own.at[2]),
@@ -449,23 +487,33 @@
     for copy in firsts:
         copy.start()
     outs = [
-        remote(o.at[p], o_home.at[dp], os.at[i], orr.at[i], "dp", p) for i, p in enumerate(peers)
+        [
+            remote(o.at[p, halves[h]], held.at[dp], os.at[h * nd + i], orr.at[h * nd + i], "dp", p)
+            for i, p in enumerate(peers)
+        ]
+        for h, held in enumerate((o_a, o_b))
     ]
     backs = [
         remote(dq.at[p], dq_home.at[dp], qs.at[i], qr.at[i], "dp", p) for i, p in enumerate(peers)
     ]
-    for move in outs:
+    for move in outs[0] + outs[1]:
         move.start()
     moves = []
 
-    def give(ref, out, s_sem, r_sem):
+    nbrs = dk.shape[1]
+    early = nbrs // 3
+
+    def give(ref, out, s_sem, r_sem, start, size, base):
+        here = pl.ds(start, size)
         for step in range(1, nf):
             peer = lax.rem(fs + step, nf)
-            move = remote(ref.at[peer], cols(out, fs, width), s_sem.at[step], r_sem.at[step], "fsdp", peer)
+            at = pl.ds(pl.multiple_of(fs * width, width), width)
+            place = base + step
+            move = remote(ref.at[peer, here], out.at[here, :, at], s_sem.at[place], r_sem.at[place], "fsdp", peer)
             move.start()
             moves.append(move)
 
-    give(dk, gk, ks, kr)
+    give(dk, gk, ks, kr, 0, early, 0)
     for copy in firsts:
         copy.wait()
     puts = [
@@ -475,32 +523,38 @@
     for put in puts:
         put.start()
 
-    def add_slots(home, c, parts):
+    def add_slots(home, place, c, parts):
         span = (dp * nf + home) * spans + c
-        first = parts[src[0, span], home].astype(jnp.float32)
-        second = parts[src[1, span], home].astype(jnp.float32)
+        first = parts[src[0, span], place].astype(jnp.float32)
+        second = parts[src[1, span], place].astype(jnp.float32)
         both = cnt[span] > 1
         return (first + jnp.where(both, second, 0.0)).astype(jnp.bfloat16)
 
-    for move in outs:
-        move.wait_recv()
-
-    @pl.loop(0, nf)
-    def _(home):
-        for c in range(spans):
-            at = pl.multiple_of((home * spans + c) * SPAN, SPAN)
-            att_all[fs, pl.ds(at, SPAN), :] = add_slots(home, c, o_home)
-
-    att = att_all.at[fs]
-    to_sibling = [remote(att, att, fa.at[chips - 1], ga.at[chips - 1], "fsdp", sibling)]
-    to_sibling[0].start()
-    around = []
-    for step in range(chips - 1):
-        there = lax.rem(chip + step + 1, chips) * 2 + core
-        move = remote(att, att, ba.at[step], ca.at[step], "fsdp", there)
+    to_sibling, around = [], []
+    per_half = (nf // 2) * spans * SPAN
+    for h, held in enumerate((o_a, o_b)):
+        for move in outs[h]:
+            move.wait_recv()
+
+        @pl.loop(0, nf // 2)
+        def _(place):
+            home = h * (nf // 2) + place
+            for c in range(spans):
+                at = pl.multiple_of((home * spans + c) * SPAN, SPAN)
+                att_all[fs, pl.ds(at, SPAN), :] = add_slots(home, place, c, held)
+
+        att = att_all.at[fs, pl.ds(h * per_half, per_half)]
+        move = remote(att, att, fa.at[chips - 1 + h], ga.at[chips - 1 + h], "fsdp", sibling)
         move.start()
-        around.append(move)
-    give(dv, gv, vs, vr)
+        to_sibling.append(move)
+        for step in range(chips - 1):
+            there = lax.rem(chip + step + 1, chips) * 2 + core
+            place = h * (chips - 1) + step
+            move = remote(att, att, ba.at[place], ca.at[place], "fsdp", there)
+            move.start()
+            around.append(move)
+    give(dk, gk, ks, kr, early, nbrs - early, nf)
+    give(dv, gv, vs, vr, 0, nbrs, 0)
     load_cot.wait()
     share = width // nd
     columns = cot_vm.shape[1]
@@ -513,7 +567,7 @@
         @pl.loop(0, nf)
         def _(home):
             for c in range(spans):
-                dq_sum[home, c] = add_slots(home, c, dq_home)
+                dq_sum[home, c] = add_slots(home, home, c, dq_home)
 
         for step in range(1, nf):
             peer = lax.rem(fs + step, nf)
@@ -626,7 +680,8 @@
                 act(turn - lag)
 
     project(0, fs)
-    to_sibling[0].wait_recv()
+    for move in to_sibling[:2]:
+        move.wait_recv()
     project(1, sibling)
     for move in backs:
         move.start()
@@ -635,6 +690,7 @@
     for step in order:
         back = lax.rem(chip + chips - step - 1, chips) * 2
         around[step].wait_recv()
+        around[chips - 1 + step].wait_recv()
         move = remote(
             att_all.at[back + core], att_all.at[back + core], fa.at[step], ga.at[step], "fsdp", sibling
         )
@@ -658,7 +714,7 @@
         )
         put.start()
         puts.append(put)
-    for move in outs + backs + to_sibling + around:
+    for move in outs[0] + outs[1] + backs + to_sibling + around:
         move.wait_send()
     for (_, stage), sent in flying.items():
         for move in sent:
@@ -725,8 +781,8 @@
             pltpu.VMEM((nd, SPAN, 128), f32),
             pltpu.VMEM((SPAN, 128), f32),
             pltpu.SMEM((refs_all,), i32),
-            dma(nf), dma(nf), dma(nf), dma(nf), dma(2 * nf), dma(2 * nf), dma(nd), dma(nd), dma(nd), dma(nd),
-            dma(chips), dma(chips), dma(chips), dma(chips), dma(nd), dma(nd), dma(nd), dma(nd), dma(13), dma(2),
+            dma(nf), dma(nf), dma(2 * nf), dma(2 * nf), dma(2 * nf), dma(2 * nf), dma(nd), dma(nd), dma(nd), dma(nd),
+            dma(chips), dma(chips), dma(6), dma(6), dma(nd), dma(nd), dma(nd), dma(nd), dma(13), dma(2),
         ],
         compiler_params=comm(1),
         name="spread",
@@ -777,7 +833,8 @@
         ],
         scratch_shapes=[
             pltpu.VMEM((nf, rows, width), bf),
-            pltpu.VMEM((nd, nf, SPAN, width), bf),
+            pltpu.VMEM((nd, nf // 2, SPAN, width), bf),
+            pltpu.VMEM((nd, nf // 2, SPAN, width), bf),
             pltpu.VMEM((nd, nf, SPAN, width), bf),
             pltpu.VMEM((nf, spans, SPAN, width), bf),
             pltpu.VMEM((nbrs, piece, width), bf),
@@ -790,9 +847,9 @@
             pltpu.VMEM((nf, nd // 2 - 1, share, columns), bf),
             pltpu.VMEM((nf, share, columns), f32),
             pltpu.VMEM((nf, share, columns), bf),
-            dma(nd), dma(nd), dma(nd), dma(nd), dma(nf), dma(nf), dma(nf), dma(nf), dma(nf), dma(nf),
-            dma(chips), dma(chips), dma(chips), dma(chips),
-            dma(nf, 2 * nd), dma(nf, 2 * nd), dma(7), dma(1 + nf), dma(nf),
+            dma(2 * nd), dma(2 * nd), dma(nd), dma(nd), dma(2 * nf), dma(2 * nf), dma(nf), dma(nf), dma(nf), dma(nf),
+            dma(chips + 1), dma(chips + 1), dma(2 * chips), dma(2 * chips),
+            dma(nf, 2 * nd), dma(nf, 2 * nd), dma(8), dma(1 + nf), dma(nf),
         ],
         compiler_params=comm(3),
         name="giveback",

time: 319 us -> 307 us (0.962)
  Pallas kernels: 319 us -> 306 us
    pallas_call x1, Pallas kernels: 136 us -> 128 us  [local(): pl.pallas_call(lambda *a: spread_kernel(nd, nf, width, *a), in_specs=[SM,...]
    pallas_call x1, Pallas kernels: 28.5 us -> 22.6 us  [local(): pl.pallas_call(lambda *a: backward_kernel(nf, *a), in_specs=[SM, ANY, ANY...]
where the time goes in v5:
time: 307 us
  Pallas kernels  306 us (100%)
    pallas_call x1, Pallas kernels, local(): pl.pallas_call(lambda *a: return_kernel(nd, nf, width, spans, *a), in_spe...  147 us
    pallas_call x1, Pallas kernels, local(): pl.pallas_call(lambda *a: spread_kernel(nd, nf, width, *a), in_specs=[SM,...  128 us
    pallas_call x1, Pallas kernels, local(): pl.pallas_call(lambda *a: backward_kernel(nf, *a), in_specs=[SM, ANY, ANY...  22.6 us
    pallas_call x1, Pallas kernels, local(): pl.pallas_call(finish_kernel, in_specs=[ANY] * len(results), out_specs=[A...  8.78 us

profile of v5, /device:TPU:0, one launch (start us, length us, event | category | flops | bytes accessed | tf_op | source)
XLA Modules:
  0.0 306.6 jit_solution(13045942651271033467)
XLA Ops:
  0.6 127.7 %spread.1 = (bf16[8,48,16,256]{3,2,1,0:T(8,128)(2,1)}, bf16[8,48,16,256]{3,2,1,0:T(8,128)(2,1)}, bf16[8,8,64,256]{3,2,1,0:T(8,128)(2,1)}, bf16[8,8,64,256]{3,2,1...) custom-call(s32[2,192]{1,0:T(2,128)} %bitcast.14, s32[2,192]{1,0:T(2,128)} %bitcast.16, s32[192]{0:T(256)} %a_1_.1, ...), custom_call_target="tpu_custom_call" | custom-call | tf_op jit(solution)/shard_map/spread/pallas_call | solution.py:751
  128.4 22.6 %backward.1 = (bf16[64,64,256]{2,1,0:T(8,128)(2,1)}, bf16[64,64,256]{2,1,0:T(8,128)(2,1)}, bf16[8,48,16,256]{3,2,1,0:T(8,128)(2,1)}, bf16[8,48,16,256]{3,2,1,0:T(8,128)(2,1)}) custom-call(s32[192]{0:T(256)} %get-tuple-element.25.a_0_, bf16[64,64,256]{2,1,0:T(8,128)(2,1)} %bitcast.10, bf16[64,64,256]{2,1,0:T(8,128)(2,1)} %bitcast.11, ...), custom_call_target="tpu_custom_call" | custom-call | tf_op jit(solution)/shard_map/backward/pallas_call | solution.py:794
  151.0 146.8 %giveback.1 = (bf16[192,2048]{1,0:T(8,128)(2,1)}, bf16[3,64,2048]{2,1,0:T(8,128)(2,1)}, bf16[48,16,2048]{2,1,0:T(8,128)(2,1)}, bf16[48,16,2048]{2,1,0:T(8,128)(2,1)}, bf16[2048,1024]{1,0:T(8,128)(2,1)}) custom-call(s32[2,192]{1,0:T(2,128)} %bitcast.15, s32[192]{0:T(256)} %a_1_.1, bf16[8,8,64,256]{3,2,1,0:T(8,128)(2,1)} %bitcast.8, bf16[1536,1024]{1,0:T(8,128)(2,1)} %a_3_.1, ...), custom_call_target="tpu_custom_call" | custom-call | tf_op jit(solution)/shard_map/giveback/pallas_call | solution.py:823
  297.9 8.8 %finish.1 = (bf16[2048,1024]{1,0:T(8,128)(2,1)}, bf16[48,16,2048]{2,1,0:T(8,128)(2,1)}, bf16[48,16,2048]{2,1,0:T(8,128)(2,1)}, bf16[192,2048]{1,0:T(8,128)(2,1)}, bf16[192,2048]{1,0:T(8,128)(2,1)}) custom-call(bf16[2048,1024]{1,0:T(8,128)(2,1)} %get-tuple-element.35.refs_0_, bf16[48,16,2048]{2,1,0:T(8,128)(2,1)} %get-tuple-element.36.refs_1_, ...), custom_call_target="tpu_custom_call" | custom-call | tf_op jit(solution)/shard_map/finish/pallas_call | solution.py:861

commit v6 on v5

--- a/solution.py
+++ b/solution.py
@@ -49,10 +49,10 @@
 
 
 def spread_kernel(
-    nd, nf, width, src, idx, cnt, q, k, v, cot, proj, kt, vt, qg, ug, hs_out, tab,
+    nd, nf, width, src, idx, cnt, q, k, v, cot, proj, kt, vt, qg, ug, hs_out, tab, o_first, weights,
     q_heads, send, kt_vm, vt_a, vt_b, qg_vm, ug_vm, u_vm, cot_vm, proj_vm, sib_send, sib_recv, mine, ring_send,
-    ring_recv, probs, st, st_home, hs, sel,
-    qs, qr, ks, kr, vs, vr, gs, gr, us, ur, bs, br, rs, rr, ss, sr, hsn, hr, own, load,
+    ring_recv, probs, st, st_home, hs, sel, o_send,
+    qs, qr, ks, kr, vs, vr, gs, gr, us, ur, bs, br, rs, rr, ss, sr, hsn, hr, oss, osr, own, load,
 ):
     dp, fs = lax.axis_index("dp"), lax.axis_index("fsdp")
     chips = nf // 2
@@ -272,14 +272,32 @@
         u_vm[i] = value.astype(jnp.bfloat16)
 
     u_there, u_put = deliver(1, lambda home, c: u_vm[home * spans + c], ug_vm, us, ur)
+    owns[2].wait()
+    for move in v_moves[0]:
+        move.wait_recv()
+
+    @pl.loop(0, nd)
+    def _(d):
+        for f in range(nf):
+            values = vt_vm[0][:, tab[d * nf + f]].reshape(length, HEAD_DIM)
+            expo = probs[0, d * nf + f].astype(jnp.bfloat16)
+            o_send[d, f] = dot(expo, values, NN).astype(jnp.bfloat16)
+
+    o_there = [
+        remote(o_send.at[p], o_first.at[dp], oss.at[i], osr.at[i], "dp", p) for i, p in enumerate(peers)
+    ]
+    for move in o_there:
+        move.start()
+    store(o_send.at[dp], o_first.at[dp], 13)
     u_put.wait()
     for move in u_there:
         move.wait_recv()
     store(ug_vm, ug, 7)
     for h in range(heads):
-        owns[2 + h].wait()
-        for move in v_moves[h]:
-            move.wait_recv()
+        if h > 0:
+            owns[2 + h].wait()
+            for move in v_moves[h]:
+                move.wait_recv()
         part = slice(h * HEAD_DIM, (h + 1) * HEAD_DIM)
 
         @pl.loop(0, nd)
@@ -320,6 +338,7 @@
     for move in stats:
         move.wait_recv()
     table = jnp.zeros((SPAN, 128), jnp.float32)
+    scales = jnp.zeros((SPAN, 128), jnp.float32)
     for c in range(spans):
         pair = []
         for slot in range(SLOTS):
@@ -341,6 +360,12 @@
             moved = pltpu.roll(value, at, axis=1) if at else value
             inside = jnp.logical_and(lane >= at, lane < at + group_lanes)
             table = jnp.where(inside, moved, table)
+        for slot, value in enumerate((a0 / total, a1 / total)):
+            at = (SLOTS * c + slot) * group_lanes
+            moved = pltpu.roll(value, at, axis=1) if at else value
+            inside = jnp.logical_and(lane >= at, lane < at + group_lanes)
+            scales = jnp.where(inside, moved, scales)
+    weights[...] = scales
     hs[...] = table
     gives = [
         remote(hs, hs_out.at[dp], hsn.at[i], hr.at[i], "dp", p) for i, p in enumerate(peers)
@@ -350,7 +375,7 @@
     store(hs, hs_out.at[dp], 10)
     for move in q_moves + k_moves + list(sib_moves.values()) + ring_moves + q_there + u_there + stats + sum(v_moves, []):
         move.wait_send()
-    for move in gives:
+    for move in gives + o_there:
         move.wait()
     for put in puts:
         put.wait()
@@ -411,13 +436,14 @@
                 rounded = probs.astype(jnp.bfloat16)
                 dprobs = dot(up[:, part], values[:, part], NT)
                 ds = (probs * (dprobs - pick(table, 64 + at + h)) * SCALE).astype(jnp.bfloat16)
-                outs.append(dot(rounded, values[:, part], NN).astype(jnp.bfloat16))
+                if h > 0:
+                    outs.append(dot(rounded, values[:, part], NN).astype(jnp.bfloat16))
                 dqs.append(dot(ds, keys[:, part], NN).astype(jnp.bfloat16))
                 dks.append(dot(ds, query[:, part], TN))
                 dvs.append(dot(rounded, up[:, part], TN))
             done.append((r, into, outs, dqs, dks, dvs))
         for r, into, outs, dqs, dks, dvs in done:
-            o_ref[r] = jnp.concatenate(outs, axis=1)
+            o_ref[r] = outs[0]
             dq_ref[r] = jnp.concatenate(dqs, axis=1)
             k_acc[into] += jnp.concatenate(dks, axis=1)
             v_acc[into] += jnp.concatenate(dvs, axis=1)
@@ -464,7 +490,7 @@
 
 
 def return_kernel(
-    nd, nf, width, spans, src, cnt, o, cot, dq, dk, dv, ga_out, gq, gk, gv, gp, att_all,
+    nd, nf, width, spans, src, cnt, weights, o_first, o, cot, dq, dk, dv, ga_out, gq, gk, gv, gp, att_all,
     o_a, o_b, dq_home, dq_sum, k_own, v_own, cot_vm, term, first_z, first_x, second, middle, keep, total,
     os, orr, qs, qr, ks, kr, vs, vr, ys, yr, fa, ga, ba, ca, ts, tr, own, load, last_sem,
 ):
@@ -476,10 +502,9 @@
     load_cot.start()
     enter((("dp", nd), ("fsdp", nf)))
     peers = [lax.rem(dp + step, nd) for step in range(1, nd)]
-    halves = [pl.ds(0, nf // 2), pl.ds(nf // 2, nf // 2)]
     firsts = [
-        pltpu.make_async_copy(o.at[dp, halves[0]], o_a.at[dp], own.at[6]),
-        pltpu.make_async_copy(o.at[dp, halves[1]], o_b.at[dp], own.at[7]),
+        pltpu.make_async_copy(o_first, o_a, own.at[6]),
+        pltpu.make_async_copy(o.at[dp], o_b.at[dp], own.at[7]),
         pltpu.make_async_copy(dq.at[dp], dq_home.at[dp], own.at[0]),
         pltpu.make_async_copy(dk.at[fs], k_own, own.at[1]),
         pltpu.make_async_copy(dv.at[fs], v_own, own.at[2]),
@@ -487,16 +512,12 @@
     for copy in firsts:
         copy.start()
     outs = [
-        [
-            remote(o.at[p, halves[h]], held.at[dp], os.at[h * nd + i], orr.at[h * nd + i], "dp", p)
-            for i, p in enumerate(peers)
-        ]
-        for h, held in enumerate((o_a, o_b))
+        remote(o.at[p], o_b.at[dp], os.at[i], orr.at[i], "dp", p) for i, p in enumerate(peers)
     ]
     backs = [
         remote(dq.at[p], dq_home.at[dp], qs.at[i], qr.at[i], "dp", p) for i, p in enumerate(peers)
     ]
-    for move in outs[0] + outs[1]:
+    for move in outs + backs:
         move.start()
     moves = []
 
@@ -513,7 +534,6 @@
             move.start()
             moves.append(move)
 
-    give(dk, gk, ks, kr, 0, early, 0)
     for copy in firsts:
         copy.wait()
     puts = [
@@ -530,31 +550,47 @@
         both = cnt[span] > 1
         return (first + jnp.where(both, second, 0.0)).astype(jnp.bfloat16)
 
-    to_sibling, around = [], []
-    per_half = (nf // 2) * spans * SPAN
-    for h, held in enumerate((o_a, o_b)):
-        for move in outs[h]:
-            move.wait_recv()
-
-        @pl.loop(0, nf // 2)
-        def _(place):
-            home = h * (nf // 2) + place
+    to_sibling, around = [], {}
+    lane = lax.broadcasted_iota(jnp.int32, (SPAN, 128), 1)
+    table = weights[...]
+    heads = width // HEAD_DIM
+
+    def head_of(block, h):
+        return att_all.at[block, :, pl.ds(h * HEAD_DIM, HEAD_DIM)]
+
+    def weigh(home, c):
+        span = (dp * nf + home) * spans + c
+        value = jnp.zeros((SPAN, HEAD_DIM), jnp.float32)
+        for slot in range(SLOTS):
+            at = heads * (nf * (SLOTS * c + slot) + home)
+            scale = jnp.sum(jnp.where(lane == at, table, 0.0), axis=1, keepdims=True)
+            part = scale * o_a[src[slot, span], home].astype(jnp.float32)
+            value += part if slot == 0 else jnp.where(cnt[span] > slot, part, 0.0)
+        return value.astype(jnp.bfloat16)
+
+    for h in range(heads):
+        if h > 0:
+            for move in outs:
+                move.wait_recv()
+
+        @pl.loop(0, nf)
+        def _(home):
             for c in range(spans):
                 at = pl.multiple_of((home * spans + c) * SPAN, SPAN)
-                att_all[fs, pl.ds(at, SPAN), :] = add_slots(home, place, c, held)
-
-        att = att_all.at[fs, pl.ds(h * per_half, per_half)]
+                value = weigh(home, c) if h == 0 else add_slots(home, home, c, o_b)
+                att_all[fs, pl.ds(at, SPAN), h * HEAD_DIM : (h + 1) * HEAD_DIM] = value
+
+        att = head_of(fs, h)
         move = remote(att, att, fa.at[chips - 1 + h], ga.at[chips - 1 + h], "fsdp", sibling)
         move.start()
         to_sibling.append(move)
-        for step in range(chips - 1):
+        for step in (0, chips - 2):
             there = lax.rem(chip + step + 1, chips) * 2 + core
             place = h * (chips - 1) + step
             move = remote(att, att, ba.at[place], ca.at[place], "fsdp", there)
             move.start()
-            around.append(move)
-    give(dk, gk, ks, kr, early, nbrs - early, nf)
-    give(dv, gv, vs, vr, 0, nbrs, 0)
+            around[h, step] = move
+        give(dk, gk, ks, kr, h * early, early, h * nf)
     load_cot.wait()
     share = width // nd
     columns = cot_vm.shape[1]
@@ -683,14 +719,24 @@
     for move in to_sibling[:2]:
         move.wait_recv()
     project(1, sibling)
-    for move in backs:
-        move.start()
+    for h, step in ((0, 0), (1, chips - 2)):
+        for each in range(heads):
+            around[each, step].wait_recv()
+        back = lax.rem(chip + chips - step - 1, chips) * 2 + core
+        there = lax.rem(chip + step + 1, chips) * 2 + core
+        place = h * (chips - 1) + 1
+        held = head_of(back, h)
+        around[h, 1] = remote(held, held, ba.at[place], ca.at[place], "fsdp", there)
+        around[h, 1].start()
+    give(dk, gk, ks, kr, heads * early, nbrs - heads * early, heads * nf)
+    give(dv, gv, vs, vr, 0, nbrs, 0)
     turn = 2
     order = [0, chips - 2] + list(range(1, chips - 2))
     for step in order:
         back = lax.rem(chip + chips - step - 1, chips) * 2
-        around[step].wait_recv()
-        around[chips - 1 + step].wait_recv()
+        if step == 1:
+            for each in range(heads):
+                around[each, 1].wait_recv()
         move = remote(
             att_all.at[back + core], att_all.at[back + core], fa.at[step], ga.at[step], "fsdp", sibling
         )
@@ -714,7 +760,7 @@
         )
         put.start()
         puts.append(put)
-    for move in outs[0] + outs[1] + backs + to_sibling + around:
+    for move in outs + backs + to_sibling + list(around.values()):
         move.wait_send()
     for (_, stage), sent in flying.items():
         for move in sent:
@@ -748,10 +794,10 @@
     sources, indices = nbr_source.T, nbr_index.T
     share = width // nd
 
-    kt, vt, qg, ug, hs, tab = pl.pallas_call(
+    kt, vt, qg, ug, hs, tab, o_first, weights = pl.pallas_call(
         lambda *a: spread_kernel(nd, nf, width, *a),
         in_specs=[SM, SM, SM, ANY, ANY, ANY, ANY, ANY],
-        out_specs=[ANY, ANY, ANY, ANY, ANY, SM],
+        out_specs=[ANY, ANY, ANY, ANY, ANY, SM, ANY, VM],
         out_shape=[
             jax.ShapeDtypeStruct((nf, nbrs, piece, width), bf),
             jax.ShapeDtypeStruct((nf, nbrs, piece, width), bf),
@@ -759,6 +805,8 @@
             jax.ShapeDtypeStruct((nd, nf, SPAN, width), bf),
             jax.ShapeDtypeStruct((nd, SPAN, 128), f32),
             jax.ShapeDtypeStruct((3 * refs_all,), i32),
+            jax.ShapeDtypeStruct((nd, nf, SPAN, HEAD_DIM), bf),
+            jax.ShapeDtypeStruct((SPAN, 128), f32),
         ],
         scratch_shapes=[
             pltpu.VMEM((nf, spans, SPAN, width), bf),
@@ -781,8 +829,9 @@
             pltpu.VMEM((nd, SPAN, 128), f32),
             pltpu.VMEM((SPAN, 128), f32),
             pltpu.SMEM((refs_all,), i32),
+            pltpu.VMEM((nd, nf, SPAN, HEAD_DIM), bf),
             dma(nf), dma(nf), dma(2 * nf), dma(2 * nf), dma(2 * nf), dma(2 * nf), dma(nd), dma(nd), dma(nd), dma(nd),
-            dma(chips), dma(chips), dma(6), dma(6), dma(nd), dma(nd), dma(nd), dma(nd), dma(13), dma(2),
+            dma(chips), dma(chips), dma(6), dma(6), dma(nd), dma(nd), dma(nd), dma(nd), dma(nd), dma(nd), dma(14), dma(2),
         ],
         compiler_params=comm(1),
         name="spread",
@@ -796,7 +845,7 @@
         in_specs=[SM, ANY, ANY, ANY, ANY, ANY],
         out_specs=[ANY, ANY, ANY, ANY],
         out_shape=[
-            jax.ShapeDtypeStruct((refs_all, SPAN, width), bf),
+            jax.ShapeDtypeStruct((refs_all, SPAN, HEAD_DIM), bf),
             jax.ShapeDtypeStruct((refs_all, SPAN, width), bf),
             jax.ShapeDtypeStruct((nf, nbrs, piece, width), bf),
             jax.ShapeDtypeStruct((nf, nbrs, piece, width), bf),
@@ -807,7 +856,7 @@
             pltpu.VMEM((nd, SPAN, 128), f32),
             pltpu.VMEM((nf, nbrs, piece, width), bf),
             pltpu.VMEM((nf, nbrs, piece, width), bf),
-            pltpu.VMEM((refs_all, SPAN, width), bf),
+            pltpu.VMEM((refs_all, SPAN, HEAD_DIM), bf),
             pltpu.VMEM((refs_all, SPAN, width), bf),
             pltpu.VMEM((nf, nbrs, piece, width), bf),
             pltpu.VMEM((nf, nbrs, piece, width), bf),
@@ -822,7 +871,7 @@
 
     attended, gq, gk, gv, grad_proj = pl.pallas_call(
         lambda *a: return_kernel(nd, nf, width, spans, *a),
-        in_specs=[SM, SM, ANY, ANY, ANY, ANY, ANY],
+        in_specs=[SM, SM, VM, ANY, ANY, ANY, ANY, ANY, ANY],
         out_specs=[ANY, ANY, ANY, ANY, ANY],
         out_shape=[
             jax.ShapeDtypeStruct((token_rows, full_width), bf),
@@ -833,8 +882,8 @@
         ],
         scratch_shapes=[
             pltpu.VMEM((nf, rows, width), bf),
-            pltpu.VMEM((nd, nf // 2, SPAN, width), bf),
-            pltpu.VMEM((nd, nf // 2, SPAN, width), bf),
+            pltpu.VMEM((nd, nf, SPAN, HEAD_DIM), bf),
+            pltpu.VMEM((nd, nf, SPAN, HEAD_DIM), bf),
             pltpu.VMEM((nd, nf, SPAN, width), bf),
             pltpu.VMEM((nf, spans, SPAN, width), bf),
             pltpu.VMEM((nbrs, piece, width), bf),
@@ -847,14 +896,14 @@
             pltpu.VMEM((nf, nd // 2 - 1, share, columns), bf),
             pltpu.VMEM((nf, share, columns), f32),
             pltpu.VMEM((nf, share, columns), bf),
-            dma(2 * nd), dma(2 * nd), dma(nd), dma(nd), dma(2 * nf), dma(2 * nf), dma(nf), dma(nf), dma(nf), dma(nf),
+            dma(nd), dma(nd), dma(nd), dma(nd), dma(3 * nf), dma(3 * nf), dma(nf), dma(nf), dma(nf), dma(nf),
             dma(chips + 1), dma(chips + 1), dma(2 * chips), dma(2 * chips),
             dma(nf, 2 * nd), dma(nf, 2 * nd), dma(8), dma(1 + nf), dma(nf),
         ],
         compiler_params=comm(3),
         name="giveback",
     )(
-        sources, nbr_count, o.reshape(nd, nf, SPAN, width), cotangent,
+        sources, nbr_count, weights, o_first, o.reshape(nd, nf, SPAN, HEAD_DIM), cotangent,
         dq.reshape(nd, nf, SPAN, width), dk, dv,
     )
     results = [grad_proj, gk, gv, attended, gq.reshape(token_rows, full_width)]

time: 307 us -> 294 us (0.958)
  Pallas kernels: 306 us -> 292 us
    pallas_call x1, Pallas kernels: 147 us -> 128 us  [local(): pl.pallas_call(lambda *a: return_kernel(nd, nf, width, spans, *a), in_spe...]
    pallas_call x1, Pallas kernels: 128 us -> 132 us  [local(): pl.pallas_call(lambda *a: spread_kernel(nd, nf, width, *a), in_specs=[SM,...]
where the time goes in v6:
time: 294 us; the launch traced here: 293 us
  Pallas kernels  292 us (99%)
    pallas_call x1, Pallas kernels, local(): pl.pallas_call(lambda *a: spread_kernel(nd, nf, width, *a), in_specs=[SM,...  132 us
    pallas_call x1, Pallas kernels, local(): pl.pallas_call(lambda *a: return_kernel(nd, nf, width, spans, *a), in_spe...  128 us
    pallas_call x1, Pallas kernels, local(): pl.pallas_call(lambda *a: backward_kernel(nf, *a), in_specs=[SM, ANY, ANY...  24.5 us
    pallas_call x1, Pallas kernels, local(): pl.pallas_call(finish_kernel, in_specs=[ANY] * len(results), out_specs=[A...  8.78 us

profile of v6, /device:TPU:0, one launch (start us, length us, event | category | flops | bytes accessed | tf_op | source)
XLA Modules:
  0.0 293.3 jit_solution(11058777546887843245)
XLA Ops:
  0.6 131.5 %spread.1 = (bf16[8,48,16,256]{3,2,1,0:T(8,128)(2,1)}, bf16[8,48,16,256]{3,2,1,0:T(8,128)(2,1)}, bf16[8,8,64,256]{3,2,1,0:T(8,128)(2,1)}, bf16[8,8,64,256]{3,2,1...) custom-call(s32[2,192]{1,0:T(2,128)} %bitcast.14, ...), custom_call_target="tpu_custom_call" | custom-call | tf_op jit(solution)/shard_map/spread/pallas_call | solution.py:797
  132.2 24.5 %backward.1 = (bf16[64,64,128]{2,1,0:T(8,128)(2,1)}, bf16[64,64,256]{2,1,0:T(8,128)(2,1)}, bf16[8,48,16,256]{3,2,1,0:T(8,128)(2,1)}, bf16[8,48,16,256]{3,2,1,0:T(8,128)(2,1)}) custom-call(s32[192]{0:T(256)} %get-tuple-element.29.a_0_, bf16[64,64,256]{2,1,0:T(8,128)(2,1)} %bitcast.9, bf16[64,64,256]{2,1,0:T(8,128)(2,1)} %bitcast.10, ...), custom_call_target="tpu_custom_call" | custom-call | tf_op jit(solution)/shard_map/backward/pallas_call | solution.py:843
  156.7 127.7 %giveback.1 = (bf16[192,2048]{1,0:T(8,128)(2,1)}, bf16[3,64,2048]{2,1,0:T(8,128)(2,1)}, bf16[48,16,2048]{2,1,0:T(8,128)(2,1)}, bf16[48,16,2048]{2,1,0:T(8,128)(2,1)}, bf16[2048,1024]{1,0:T(8,128)(2,1)}) custom-call(s32[2,192]{1,0:T(2,128)} %bitcast.15, s32[192]{0:T(256)} %a_1_.1, f32[64,128]{1,0:T(8,128)} %get-tuple-element.27.a_2_, ...), custom_call_target="tpu_custom_call" | custom-call | tf_op jit(solution)/shard_map/giveback/pallas_call | solution.py:872
  284.4 8.8 %finish.1 = (bf16[2048,1024]{1,0:T(8,128)(2,1)}, bf16[48,16,2048]{2,1,0:T(8,128)(2,1)}, bf16[48,16,2048]{2,1,0:T(8,128)(2,1)}, bf16[192,2048]{1,0:T(8,128)(2,1)}, bf16[192,2048]{1,0:T(8,128)(2,1)}) custom-call(bf16[2048,1024]{1,0:T(8,128)(2,1)} %get-tuple-element.39.refs_0_, bf16[48,16,2048]{2,1,0:T(8,128)(2,1)} %get-tuple-element.40.refs_1_, ...), custom_call_target="tpu_custom_call" | custom-call | tf_op jit(solution)/shard_map/finish/pallas_call | solution.py:910

commit v7 on v6

--- a/solution.py
+++ b/solution.py
@@ -419,34 +419,41 @@
 
     @pl.loop(0, (count + UNROLL - 1) // UNROLL)
     def _(step):
-        done = []
+        items = []
         for more in range(UNROLL):
             r = listed[step * UNROLL + more]
             n, c, live = tab[r], tab[refs + r], tab[2 * refs + r]
             into = jnp.where(live > 0, n, nbrs)
-            keys = kt[:, n].reshape(length, -1)
-            values = vt[:, n].reshape(length, -1)
-            query, up, table = q[r], u[r], hs[r // nf]
-            at = heads * (nf * c + r % nf)
-            outs, dqs, dks, dvs = [], [], [], []
-            for h in range(heads):
-                part = slice(h * HEAD_DIM, (h + 1) * HEAD_DIM)
-                scores = dot(query[:, part], keys[:, part], NT) * SCALE
-                probs = jnp.exp(scores - pick(table, at + h))
-                rounded = probs.astype(jnp.bfloat16)
-                dprobs = dot(up[:, part], values[:, part], NT)
-                ds = (probs * (dprobs - pick(table, 64 + at + h)) * SCALE).astype(jnp.bfloat16)
-                if h > 0:
-                    outs.append(dot(rounded, values[:, part], NN).astype(jnp.bfloat16))
-                dqs.append(dot(ds, keys[:, part], NN).astype(jnp.bfloat16))
-                dks.append(dot(ds, query[:, part], TN))
-                dvs.append(dot(rounded, up[:, part], TN))
-            done.append((r, into, outs, dqs, dks, dvs))
-        for r, into, outs, dqs, dks, dvs in done:
-            o_ref[r] = outs[0]
-            dq_ref[r] = jnp.concatenate(dqs, axis=1)
-            k_acc[into] += jnp.concatenate(dks, axis=1)
-            v_acc[into] += jnp.concatenate(dvs, axis=1)
+            items.append((r, n, into, heads * (nf * c + r % nf)))
+        pairs = [(i, h) for i in range(UNROLL) for h in range(heads)]
+        parts = [slice(h * HEAD_DIM, (h + 1) * HEAD_DIM) for h in range(heads)]
+
+        def rows_of(ref, i, h):
+            return ref[:, items[i][1], :, parts[h]].reshape(length, HEAD_DIM)
+
+        def mark(i, h, offset):
+            return pick(hs[items[i][0] // nf], offset + items[i][3] + h)
+
+        scores = [dot(q[items[i][0], :, parts[h]], rows_of(kt, i, h), NT) for i, h in pairs]
+        dprobs = [dot(u[items[i][0], :, parts[h]], rows_of(vt, i, h), NT) for i, h in pairs]
+        probs = [jnp.exp(s * SCALE - mark(i, h, 0)) for s, (i, h) in zip(scores, pairs)]
+        rounded = [value.astype(jnp.bfloat16) for value in probs]
+        slopes = [
+            (value * (d - mark(i, h, 64)) * SCALE).astype(jnp.bfloat16)
+            for value, d, (i, h) in zip(probs, dprobs, pairs)
+        ]
+        for value, (i, h) in zip(rounded, pairs):
+            if h > 0:
+                o_ref[items[i][0]] = dot(value, rows_of(vt, i, h), NN).astype(jnp.bfloat16)
+        dqs = [dot(value, rows_of(kt, i, h), NN) for value, (i, h) in zip(slopes, pairs)]
+        for value, (i, h) in zip(dqs, pairs):
+            dq_ref[items[i][0], :, parts[h]] = value.astype(jnp.bfloat16)
+        dks = [dot(value, q[items[i][0], :, parts[h]], TN) for value, (i, h) in zip(slopes, pairs)]
+        for value, (i, h) in zip(dks, pairs):
+            k_acc[items[i][2], :, parts[h]] += value
+        dvs = [dot(value, u[items[i][0], :, parts[h]], TN) for value, (i, h) in zip(rounded, pairs)]
+        for value, (i, h) in zip(dvs, pairs):
+            v_acc[items[i][2], :, parts[h]] += value
 
     puts = [
         pltpu.make_async_copy(o_ref, o_any, sems.at[5]),

time: 294 us -> 282 us (0.959)
  Pallas kernels: 292 us -> 281 us
    pallas_call x1, Pallas kernels: 24.5 us -> 16.5 us  [local(): pl.pallas_call(lambda *a: backward_kernel(nf, *a), in_specs=[SM, ANY, ANY...]
    pallas_call x1, Pallas kernels: 128 us -> 124 us  [local(): pl.pallas_call(lambda *a: return_kernel(nd, nf, width, spans, *a), in_spe...]
where the time goes in v7:
time: 282 us; the launch traced here: 281 us
  Pallas kernels  281 us (100%)
    pallas_call x1, Pallas kernels, local(): pl.pallas_call(lambda *a: spread_kernel(nd, nf, width, *a), in_specs=[SM,...  132 us
    pallas_call x1, Pallas kernels, local(): pl.pallas_call(lambda *a: return_kernel(nd, nf, width, spans, *a), in_spe...  124 us
    pallas_call x1, Pallas kernels, local(): pl.pallas_call(lambda *a: backward_kernel(nf, *a), in_specs=[SM, ANY, ANY...  16.5 us
    pallas_call x1, Pallas kernels, local(): pl.pallas_call(finish_kernel, in_specs=[ANY] * len(results), out_specs=[A...  8.78 us

profile of v7, /device:TPU:0, one launch (start us, length us, event | category | flops | bytes accessed | tf_op | source)
XLA Modules:
  0.0 281.3 jit_solution(16620277413351221689)
XLA Ops:
  0.6 131.5 %spread.1 = (bf16[8,48,16,256]{3,2,1,0:T(8,128)(2,1)}, bf16[8,48,16,256]{3,2,1,0:T(8,128)(2,1)}, bf16[8,8,64,256]{3,2,1,0:T(8,128)(2,1)}, bf16[8,8,64,256]{3,2,1...) custom-call(s32[2,192]{1,0:T(2,128)} %bitcast.14, ...), custom_call_target="tpu_custom_call" | custom-call | tf_op jit(solution)/shard_map/spread/pallas_call | solution.py:804
  132.2 16.5 %backward.1 = (bf16[64,64,128]{2,1,0:T(8,128)(2,1)}, bf16[64,64,256]{2,1,0:T(8,128)(2,1)}, bf16[8,48,16,256]{3,2,1,0:T(8,128)(2,1)}, bf16[8,48,16,256]{3,2,1,0:T(8,128)(2,1)}) custom-call(s32[192]{0:T(256)} %get-tuple-element.29.a_0_, bf16[64,64,256]{2,1,0:T(8,128)(2,1)} %bitcast.9, bf16[64,64,256]{2,1,0:T(8,128)(2,1)} %bitcast.10, ...), custom_call_target="tpu_custom_call" | custom-call | tf_op jit(solution)/shard_map/backward/pallas_call | solution.py:850
  148.6 123.8 %giveback.1 = (bf16[192,2048]{1,0:T(8,128)(2,1)}, bf16[3,64,2048]{2,1,0:T(8,128)(2,1)}, bf16[48,16,2048]{2,1,0:T(8,128)(2,1)}, bf16[48,16,2048]{2,1,0:T(8,128)(2,1)}, bf16[2048,1024]{1,0:T(8,128)(2,1)}) custom-call(s32[2,192]{1,0:T(2,128)} %bitcast.15, s32[192]{0:T(256)} %a_1_.1, f32[64,128]{1,0:T(8,128)} %get-tuple-element.27.a_2_, ...), custom_call_target="tpu_custom_call" | custom-call | tf_op jit(solution)/shard_map/giveback/pallas_call | solution.py:879
  272.5 8.8 %finish.1 = (bf16[2048,1024]{1,0:T(8,128)(2,1)}, bf16[48,16,2048]{2,1,0:T(8,128)(2,1)}, bf16[48,16,2048]{2,1,0:T(8,128)(2,1)}, bf16[192,2048]{1,0:T(8,128)(2,1)}, bf16[192,2048]{1,0:T(8,128)(2,1)}) custom-call(bf16[2048,1024]{1,0:T(8,128)(2,1)} %get-tuple-element.39.refs_0_, bf16[48,16,2048]{2,1,0:T(8,128)(2,1)} %get-tuple-element.40.refs_1_, ...), custom_call_target="tpu_custom_call" | custom-call | tf_op jit(solution)/shard_map/finish/pallas_call | solution.py:917

commit v8 on v7

--- a/solution.py
+++ b/solution.py
@@ -303,11 +303,14 @@
         @pl.loop(0, nd)
         def _(d):
             marks = st[d]
-            for f in range(nf):
-                n = tab[d * nf + f]
-                values = vt_vm[h][:, n].reshape(length, HEAD_DIM)
-                dprobs = dot(ug_vm[d, f, :, part], values, NT)
-                mean = jnp.sum(probs[h, d * nf + f] * dprobs, axis=1, keepdims=True)
+            dprobs = [
+                dot(ug_vm[d, f, :, part], vt_vm[h][:, tab[d * nf + f]].reshape(length, HEAD_DIM), NT)
+                for f in range(nf)
+            ]
+            means = [
+                jnp.sum(probs[h, d * nf + f] * dprobs[f], axis=1, keepdims=True) for f in range(nf)
+            ]
+            for f, mean in enumerate(means):
                 marks = jnp.where(lane == 2 * group_lanes + heads * f + h, mean, marks)
             st[d] = marks
 
@@ -529,7 +532,7 @@
     moves = []
 
     nbrs = dk.shape[1]
-    early = nbrs // 3
+    early = nbrs // 4
 
     def give(ref, out, s_sem, r_sem, start, size, base):
         here = pl.ds(start, size)
@@ -541,6 +544,7 @@
             move.start()
             moves.append(move)
 
+    give(dk, gk, ks, kr, 0, 8, 3 * nf)
     for copy in firsts:
         copy.wait()
     puts = [
@@ -597,7 +601,7 @@
             move = remote(att, att, ba.at[place], ca.at[place], "fsdp", there)
             move.start()
             around[h, step] = move
-        give(dk, gk, ks, kr, h * early, early, h * nf)
+        give(dk, gk, ks, kr, 8 + h * early, early, h * nf)
     load_cot.wait()
     share = width // nd
     columns = cot_vm.shape[1]
@@ -735,7 +739,7 @@
         held = head_of(back, h)
         around[h, 1] = remote(held, held, ba.at[place], ca.at[place], "fsdp", there)
         around[h, 1].start()
-    give(dk, gk, ks, kr, heads * early, nbrs - heads * early, heads * nf)
+    give(dk, gk, ks, kr, 8 + heads * early, nbrs - 8 - heads * early, heads * nf)
     give(dv, gv, vs, vr, 0, nbrs, 0)
     turn = 2
     order = [0, chips - 2] + list(range(1, chips - 2))
@@ -903,7 +907,7 @@
             pltpu.VMEM((nf, nd // 2 - 1, share, columns), bf),
             pltpu.VMEM((nf, share, columns), f32),
             pltpu.VMEM((nf, share, columns), bf),
-            dma(nd), dma(nd), dma(nd), dma(nd), dma(3 * nf), dma(3 * nf), dma(nf), dma(nf), dma(nf), dma(nf),
+            dma(nd), dma(nd), dma(nd), dma(nd), dma(4 * nf), dma(4 * nf), dma(nf), dma(nf), dma(nf), dma(nf),
             dma(chips + 1), dma(chips + 1), dma(2 * chips), dma(2 * chips),
             dma(nf, 2 * nd), dma(nf, 2 * nd), dma(8), dma(1 + nf), dma(nf),
         ],

time: 282 us -> 284 us (level)
  no operation moved by 1% of the time
where the time goes in v8:
time: 284 us
  Pallas kernels  283 us (100%)
    pallas_call x1, Pallas kernels, local(): pl.pallas_call(lambda *a: spread_kernel(nd, nf, width, *a), in_specs=[SM,...  132 us
    pallas_call x1, Pallas kernels, local(): pl.pallas_call(lambda *a: return_kernel(nd, nf, width, spans, *a), in_spe...  125 us
    pallas_call x1, Pallas kernels, local(): pl.pallas_call(lambda *a: backward_kernel(nf, *a), in_specs=[SM, ANY, ANY...  18 us
    pallas_call x1, Pallas kernels, local(): pl.pallas_call(finish_kernel, in_specs=[ANY] * len(results), out_specs=[A...  8.78 us

profile of v8, /device:TPU:0, one launch (start us, length us, event | category | flops | bytes accessed | tf_op | source)
XLA Modules:
  0.0 284.1 jit_solution(3531172703318590714)
XLA Ops:
  0.6 131.5 %spread.1 = (bf16[8,48,16,256]{3,2,1,0:T(8,128)(2,1)}, bf16[8,48,16,256]{3,2,1,0:T(8,128)(2,1)}, bf16[8,8,64,256]{3,2,1,0:T(8,128)(2,1)}, bf16[8,8,64,256]{3,2,1...) custom-call(s32[2,192]{1,0:T(2,128)} %bitcast.14, ...), custom_call_target="tpu_custom_call" | custom-call | tf_op jit(solution)/shard_map/spread/pallas_call | solution.py:808
  132.2 18.0 %backward.1 = (bf16[64,64,128]{2,1,0:T(8,128)(2,1)}, bf16[64,64,256]{2,1,0:T(8,128)(2,1)}, bf16[8,48,16,256]{3,2,1,0:T(8,128)(2,1)}, bf16[8,48,16,256]{3,2,1,0:T(8,128)(2,1)}) custom-call(s32[192]{0:T(256)} %get-tuple-element.29.a_0_, bf16[64,64,256]{2,1,0:T(8,128)(2,1)} %bitcast.9, bf16[64,64,256]{2,1,0:T(8,128)(2,1)} %bitcast.10, ...), custom_call_target="tpu_custom_call" | custom-call | tf_op jit(solution)/shard_map/backward/pallas_call | solution.py:854
  150.2 125.2 %giveback.1 = (bf16[192,2048]{1,0:T(8,128)(2,1)}, bf16[3,64,2048]{2,1,0:T(8,128)(2,1)}, bf16[48,16,2048]{2,1,0:T(8,128)(2,1)}, bf16[48,16,2048]{2,1,0:T(8,128)(2,1)}, bf16[2048,1024]{1,0:T(8,128)(2,1)}) custom-call(s32[2,192]{1,0:T(2,128)} %bitcast.15, s32[192]{0:T(256)} %a_1_.1, f32[64,128]{1,0:T(8,128)} %get-tuple-element.27.a_2_, ...), custom_call_target="tpu_custom_call" | custom-call | tf_op jit(solution)/shard_map/giveback/pallas_call | solution.py:883
  275.3 8.8 %finish.1 = (bf16[2048,1024]{1,0:T(8,128)(2,1)}, bf16[48,16,2048]{2,1,0:T(8,128)(2,1)}, bf16[48,16,2048]{2,1,0:T(8,128)(2,1)}, bf16[192,2048]{1,0:T(8,128)(2,1)}, bf16[192,2048]{1,0:T(8,128)(2,1)}) custom-call(bf16[2048,1024]{1,0:T(8,128)(2,1)} %get-tuple-element.39.refs_0_, bf16[48,16,2048]{2,1,0:T(8,128)(2,1)} %get-tuple-element.40.refs_1_, ...), custom_call_target="tpu_custom_call" | custom-call | tf_op jit(solution)/shard_map/finish/pallas_call | solution.py:921
